TPU v7x, 512 devices: a whole 4x8x8 slice. The times are simulated.
512 devices in a mesh: ex: 32 (over y_hi, x, core), feat: 16 (over z, y_lo).
Axes of the slice: x: 4, y: 8 (y_hi: 4, y_lo: 2; y = y_hi * 2 + y_lo), z: 8, core: 2. Of those that a mesh axis runs over, the one named last changes fastest.
Arguments:
- train_grads: bfloat16 [32768, 16384], P('ex', 'feat'), may hold values from -200 to 200
- target_grads: bfloat16 [512, 16384], P('ex', 'feat'), may hold values from -300 to 300
- target_mass: float32 [512], replicated, may hold values from 0.25 to 4
Outputs:
- mixtures: bfloat16 [512, 16384], P('ex', 'feat')
All inputs are finite; a program needn't handle non-finite values.
Results may differ from a plain program's by a relative error of at most 0.0048.
Values may be sent and summed in bfloat16 or wider, within the bound.
No kernel may reach another device: no remote copies, remote signals or barrier semaphores. Data moves between devices by JAX's collectives and lax.ppermute only.
A program may use at most 64 MiB of HBM per device.

v0:
```python
import math

import jax
import jax.numpy as jnp
from jax import lax
from jax.sharding import PartitionSpec as P

F = 16384
ITERS = 3


def column_lse(values):
    local_max = jnp.max(values, axis=0)
    top = lax.pmax(local_max, "ex")
    total = lax.psum(jnp.sum(jnp.exp(values - top[None, :]), axis=0), "ex")
    return top + jnp.log(total)


def row_lse_local(values):
    top = jnp.max(values, axis=1)
    return top + jnp.log(jnp.sum(jnp.exp(values - top[:, None]), axis=1))


def shards(train_grads, target_grads, target_mass):
    rows = train_grads.shape[0]
    my_targets = target_grads.shape[0]
    total_rows = rows * lax.axis_size("ex")
    scale = 3.0 / math.sqrt(F)
    log_a = -math.log(total_rows)
    partial_value = lax.dot_general(
        train_grads,
        lax.all_gather(target_grads, "ex", axis=0, tiled=True),
        (((1,), (1,)), ((), ())),
        preferred_element_type=jnp.float32,
    )
    mass_total = jnp.sum(target_mass)
    weights = target_mass / mass_total
    log_b = jnp.log(target_mass) - jnp.log(mass_total)
    logits = lax.psum(partial_value, "feat") * scale
    col_pot = jnp.zeros(log_b.shape, jnp.float32)
    row_pot = jnp.zeros((rows,), jnp.float32)
    for step in range(ITERS):
        row_pot = log_a - row_lse_local(logits + col_pot[None, :])
        col_pot = log_b - column_lse(logits + row_pot[:, None])
    plan = jnp.exp(logits + row_pot[:, None] + col_pot[None, :]).astype(jnp.bfloat16)
    mixed = lax.psum_scatter(
        lax.dot_general(
            plan, train_grads, (((0,), (0,)), ((), ())), preferred_element_type=jnp.float32
        ),
        "ex",
        scatter_dimension=0,
        tiled=True,
    )
    my_start = lax.axis_index("ex") * my_targets
    my_weights = lax.dynamic_slice_in_dim(weights, my_start, my_targets)
    return (mixed / my_weights[:, None]).astype(jnp.bfloat16)


def solution(mesh):
    return jax.shard_map(
        shards,
        mesh=mesh,
        in_specs=(P("ex", "feat"), P("ex", "feat"), P()),
        out_specs=P("ex", "feat"),
        check_vma=False,
    )
```

profile of v0, /device:TPU:6, one launch (start us, length us, event | category | flops | bytes accessed | tf_op | source)
XLA Modules:
  0.0 774.3 jit_solution(3098057220426738019)
XLA Ops:
  6.5 0.7 all-gather.2.cloned.1.call-update
  7.3 63.7 %all-gather.2.cloned.1.call-done = bf16[512,1024]{1,0:T(8,128)(2,1)} async-done(((bf16[16,1024]{1,0:T(8,128)(2,1)}), bf16[512,1024]{1,0:T(8,128)(2,1)}) %all-gather.2.cloned.1.call-update) | async-done | bytes 1048592 | tf_op jit(solution)/shard_map/all_gather | solution.py:32
  71.0 3.8 fusion.5
  74.9 0.0 reduce-scatter.2.cloned.1.call-start
  74.9 0.6 copy-done.4
  75.5 0.6 reduce_sum.63
  76.8 155.8 %all-reduce.2.cloned.1.call-done = f32[1024,512]{1,0:T(8,128)} async-done(((f32[1024,512]{1,0:T(8,128)}), f32[1024,512]{1,0:T(8,128)}) %all-reduce.2.cloned.1.call-update) | async-done | bytes 2097168 | tf_op jit(solution)/shard_map/psum | solution.py:39
  232.6 2.0 fusion.3
  234.6 0.3 copy-done.1
  234.8 0.6 exponential_reduce_fusion.5
  235.4 0.3 add_reduce_fusion.3
  235.7 56.8 %pmax.21 = f32[512]{0:T(512)S(1)} all-reduce(f32[512]{0:T(512)S(1)} %add_reduce_fusion.3), channel_id=1, replica_groups=mesh['ex'=32,'feat'=16] {'ex'}, use_global_device_ids=true, to_apply=%region_5.0 | all-reduce | flops 512 | bytes 4096 | tf_op jit(solution)/shard_map/pmax | solution.py:14
  292.5 2.1 exponential_reduce_fusion.4
  294.6 65.4 %psum.29 = f32[512]{0:T(512)S(1)} all-reduce(f32[512]{0:T(512)S(1)} %exponential_reduce_fusion.4), channel_id=1, replica_groups=mesh['ex'=32,'feat'=16] {'ex'}, use_global_device_ids=true, to_apply=%region_7.0 | all-reduce | flops 512 | bytes 4096 | tf_op jit(solution)/shard_map/psum | solution.py:15
  360.0 2.0 add_reduce_fusion.2
  362.0 0.2 copy-done.2
  362.2 0.6 exponential_reduce_fusion.3
  362.8 0.3 add_reduce_fusion.1
  363.1 69.9 %pmax.22 = f32[512]{0:T(512)S(1)} all-reduce(f32[512]{0:T(512)S(1)} %add_reduce_fusion.1), channel_id=1, replica_groups=mesh['ex'=32,'feat'=16] {'ex'}, use_global_device_ids=true, to_apply=%region_11.0 | all-reduce | flops 512 | bytes 4096 | tf_op jit(solution)/shard_map/pmax | solution.py:14
  432.9 2.1 exponential_reduce_fusion.2
  435.0 69.9 %psum.30 = f32[512]{0:T(512)S(1)} all-reduce(f32[512]{0:T(512)S(1)} %exponential_reduce_fusion.2), channel_id=1, replica_groups=mesh['ex'=32,'feat'=16] {'ex'}, use_global_device_ids=true, to_apply=%region_13.0 | all-reduce | flops 512 | bytes 4096 | tf_op jit(solution)/shard_map/psum | solution.py:15
  504.9 0.8 broadcast_divide_fusion
  505.7 1.9 add_reduce_fusion
  507.6 0.6 exponential_reduce_fusion.1
  508.2 0.3 add_reduce_fusion.4
  508.5 69.9 %pmax.23 = f32[512]{0:T(512)S(1)} all-reduce(f32[512]{0:T(512)S(1)} %add_reduce_fusion.4), channel_id=1, replica_groups=mesh['ex'=32,'feat'=16] {'ex'}, use_global_device_ids=true, to_apply=%region_17.0 | all-reduce | flops 512 | bytes 4096 | tf_op jit(solution)/shard_map/pmax | solution.py:14
  578.4 2.1 exponential_reduce_fusion
  580.4 69.9 %psum.31 = f32[512]{0:T(512)S(1)} all-reduce(f32[512]{0:T(512)S(1)} %exponential_reduce_fusion), channel_id=1, replica_groups=mesh['ex'=32,'feat'=16] {'ex'}, use_global_device_ids=true, to_apply=%region_19.0 | all-reduce | flops 512 | bytes 4096 | tf_op jit(solution)/shard_map/psum | solution.py:15
  650.3 4.3 fusion
  654.6 0.1 dynamic_slice.3
  654.7 111.5 %reduce-scatter.2.cloned.1.call-done = f32[16,1024]{1,0:T(8,128)} async-done(((f32[512,1024]{1,0:T(8,128)}), f32[16,1024]{1,0:T(8,128)}) %reduce-scatter.2.cloned.1.call-update) | async-done | bytes 65552 | tf_op jit(solution)/shard_map/reduce_scatter | solution.py:46
  766.2 1.5 divide_convert_fusion
  (16 shorter events, 0.1 us)
Async XLA Ops:
  6.5 64.5 %copy-start = (bf16[1024,1024]{1,0:T(8,128)(2,1)S(1)}, bf16[1024,1024]{1,0:T(8,128)(2,1)}, u32[]{:S(2)}) copy-start(bf16[1024,1024]{1,0:T(8,128)(2,1)} %param.3) | copy-start | bytes 6291460
  6.5 64.5 %all-gather.2.cloned.1.call-start = ((), (), s32[]{:S(2)}) async-start(), calls=%async_computation.1 | async-start | bytes 1081344 | tf_op jit(solution)/shard_map/all_gather | solution.py:32
  7.3 225.3 %all-reduce.2.cloned.1.call-start = ((), (), s32[]{:S(2)}) async-start(), calls=%async_computation.2 | async-start | bytes 4194304 | tf_op jit(solution)/shard_map/psum | solution.py:39
  74.8 0.7 copy-start.4
  74.9 691.4 %reduce-scatter.2.cloned.1.call-start = ((), (), s32[]{:S(2)}) async-start(), calls=%async_computation.3 | async-start | bytes 2162688 | tf_op jit(solution)/shard_map/reduce_scatter | solution.py:46
  232.6 2.2 copy-start.1
  360.0 2.2 copy-start.2
  504.9 2.7 copy-start.3
Sparse Core Ops, SparseCore 0:
  10.5 60.5 all-gather.1
  75.0 157.5 all-reduce.1
  654.7 111.4 reduce-scatter.1
where the time goes:
time: 775 us; the launch traced here: 774 us
  blocking collectives  402 us (52%)
  waiting for transfers between devices  332 us (43%)
  other arithmetic  17.6 us (2%)
  between operations  13.9 us (2%)
  matrix products  8.09 us (1%)
    psum x3, blocking collectives, column_lse(): total = lax.psum(jnp.sum(jnp.exp(values - top[None, :]), axis=0), 'ex')  205 us
    pmax x3, blocking collectives, column_lse(): top = lax.pmax(local_max, 'ex')  197 us
    psum x1, waiting for transfers between devices, shards(): logits = lax.psum(partial_value, 'feat') * scale  156 us
    reduce_scatter x1, waiting for transfers between devices, shards(): lax.psum_scatter(lax.dot_general(plan, train_grads, (((0,), (0,)), ((), (...  112 us
    all_gather x1, waiting for transfers between devices, shards(): lax.all_gather(target_grads, 'ex', axis=0, tiled=True)  63.7 us
  transfers between devices with their start and end apart: 3, of which 3 were waited for; matrix products, arithmetic and copies ran while one was open for 0% of the time, Pallas kernels for 0%

commit v1 on v0

v1 whole, which is shorter than its diff:
```python
import math

import jax
import jax.numpy as jnp
from jax import lax
from jax.sharding import Mesh, PartitionSpec as P

F = 16384
CHIPS = ("yh", "x")
EX = ("yh", "x", "c")
FEAT = ("z", "yl")


def split3(v):
    hi = lax.reduce_precision(v, 8, 7)
    rest = v - hi
    mid = lax.reduce_precision(rest, 8, 7)
    return hi, mid, rest - mid


def spread(block, axes, n):
    copies = jnp.broadcast_to(block[None], (n,) + block.shape)
    return lax.all_to_all(copies, axes, 0, 0, tiled=True)


def shards(train, target, mass):
    rows, feats = train.shape
    nc = lax.axis_size("c")
    nchips = lax.axis_size(CHIPS)
    nex = nc * nchips
    nf = lax.axis_size(FEAT)
    mine = target.shape[0]
    nt = mine * nex
    sub = rows // nf
    scale = 3.0 / math.sqrt(F)
    a = 1.0 / (rows * nex)

    same_core = spread(target, CHIPS, nchips).reshape(nchips * mine, feats)
    targets = spread(same_core, "c", nc).reshape(nt, feats)
    mass = mass.reshape(nchips, nc, mine).transpose(1, 0, 2).reshape(nt)
    b = mass / jnp.sum(mass)

    partial = lax.dot_general(
        train, targets, (((1,), (1,)), ((), ())), preferred_element_type=jnp.float32
    )
    parts = lax.all_to_all(partial.reshape(nf, sub, nt), FEAT, 0, 0, tiled=True)
    logits = jnp.sum(parts, axis=0) * scale

    top = jnp.max(logits, axis=1, keepdims=True)
    total = jnp.sum(jnp.exp(logits - top), axis=1, keepdims=True)
    v = logits - top - jnp.log(total)
    shift = jnp.max(v, axis=0)
    kern = jnp.exp(v - shift[None, :]).astype(jnp.bfloat16)
    tail = jnp.stack(split3(shift)).astype(jnp.bfloat16)
    tail = jnp.concatenate([tail, jnp.zeros((5, nt), jnp.bfloat16)], axis=0)
    block = jnp.concatenate([kern, tail], axis=0)
    blocks = spread(block, FEAT, nf).reshape(nf, sub + 8, nt)
    kern = blocks[:, :sub].astype(jnp.float32)
    shifts = jnp.sum(blocks[:, sub : sub + 3].astype(jnp.float32), axis=1)

    near = jnp.max(shifts, axis=0)
    near_sum = jnp.sum(jnp.exp(shifts - near[None]) * jnp.sum(kern, axis=1), axis=0)
    pairs = spread(jnp.stack([near, near_sum]), EX, nex).reshape(nex, 2, nt)
    far = jnp.max(pairs[:, 0], axis=0)
    far_sum = jnp.sum(jnp.exp(pairs[:, 0] - far[None]) * pairs[:, 1], axis=0)
    factor = jnp.exp(shifts - far[None]) * (b / far_sum)[None]
    plan = kern * factor[:, None, :]

    row = a / jnp.sum(plan, axis=2, keepdims=True)
    cols = jnp.sum(plan * row, axis=(0, 1))
    col = b / jnp.sum(spread(cols[None], EX, nex).reshape(nex, nt), axis=0)

    plan = plan * col[None, None, :]
    row = a / jnp.sum(plan, axis=2, keepdims=True)
    plan = plan * row
    cols = jnp.sum(plan, axis=(0, 1))
    cols = cols + lax.ppermute(cols, "c", [(0, 1), (1, 0)])
    plan = plan.astype(jnp.bfloat16).reshape(rows, nt)

    mixed = lax.dot_general(
        plan, train, (((0,), (0,)), ((), ())), preferred_element_type=jnp.float32
    )
    half = nt // nc
    halves = lax.all_to_all(mixed.reshape(nc, half, feats), "c", 0, 0, tiled=True)
    mixed = jnp.sum(halves, axis=0)
    my_cols = lax.dynamic_slice_in_dim(cols, lax.axis_index("c") * half, half)
    hi, mid, lo = split3(my_cols)
    lane = lax.broadcasted_iota(jnp.int32, (half, 128), 1)
    tail = jnp.where(lane == 0, hi[:, None], jnp.where(lane == 1, mid[:, None], lo[:, None]))
    send = jnp.concatenate([mixed, tail], axis=1).astype(jnp.bfloat16)
    got = lax.all_to_all(
        send.reshape(nchips, mine, feats + 128), CHIPS, 0, 0, tiled=True
    )
    got = jnp.sum(got.astype(jnp.float32), axis=0)
    mass_in = jnp.sum(got[:, feats : feats + 3], axis=1, keepdims=True)
    return (got[:, :feats] / mass_in).astype(jnp.bfloat16)


def solution(mesh):
    fine = Mesh(mesh.devices.reshape(4, 4, 2, 8, 2), ("yh", "x", "c", "z", "yl"))
    return jax.shard_map(
        shards,
        mesh=fine,
        in_specs=(P(EX, FEAT), P(EX, FEAT), P()),
        out_specs=P(EX, FEAT),
        check_vma=False,
    )
```

time: 775 us -> 206 us (0.27)
  waiting for transfers between devices: 332 us -> 17 us
  blocking collectives: 402 us -> 156 us
  starting transfers between devices: 0.08 us -> 14 us
  between operations: 13.9 us -> 0.24 us
    psum x3 -> x0, blocking collectives: 205 us -> none  [column_lse(): total = lax.psum(jnp.sum(jnp.exp(values - top[None, :]), axis=0), 'ex')]
    pmax x3 -> x0, blocking collectives: 197 us -> none  [column_lse(): top = lax.pmax(local_max, 'ex')]
    psum x1 -> x0, waiting for transfers between devices: 156 us -> none  [shards(): logits = lax.psum(partial_value, 'feat') * scale]
    all_to_all x0 -> x6, blocking collectives: none -> 156 us  [the longest x3 64.6 us: spread(): return lax.all_to_all(copies, axes, 0, 0, tiled=True)]
    reduce_scatter x1 -> x0, waiting for transfers between devices: 112 us -> none  [shards(): lax.psum_scatter(lax.dot_general(plan, train_grads, (((0,), (0,)), ((), (...]
    all_gather x1 -> x0, waiting for transfers between devices: 63.7 us -> none  [shards(): lax.all_gather(target_grads, 'ex', axis=0, tiled=True)]
    all_to_all x0 -> x2, waiting for transfers between devices: none -> 17 us  [spread(): return lax.all_to_all(copies, axes, 0, 0, tiled=True)]
    all_to_all x0 -> x2, starting transfers between devices: none -> 12 us  [spread(): return lax.all_to_all(copies, axes, 0, 0, tiled=True)]
  transfers between devices with their start and end apart: 3 -> 3, of which waited for: 3 -> 2; matrix products, arithmetic and copies ran while one was open for 0% -> 2% of each run, Pallas kernels for 0% -> 0%
where the time goes in v1:
time: 206 us; the launch traced here: 204 us
  blocking collectives  156 us (76%)
  waiting for transfers between devices  17 us (8%)
  starting transfers between devices  14 us (7%)
  other arithmetic  10.2 us (5%)
  local copies, waits for them, and re-layouts  4.46 us (2%)
  matrix products  2.55 us (1%)
    all_to_all x3, blocking collectives, spread(): return lax.all_to_all(copies, axes, 0, 0, tiled=True)  64.6 us
    all_to_all x1, blocking collectives, shards(): parts = lax.all_to_all(partial.reshape(nf, sub, nt), FEAT, 0, 0, tiled=True)  61.3 us
    all_to_all x1, blocking collectives, shards(): lax.all_to_all(send.reshape(nchips, mine, feats + 128), CHIPS, 0, 0, tile...  23.3 us
    all_to_all x2, waiting for transfers between devices, spread(): return lax.all_to_all(copies, axes, 0, 0, tiled=True)  17 us
    all_to_all x2, starting transfers between devices, spread(): return lax.all_to_all(copies, axes, 0, 0, tiled=True)  12 us
    all_to_all x1, blocking collectives, shards(): lax.all_to_all(mixed.reshape(nc, half, feats), 'c', 0, 0, tiled=True)  6.31 us
  transfers between devices with their start and end apart: 3, of which 2 were waited for; matrix products, arithmetic and copies ran while one was open for 2% of the time, Pallas kernels for 0%

profile of v1, /device:TPU:6, one launch (start us, length us, event | category | flops | bytes accessed | tf_op | source)
XLA Modules:
  0.0 204.0 jit_solution(10682809618230394285)
XLA Ops:
  0.0 1.0 broadcast_in_dim.35
  1.0 25.9 %all_to_all.40 = bf16[16,16,1024]{2,1,0:T(8,128)(2,1)S(1)} all-to-all(bf16[16,16,1024]{2,1,0:T(8,128)(2,1)S(1)} %broadcast_in_dim.35), channel_id=1, replica_groups=mesh['yh'=4,'x'=4,'c'=2,'z'=8,'yl'=2] {'yh','x'}, dimensions={0} | all-to-all | bytes 1048576 | tf_op jit(solution)/shard_map/all_to_all | solution.py:23
  26.9 0.1 broadcast_in_dim.37
  27.0 4.6 %all_to_all.41 = bf16[2,256,1024]{2,1,0:T(8,128)(2,1)S(1)} all-to-all(bf16[2,256,1024]{2,1,0:T(8,128)(2,1)S(1)} %broadcast_in_dim.37), channel_id=1, replica_groups=mesh['yh'=4,'x'=4,'c'=2,'z'=8,'yl'=2] {'c'}, dimensions={0} | all-to-all | bytes 2097152 | tf_op jit(solution)/shard_map/all_to_all | solution.py:23
  31.6 1.3 fusion.17
  32.9 61.3 %all_to_all.42 = f32[16,64,512]{2,1,0:T(8,128)} all-to-all(f32[16,64,512]{2,1,0:T(8,128)S(1)} %fusion.17), channel_id=1, replica_groups=mesh['yh'=4,'x'=4,'c'=2,'z'=8,'yl'=2] {'z','yl'}, dimensions={0} | all-to-all | bytes 4194304 | tf_op jit(solution)/shard_map/all_to_all | solution.py:46
  94.2 1.8 reduce_sum.135
  96.1 0.2 exponential_reduce_fusion
  96.7 34.1 %all_to_all.43 = bf16[16,72,512]{2,1,0:T(8,128)(2,1)S(1)} all-to-all(bf16[16,72,512]{2,1,0:T(8,128)(2,1)S(1)} %broadcast_in_dim.45), channel_id=1, replica_groups=mesh['yh'=4,'x'=4,'c'=2,'z'=8,'yl'=2] {'z','yl'}, dimensions={0} | all-to-all | bytes 2359296 | tf_op jit(solution)/shard_map/all_to_all | solution.py:23
  130.9 0.2 convert_reduce_fusion
  131.1 0.7 broadcast_in_dim.46
  131.8 6.4 %all-to-all-start.4 = ((f32[32,2,512]{2,1,0:T(2,128)}), f32[32,2,512]{2,1,0:T(2,128)S(1)}, u32[]{:S(2)}, u32[]{:S(2)}) async-start(f32[32,2,512]{2,1,0:T(2,128)} %broadcast_in_dim.46), calls=%async_computation.4 | async-start | bytes 262144 | tf_op jit(solution)/shard_map/all_to_all | solution.py:23
  138.3 0.6 reduce_sum.140
  139.0 8.7 %all-to-all-done.4 = f32[32,2,512]{2,1,0:T(2,128)S(1)} async-done(((f32[32,2,512]{2,1,0:T(2,128)}), f32[32,2,512]{2,1,0:T(2,128)S(1)}, u32[]{:S(2)}, u32[]{:S(2)}) %all-to-all-start.4) | async-done | bytes 131104 | tf_op jit(solution)/shard_map/all_to_all | solution.py:23
  147.7 0.1 slice_reduce_fusion.1
  147.8 0.6 multiply_divide_fusion.1
  148.5 0.3 fusion.2
  148.8 0.4 fusion.7
  149.2 0.7 broadcast_in_dim.47
  149.8 5.6 %all-to-all-start.5 = ((f32[32,1,512]{2,1,0:T(1,128)}), f32[32,1,512]{2,1,0:T(1,128)S(1)}, u32[]{:S(2)}, u32[]{:S(2)}) async-start(f32[32,1,512]{2,1,0:T(1,128)} %broadcast_in_dim.47), calls=%async_computation.5 | async-start | bytes 131072 | tf_op jit(solution)/shard_map/all_to_all | solution.py:23
  155.5 8.4 %all-to-all-done.5 = f32[32,1,512]{2,1,0:T(1,128)S(1)} async-done(((f32[32,1,512]{2,1,0:T(1,128)}), f32[32,1,512]{2,1,0:T(1,128)S(1)}, u32[]{:S(2)}, u32[]{:S(2)}) %all-to-all-start.5) | async-done | bytes 65568 | tf_op jit(solution)/shard_map/all_to_all | solution.py:23
  163.9 0.6 multiply_divide_fusion
  164.6 0.3 fusion.4
  164.9 1.4 fusion.6
  166.3 1.5 copy.16
  167.8 2.0 collective-permute-start
  169.8 1.3 fusion.8
  171.1 6.3 %all_to_all.44 = f32[2,256,1024]{2,1,0:T(8,128)} all-to-all(f32[2,256,1024]{2,1,0:T(8,128)S(1)} %fusion.8), channel_id=1, replica_groups=mesh['yh'=4,'x'=4,'c'=2,'z'=8,'yl'=2] {'c'}, dimensions={0} | all-to-all | bytes 4194304 | tf_op jit(solution)/shard_map/all_to_all | solution.py:84
  177.4 1.8 reduce_sum.146
  179.6 0.2 select_convert_fusion
  179.8 23.3 %all_to_all.45 = bf16[16,16,1152]{2,1,0:T(8,128)(2,1)S(1)} all-to-all(bf16[16,16,1152]{2,1,0:T(8,128)(2,1)S(1)} %pad_maximum_fusion), channel_id=1, replica_groups=mesh['yh'=4,'x'=4,'c'=2,'z'=8,'yl'=2] {'yh','x'}, dimensions={0} | all-to-all | bytes 1179648 | tf_op jit(solution)/shard_map/all_to_all | solution.py:91
  203.3 0.7 fusion.10
  (34 shorter events, 1.5 us)
Async XLA Ops:
  0.0 31.6 %copy-start = (bf16[1024,1024]{1,0:T(8,128)(2,1)S(1)}, bf16[1024,1024]{1,0:T(8,128)(2,1)}, u32[]{:S(2)}) copy-start(bf16[1024,1024]{1,0:T(8,128)(2,1)} %param.3) | copy-start | bytes 6291460
  96.7 41.6 %copy-start.1 = (f32[512]{0:T(512)S(1)}, f32[512]{0:T(512)}, u32[]{:S(2)}) copy-start(f32[512]{0:T(512)} %param.5) | copy-start | bytes 6148
  131.8 15.9 %all-to-all-start.4 = ((f32[32,2,512]{2,1,0:T(2,128)}), f32[32,2,512]{2,1,0:T(2,128)S(1)}, u32[]{:S(2)}, u32[]{:S(2)}) async-start(f32[32,2,512]{2,1,0:T(2,128)} %broadcast_in_dim.46), calls=%async_computation.4 | async-start | bytes 262144 | tf_op jit(solution)/shard_map/all_to_all | solution.py:23
  149.8 14.0 %all-to-all-start.5 = ((f32[32,1,512]{2,1,0:T(1,128)}), f32[32,1,512]{2,1,0:T(1,128)S(1)}, u32[]{:S(2)}, u32[]{:S(2)}) async-start(f32[32,1,512]{2,1,0:T(1,128)} %broadcast_in_dim.47), calls=%async_computation.5 | async-start | bytes 131072 | tf_op jit(solution)/shard_map/all_to_all | solution.py:23
  167.8 11.4 %collective-permute-start = (f32[512]{0:T(512)S(1)}, f32[512]{0:T(512)S(1)}, u32[]{:S(2)}, u32[]{:S(2)}) collective-permute-start(f32[512]{0:T(512)S(1)} %get-tuple-element.6), channel_id=1, source_target_pairs={{0,16},{16,0},{1,17},{17,1},{2,18},{18,2},{3,19},{19,3},{4,20},{20... | collective-permute-start | bytes 6152 | tf_op jit(solution)/shard_map/ppermute | solution.py:77

commit v2 on v1

--- a/solution.py
+++ b/solution.py
@@ -9,6 +9,8 @@
 CHIPS = ("yh", "x")
 EX = ("yh", "x", "c")
 FEAT = ("z", "yl")
+PIECES = ("yl", "z")
+ROWS = ("yh", "x", "c", "yl")
 
 
 def split3(v):
@@ -28,6 +30,7 @@
     nc = lax.axis_size("c")
     nchips = lax.axis_size(CHIPS)
     nex = nc * nchips
+    nz = lax.axis_size("z")
     nf = lax.axis_size(FEAT)
     mine = target.shape[0]
     nt = mine * nex
@@ -43,7 +46,7 @@
     partial = lax.dot_general(
         train, targets, (((1,), (1,)), ((), ())), preferred_element_type=jnp.float32
     )
-    parts = lax.all_to_all(partial.reshape(nf, sub, nt), FEAT, 0, 0, tiled=True)
+    parts = lax.all_to_all(partial.reshape(nf, sub, nt), PIECES, 0, 0, tiled=True)
     logits = jnp.sum(parts, axis=0) * scale
 
     top = jnp.max(logits, axis=1, keepdims=True)
@@ -54,31 +57,47 @@
     tail = jnp.stack(split3(shift)).astype(jnp.bfloat16)
     tail = jnp.concatenate([tail, jnp.zeros((5, nt), jnp.bfloat16)], axis=0)
     block = jnp.concatenate([kern, tail], axis=0)
-    blocks = spread(block, FEAT, nf).reshape(nf, sub + 8, nt)
-    kern = blocks[:, :sub].astype(jnp.float32)
-    shifts = jnp.sum(blocks[:, sub : sub + 3].astype(jnp.float32), axis=1)
+    blocks = spread(block, "z", nz).reshape(nz, sub + 8, nt)
+    others = lax.ppermute(blocks, "yl", [(0, 1), (1, 0)])
 
+    def unpack(blocks):
+        kern = blocks[:, :sub].astype(jnp.float32)
+        return kern, jnp.sum(blocks[:, sub : sub + 3].astype(jnp.float32), axis=1)
+
+    kern, shifts = unpack(blocks)
+
+    nrows = nex * lax.axis_size("yl")
     near = jnp.max(shifts, axis=0)
     near_sum = jnp.sum(jnp.exp(shifts - near[None]) * jnp.sum(kern, axis=1), axis=0)
-    pairs = spread(jnp.stack([near, near_sum]), EX, nex).reshape(nex, 2, nt)
+    pairs = spread(jnp.stack([near, near_sum]), ROWS, nrows).reshape(nrows, 2, nt)
     far = jnp.max(pairs[:, 0], axis=0)
     far_sum = jnp.sum(jnp.exp(pairs[:, 0] - far[None]) * pairs[:, 1], axis=0)
-    factor = jnp.exp(shifts - far[None]) * (b / far_sum)[None]
-    plan = kern * factor[:, None, :]
+    col = b / far_sum
+    plan = kern * (jnp.exp(shifts - far[None]) * col[None])[:, None, :]
 
     row = a / jnp.sum(plan, axis=2, keepdims=True)
     cols = jnp.sum(plan * row, axis=(0, 1))
-    col = b / jnp.sum(spread(cols[None], EX, nex).reshape(nex, nt), axis=0)
+    col = col * (b / jnp.sum(spread(cols[None], ROWS, nrows).reshape(nrows, nt), axis=0))
 
-    plan = plan * col[None, None, :]
-    row = a / jnp.sum(plan, axis=2, keepdims=True)
-    plan = plan * row
-    cols = jnp.sum(plan, axis=(0, 1))
+    def third(kern, shifts):
+        plan = kern * (jnp.exp(shifts - far[None]) * col[None])[:, None, :]
+        plan = plan * (a / jnp.sum(plan, axis=2, keepdims=True))
+        return plan.astype(jnp.bfloat16).reshape(nz * sub, nt), jnp.sum(plan, axis=(0, 1))
+
+    plan, cols = third(kern, shifts)
+    other_plan, other_cols = third(*unpack(others))
+    cols = cols + other_cols
     cols = cols + lax.ppermute(cols, "c", [(0, 1), (1, 0)])
-    plan = plan.astype(jnp.bfloat16).reshape(rows, nt)
 
-    mixed = lax.dot_general(
-        plan, train, (((0,), (0,)), ((), ())), preferred_element_type=jnp.float32
+    yl = lax.axis_index("yl")
+    mixed = sum(
+        lax.dot_general(
+            p,
+            lax.dynamic_slice_in_dim(train, side * (nz * sub), nz * sub),
+            (((0,), (0,)), ((), ())),
+            preferred_element_type=jnp.float32,
+        )
+        for p, side in ((plan, yl), (other_plan, 1 - yl))
     )
     half = nt // nc
     halves = lax.all_to_all(mixed.reshape(nc, half, feats), "c", 0, 0, tiled=True)

time: 206 us -> 200 us (0.971)
  blocking collectives: 156 us -> 143 us
  starting transfers between devices: 14 us -> 19.4 us
    all_to_all x3, blocking collectives: 64.6 us -> 53.3 us  [spread(): return lax.all_to_all(copies, axes, 0, 0, tiled=True)]
    ppermute x0 -> x1, starting transfers between devices: none -> 3.36 us  [shards(): others = lax.ppermute(blocks, 'yl', [(0, 1), (1, 0)])]
  transfers between devices with their start and end apart: 3 -> 4, of which waited for: 2 -> 2; matrix products, arithmetic and copies ran while one was open for 2% -> 4% of each run, Pallas kernels for 0% -> 0%
where the time goes in v2:
time: 200 us; the launch traced here: 198 us
  blocking collectives  143 us (72%)
  starting transfers between devices  19.4 us (10%)
  waiting for transfers between devices  16.6 us (8%)
  other arithmetic  11.1 us (6%)
  local copies, waits for them, and re-layouts  4.93 us (2%)
  matrix products  2.77 us (1%)
    all_to_all x1, blocking collectives, shards(): lax.all_to_all(partial.reshape(nf, sub, nt), PIECES, 0, 0, tiled=True)  59.4 us
    all_to_all x3, blocking collectives, spread(): return lax.all_to_all(copies, axes, 0, 0, tiled=True)  53.3 us
    all_to_all x1, blocking collectives, shards(): lax.all_to_all(send.reshape(nchips, mine, feats + 128), CHIPS, 0, 0, tile...  23.5 us
    all_to_all x2, waiting for transfers between devices, spread(): return lax.all_to_all(copies, axes, 0, 0, tiled=True)  16.6 us
    all_to_all x2, starting transfers between devices, spread(): return lax.all_to_all(copies, axes, 0, 0, tiled=True)  13.9 us
    all_to_all x1, blocking collectives, shards(): lax.all_to_all(mixed.reshape(nc, half, feats), 'c', 0, 0, tiled=True)  6.31 us
  transfers between devices with their start and end apart: 4, of which 2 were waited for; matrix products, arithmetic and copies ran while one was open for 4% of the time, Pallas kernels for 0%

profile of v2, /device:TPU:6, one launch (start us, length us, event | category | flops | bytes accessed | tf_op | source)
XLA Modules:
  0.0 197.7 jit_solution(2410652396515028182)
XLA Ops:
  0.0 1.0 broadcast_in_dim.35
  1.0 25.9 %all_to_all.40 = bf16[16,16,1024]{2,1,0:T(8,128)(2,1)S(1)} all-to-all(bf16[16,16,1024]{2,1,0:T(8,128)(2,1)S(1)} %broadcast_in_dim.35), channel_id=1, replica_groups=mesh['yh'=4,'x'=4,'c'=2,'z'=8,'yl'=2] {'yh','x'}, dimensions={0} | all-to-all | bytes 1048576 | tf_op jit(solution)/shard_map/all_to_all | solution.py:25
  27.0 4.6 %all_to_all.41 = bf16[2,256,1024]{2,1,0:T(8,128)(2,1)S(1)} all-to-all(bf16[2,256,1024]{2,1,0:T(8,128)(2,1)S(1)} %broadcast_in_dim.37), channel_id=1, replica_groups=mesh['yh'=4,'x'=4,'c'=2,'z'=8,'yl'=2] {'c'}, dimensions={0} | all-to-all | bytes 2097152 | tf_op jit(solution)/shard_map/all_to_all | solution.py:25
  31.6 1.3 fusion.25
  32.9 59.4 %all_to_all.42 = f32[16,64,512]{2,1,0:T(8,128)} all-to-all(f32[16,64,512]{2,1,0:T(8,128)S(1)} %fusion.25), channel_id=1, replica_groups=mesh['yh'=4,'x'=4,'c'=2,'z'=8,'yl'=2] {'yl','z'}, dimensions={0} | all-to-all | bytes 4194304 | tf_op jit(solution)/shard_map/all_to_all | solution.py:49
  92.3 1.8 reduce_sum.162
  94.2 0.2 exponential_reduce_fusion
  94.8 22.8 %all_to_all.43 = bf16[8,72,512]{2,1,0:T(8,128)(2,1)S(1)} all-to-all(bf16[8,72,512]{2,1,0:T(8,128)(2,1)S(1)} %broadcast_in_dim.39), channel_id=1, replica_groups=mesh['yh'=4,'x'=4,'c'=2,'z'=8,'yl'=2] {'z'}, dimensions={0} | all-to-all | bytes 1179648 | tf_op jit(solution)/shard_map/all_to_all | solution.py:25
  117.8 0.8 copy-done.1
  118.8 0.8 broadcast_in_dim.40
  119.5 8.0 %all-to-all-start.4 = ((f32[64,2,512]{2,1,0:T(2,128)}), f32[64,2,512]{2,1,0:T(2,128)S(1)}, u32[]{:S(2)}, u32[]{:S(2)}) async-start(f32[64,2,512]{2,1,0:T(2,128)} %broadcast_in_dim.40), calls=%async_computation.4 | async-start | bytes 524288 | tf_op jit(solution)/shard_map/all_to_all | solution.py:25
  127.6 0.6 reduce_sum.167
  128.3 0.7 reshape.197
  128.9 3.4 %collective-permute-start = (bf16[8,72,512]{2,0,1:T(8,128)(2,1)}, bf16[8,72,512]{2,0,1:T(8,128)(2,1)S(1)}, u32[]{:S(2)}, u32[]{:S(2)}) collective-permute-start(bf16[8,72,512]{2,0,1:T(8,128)(2,1)} %copy-done.1), channel_id=1, source_target_pairs={{0,1},{1,0},{2,3},{3,2},{4,5},{5,4},{6,7},{7,6},{8,9},{9,8},{10,11... | collective-permute-start | bytes 1769480 | tf_op jit(solution)/shard_map/ppermute | solution.py:61
  132.3 7.5 %all-to-all-done.4 = f32[64,2,512]{2,1,0:T(2,128)S(1)} async-done(((f32[64,2,512]{2,1,0:T(2,128)}), f32[64,2,512]{2,1,0:T(2,128)S(1)}, u32[]{:S(2)}, u32[]{:S(2)}) %all-to-all-start.4) | async-done | bytes 262176 | tf_op jit(solution)/shard_map/all_to_all | solution.py:25
  139.8 0.3 slice_reduce_fusion.1
  140.1 1.3 multiply_divide_fusion
  141.6 0.2 fusion.6
  141.9 0.7 broadcast_in_dim.41
  142.6 5.9 %all-to-all-start.5 = ((f32[64,1,512]{2,1,0:T(1,128)}), f32[64,1,512]{2,1,0:T(1,128)S(1)}, u32[]{:S(2)}, u32[]{:S(2)}) async-start(f32[64,1,512]{2,1,0:T(1,128)} %broadcast_in_dim.41), calls=%async_computation.5 | async-start | bytes 262144 | tf_op jit(solution)/shard_map/all_to_all | solution.py:25
  148.5 9.2 %all-to-all-done.5 = f32[64,1,512]{2,1,0:T(1,128)S(1)} async-done(((f32[64,1,512]{2,1,0:T(1,128)}), f32[64,1,512]{2,1,0:T(1,128)S(1)}, u32[]{:S(2)}, u32[]{:S(2)}) %all-to-all-start.5) | async-done | bytes 131104 | tf_op jit(solution)/shard_map/all_to_all | solution.py:25
  157.8 1.3 divide_multiply_fusion
  159.1 0.7 exponential_multiply_fusion
  160.3 0.2 fusion.11
  160.7 0.2 fusion.5
  160.9 2.1 %collective-permute-start.1 = (f32[512]{0:T(512)S(1)}, f32[512]{0:T(512)S(1)}, u32[]{:S(2)}, u32[]{:S(2)}) collective-permute-start(f32[512]{0:T(512)S(1)} %add.21), channel_id=1, source_target_pairs={{0,16},{16,0},{1,17},{17,1},{2,18},{18,2},{3,19},{19,3},{4,20},{20... | collective-permute-start | bytes 6152 | tf_op jit(solution)/shard_map/ppermute | solution.py:90
  163.0 0.7 fusion.12
  163.8 0.8 convolution_add_fusion
  164.5 6.3 %all_to_all.44 = f32[2,256,1024]{2,1,0:T(8,128)} all-to-all(f32[2,256,1024]{2,1,0:T(8,128)S(1)} %bitcast.30), channel_id=1, replica_groups=mesh['yh'=4,'x'=4,'c'=2,'z'=8,'yl'=2] {'c'}, dimensions={0} | all-to-all | bytes 4194304 | tf_op jit(solution)/shard_map/all_to_all | solution.py:103
  170.8 1.8 reduce_sum.175
  173.3 23.5 %all_to_all.45 = bf16[16,16,1152]{2,1,0:T(8,128)(2,1)S(1)} all-to-all(bf16[16,16,1152]{2,1,0:T(8,128)(2,1)S(1)} %pad_maximum_fusion), channel_id=1, replica_groups=mesh['yh'=4,'x'=4,'c'=2,'z'=8,'yl'=2] {'yh','x'}, dimensions={0} | all-to-all | bytes 1179648 | tf_op jit(solution)/shard_map/all_to_all | solution.py:110
  197.0 0.7 fusion.18
  (50 shorter events, 2.8 us)
Async XLA Ops:
  0.0 31.6 %copy-start = (bf16[1024,1024]{1,0:T(8,128)(2,1)S(1)}, bf16[1024,1024]{1,0:T(8,128)(2,1)}, u32[]{:S(2)}) copy-start(bf16[1024,1024]{1,0:T(8,128)(2,1)} %param.3) | copy-start | bytes 6291460
  94.7 32.8 %copy-start.3 = (f32[512]{0:T(512)S(1)}, f32[512]{0:T(512)}, u32[]{:S(2)}) copy-start(f32[512]{0:T(512)} %param.5) | copy-start | bytes 6148
  117.8 0.8 copy-start.1
  119.5 20.3 %all-to-all-start.4 = ((f32[64,2,512]{2,1,0:T(2,128)}), f32[64,2,512]{2,1,0:T(2,128)S(1)}, u32[]{:S(2)}, u32[]{:S(2)}) async-start(f32[64,2,512]{2,1,0:T(2,128)} %broadcast_in_dim.40), calls=%async_computation.4 | async-start | bytes 524288 | tf_op jit(solution)/shard_map/all_to_all | solution.py:25
  128.9 19.5 %collective-permute-start = (bf16[8,72,512]{2,0,1:T(8,128)(2,1)}, bf16[8,72,512]{2,0,1:T(8,128)(2,1)S(1)}, u32[]{:S(2)}, u32[]{:S(2)}) collective-permute-start(bf16[8,72,512]{2,0,1:T(8,128)(2,1)} %copy-done.1), channel_id=1, source_target_pairs={{0,1},{1,0},{2,3},{3,2},{4,5},{5,4},{6,7},{7,6},{8,9},{9,8},{10,11... | collective-permute-start | bytes 1769480 | tf_op jit(solution)/shard_map/ppermute | solution.py:61
  140.0 1.8 copy-start.2
  142.6 15.1 %all-to-all-start.5 = ((f32[64,1,512]{2,1,0:T(1,128)}), f32[64,1,512]{2,1,0:T(1,128)S(1)}, u32[]{:S(2)}, u32[]{:S(2)}) async-start(f32[64,1,512]{2,1,0:T(1,128)} %broadcast_in_dim.41), calls=%async_computation.5 | async-start | bytes 262144 | tf_op jit(solution)/shard_map/all_to_all | solution.py:25
  160.9 11.7 %collective-permute-start.1 = (f32[512]{0:T(512)S(1)}, f32[512]{0:T(512)S(1)}, u32[]{:S(2)}, u32[]{:S(2)}) collective-permute-start(f32[512]{0:T(512)S(1)} %add.21), channel_id=1, source_target_pairs={{0,16},{16,0},{1,17},{17,1},{2,18},{18,2},{3,19},{19,3},{4,20},{20... | collective-permute-start | bytes 6152 | tf_op jit(solution)/shard_map/ppermute | solution.py:90

commit v3 on v1

v3 whole, which is shorter than its diff:
```python
import functools
import math

import jax
import jax.numpy as jnp
from jax import lax
from jax.experimental import pallas as pl
from jax.experimental.pallas import tpu as pltpu
from jax.sharding import Mesh, PartitionSpec as P


F = 16384
CHIPS = ("yh", "x")
EX = ("yh", "x", "c")
FEAT = ("z", "yl")
PIECES = ("yl", "z")
ROWS = ("yh", "x", "c", "yl")
TAIL = 8
SWAP = [(0, 1), (1, 0)]
VMEM = pltpu.VMEM
SMALL = pltpu.CompilerParams(vmem_limit_bytes=4 * 2**20)
LARGE = pltpu.CompilerParams(vmem_limit_bytes=24 * 2**20)


def split3(v):
    hi = lax.reduce_precision(v, 8, 7)
    rest = v - hi
    mid = lax.reduce_precision(rest, 8, 7)
    return hi, mid, rest - mid


def spread(block, axes, n):
    copies = jnp.broadcast_to(block[None], (n,) + block.shape)
    return lax.all_to_all(copies, axes, 0, 0, tiled=True)


def block_shift(ref, z, sub):
    tail = ref[z, sub : sub + TAIL, :].astype(jnp.float32)
    return jnp.sum(tail, axis=0, keepdims=True)


def statistics_kernel(sub, own_ref, out_ref):
    nz = own_ref.shape[0]
    shifts = [block_shift(own_ref, z, sub) for z in range(nz)]
    top = functools.reduce(jnp.maximum, shifts)
    total = jnp.zeros_like(top)
    for z in range(nz):
        kern = own_ref[z, :sub, :].astype(jnp.float32)
        total += jnp.exp(shifts[z] - top) * jnp.sum(kern, axis=0, keepdims=True)
    log_sum = top + jnp.log(total)
    out_ref[...] = jnp.broadcast_to(log_sum[None], out_ref.shape)


def columns_kernel(sub, a, stats_ref, own_ref, b_ref, far_ref, col_ref, out_ref):
    nz = own_ref.shape[0]
    stats = stats_ref[:, 0, :]
    far = jnp.max(stats, axis=0, keepdims=True)
    col = b_ref[...] / jnp.sum(jnp.exp(stats - far), axis=0, keepdims=True)
    cols = jnp.zeros_like(col)
    for z in range(nz):
        factor = jnp.exp(block_shift(own_ref, z, sub) - far) * col
        plan = own_ref[z, :sub, :].astype(jnp.float32) * factor
        row = a / jnp.sum(plan, axis=1, keepdims=True)
        cols += jnp.sum(plan * row, axis=0, keepdims=True)
    far_ref[...] = far
    col_ref[...] = col
    out_ref[...] = jnp.broadcast_to(cols[None], out_ref.shape)


def mixture_kernel(
    sub,
    a,
    place_ref,
    sums_ref,
    far_ref,
    col_ref,
    b_ref,
    own_ref,
    other_ref,
    core_own_ref,
    core_other_ref,
    train_ref,
    core_train_ref,
    out_ref,
    plan_ref,
    cols_ref,
    train_vmem,
    sems,
):
    nz, _, nt = own_ref.shape
    half = nt // 2
    rows = nz * sub
    c, yl = place_ref[0], place_ref[1]
    copies = [
        pltpu.make_async_copy(src, train_vmem.at[k], sems.at[k])
        for k, src in enumerate((train_ref, core_train_ref))
    ]
    for copy in copies:
        copy.start()
    far = far_ref[...]
    total = jnp.sum(sums_ref[:, 0, :], axis=0, keepdims=True)
    col = col_ref[...] * (b_ref[...] / total)

    refs = ((own_ref, 0, 0), (other_ref, 0, 1), (core_own_ref, 1, 0), (core_other_ref, 1, 1))

    def step(z, cols):
        for ref, k, flip in refs:
            tail = ref[z, sub : sub + TAIL, :].astype(jnp.float32)
            shift = jnp.sum(tail, axis=0, keepdims=True)
            plan = ref[z, :sub, :].astype(jnp.float32) * (jnp.exp(shift - far) * col)
            plan = plan * (a / jnp.sum(plan, axis=1, keepdims=True))
            cols = cols + jnp.sum(plan, axis=0, keepdims=True)
            side = yl + flip * (1 - 2 * yl)
            start = pl.multiple_of(side * rows + z * sub, sub)
            small = plan.astype(jnp.bfloat16)
            plan_ref[0, k, pl.ds(start, sub), :] = small[:, :half]
            plan_ref[1, k, pl.ds(start, sub), :] = small[:, half:]
        return cols

    cols = lax.fori_loop(0, nz, step, jnp.zeros((1, nt), jnp.float32))
    cols_ref[0] = cols[:, :half]
    cols_ref[1] = cols[:, half:]

    mixed = jnp.zeros((half, train_ref.shape[1]), jnp.float32)
    for k in range(2):
        copies[k].wait()
        mixed += lax.dot_general(
            plan_ref[c, k],
            train_vmem[k],
            (((0,), (0,)), ((), ())),
            preferred_element_type=jnp.float32,
        )
    nchips, mine, _ = out_ref.shape
    feats = train_ref.shape[1]
    out_ref[:, :, :feats] = mixed.astype(jnp.bfloat16).reshape(nchips, mine, feats)

    my_cols = cols_ref[c]
    lane = lax.broadcasted_iota(jnp.int32, (128, 128), 1)
    per = 128 // mine
    for k in range(half // 128):
        v = jnp.broadcast_to(my_cols[:, k * 128 : (k + 1) * 128], (128, 128)).T
        hi = v.astype(jnp.bfloat16).astype(jnp.float32)
        mid = (v - hi).astype(jnp.bfloat16).astype(jnp.float32)
        lo = v - hi - mid
        tail = jnp.where(lane == 0, hi, jnp.where(lane == 1, mid, lo))
        out_ref[k * per : (k + 1) * per, :, feats:] = tail.astype(jnp.bfloat16).reshape(
            per, mine, 128
        )


def shards(train, target, mass):
    rows, feats = train.shape
    nc = lax.axis_size("c")
    nchips = lax.axis_size(CHIPS)
    nex = nc * nchips
    nz = lax.axis_size("z")
    nf = lax.axis_size(FEAT)
    nrows = lax.axis_size(ROWS)
    mine = target.shape[0]
    nt = mine * nex
    half = nt // nc
    sub = rows // nf
    scale = 3.0 / math.sqrt(F)
    a = 1.0 / (rows * nex)
    full = pl.BlockSpec(memory_space=VMEM)
    anywhere = pl.BlockSpec(memory_space=pl.ANY)

    core_train = lax.ppermute(train, "c", SWAP)

    same_core = spread(target, CHIPS, nchips).reshape(nchips * mine, feats)
    targets = spread(same_core, "c", nc).reshape(nt, feats)
    mass = mass.reshape(nchips, nc, mine).transpose(1, 0, 2).reshape(1, nt)
    b = mass / jnp.sum(mass)

    partial = lax.dot_general(
        train, targets, (((1,), (1,)), ((), ())), preferred_element_type=jnp.float32
    )
    parts = lax.all_to_all(partial.reshape(nf, sub, nt), PIECES, 0, 0, tiled=True)
    logits = jnp.sum(parts, axis=0) * scale

    top = jnp.max(logits, axis=1, keepdims=True)
    total = jnp.sum(jnp.exp(logits - top), axis=1, keepdims=True)
    v = logits - top - jnp.log(total)
    shift = jnp.max(v, axis=0)
    kern = jnp.exp(v - shift[None, :]).astype(jnp.bfloat16)
    tail = jnp.stack(split3(shift)).astype(jnp.bfloat16)
    tail = jnp.concatenate([tail, jnp.zeros((TAIL - 3, nt), jnp.bfloat16)], axis=0)
    block = jnp.concatenate([kern, tail], axis=0)

    own = spread(block, "z", nz).reshape(nz, sub + TAIL, nt)
    other = lax.ppermute(own, "yl", SWAP)
    core_own = lax.ppermute(own, "c", SWAP)

    vector = jax.ShapeDtypeStruct((1, nt), jnp.float32)
    copies = jax.ShapeDtypeStruct((nrows, 1, nt), jnp.float32)
    stats = pl.pallas_call(
        functools.partial(statistics_kernel, sub),
        out_shape=copies,
        in_specs=[full],
        out_specs=full,
        compiler_params=SMALL,
    )(own)
    stats = lax.all_to_all(stats, ROWS, 0, 0, tiled=True)
    far, col, sums = pl.pallas_call(
        functools.partial(columns_kernel, sub, a),
        out_shape=(vector, vector, copies),
        in_specs=[full] * 3,
        out_specs=(full,) * 3,
        compiler_params=SMALL,
    )(stats, own, b)
    sums = lax.all_to_all(sums, ROWS, 0, 0, tiled=True)
    other, _ = lax.optimization_barrier((other, col))
    core_other = lax.ppermute(other, "c", SWAP)

    place = jnp.stack([lax.axis_index("c"), lax.axis_index("yl")]).astype(jnp.int32)
    send = pl.pallas_call(
        functools.partial(mixture_kernel, sub, a),
        out_shape=jax.ShapeDtypeStruct((nchips, mine, feats + 128), jnp.bfloat16),
        in_specs=[pl.BlockSpec(memory_space=pltpu.SMEM)] + [full] * 8 + [anywhere] * 2,
        out_specs=full,
        scratch_shapes=[
            VMEM((nc, 2, rows, half), jnp.bfloat16),
            VMEM((nc, 1, half), jnp.float32),
            VMEM((2, rows, feats), jnp.bfloat16),
            pltpu.SemaphoreType.DMA((2,)),
        ],
        compiler_params=LARGE,
    )(place, sums, far, col, b, own, other, core_own, core_other, train, core_train)
    got = lax.all_to_all(send, CHIPS, 0, 0, tiled=True)
    got = jnp.sum(got.astype(jnp.float32), axis=0)
    mass_in = jnp.sum(got[:, feats : feats + 3], axis=1, keepdims=True)
    return (got[:, :feats] / mass_in).astype(jnp.bfloat16)


def solution(mesh):
    fine = Mesh(mesh.devices.reshape(4, 4, 2, 8, 2), ("yh", "x", "c", "z", "yl"))

    return jax.shard_map(
        shards,
        mesh=fine,
        in_specs=(P(EX, FEAT), P(EX, FEAT), P()),
        out_specs=P(EX, FEAT),
        check_vma=False,
    )
```

time: 206 us -> 192 us (0.932)
  blocking collectives: 156 us -> 113 us
  waiting for transfers between devices: 17 us -> 33.5 us
  starting transfers between devices: 14 us -> 29.4 us
  Pallas kernels: 0 us -> 6.32 us
  other arithmetic: 10.2 us -> 4.52 us
  local copies, waits for them, and re-layouts: 4.46 us -> 2.01 us
    all_to_all x3 -> x2, blocking collectives: 64.6 us -> 30.6 us  [spread(): return lax.all_to_all(copies, axes, 0, 0, tiled=True)]
    all_to_all x0 -> x2, waiting for transfers between devices: none -> 16.6 us  [the longest x1 9.12 us: shards(): sums = lax.all_to_all(sums, ROWS, 0, 0, tiled=True)]
    all_to_all x0 -> x2, starting transfers between devices: none -> 15.5 us  [the longest x1 8.7 us: shards(): sums = lax.all_to_all(sums, ROWS, 0, 0, tiled=True)]
    all_to_all x3 -> x2, blocking collectives: 90.9 us -> 82.7 us  [the longest x1 59.4 us: shards(): lax.all_to_all(partial.reshape(nf, sub, nt), PIECES, 0, 0, tiled=True)]
    all_to_all x2 -> x1, starting transfers between devices: 12 us -> 4.24 us  [spread(): return lax.all_to_all(copies, axes, 0, 0, tiled=True)]
    ppermute x1 -> x4, starting transfers between devices: 1.98 us -> 9.65 us  [the longest x1 3.71 us: shards(): other = lax.ppermute(own, 'yl', SWAP)]
    pallas_call x0 -> x3, Pallas kernels: none -> 6.32 us  [the longest x1 4.48 us: shards(): pl.pallas_call(functools.partial(mixture_kernel, sub, a), out_shape=jax.S...]
    reduce_sum x9 -> x0, other arithmetic: 3.19 us -> none  [the longest x1 1.81 us: shards(): mixed = jnp.sum(halves, axis=0)]
  transfers between devices with their start and end apart: 3 -> 7, of which waited for: 2 -> 3; matrix products, arithmetic and copies ran while one was open for 2% -> 1% of each run, Pallas kernels for 0% -> 1%
where the time goes in v3:
time: 192 us; the launch traced here: 191 us
  blocking collectives  113 us (59%)
  waiting for transfers between devices  33.5 us (17%)
  starting transfers between devices  29.4 us (15%)
  Pallas kernels  6.32 us (3%)
  other arithmetic  4.52 us (2%)
  local copies, waits for them, and re-layouts  2.01 us (1%)
    all_to_all x1, blocking collectives, shards(): lax.all_to_all(partial.reshape(nf, sub, nt), PIECES, 0, 0, tiled=True)  59.4 us
    all_to_all x2, blocking collectives, spread(): return lax.all_to_all(copies, axes, 0, 0, tiled=True)  30.6 us
    all_to_all x1, blocking collectives, shards(): got = lax.all_to_all(send, CHIPS, 0, 0, tiled=True)  23.2 us
    all_to_all x1, waiting for transfers between devices, spread(): return lax.all_to_all(copies, axes, 0, 0, tiled=True)  16.9 us
    all_to_all x1, waiting for transfers between devices, shards(): sums = lax.all_to_all(sums, ROWS, 0, 0, tiled=True)  9.12 us
    all_to_all x1, starting transfers between devices, shards(): sums = lax.all_to_all(sums, ROWS, 0, 0, tiled=True)  8.7 us
    all_to_all x1, waiting for transfers between devices, shards(): stats = lax.all_to_all(stats, ROWS, 0, 0, tiled=True)  7.49 us
    all_to_all x1, starting transfers between devices, shards(): stats = lax.all_to_all(stats, ROWS, 0, 0, tiled=True)  6.82 us
  transfers between devices with their start and end apart: 7, of which 3 were waited for; matrix products, arithmetic and copies ran while one was open for 1% of the time, Pallas kernels for 1%

profile of v3, /device:TPU:6, one launch (start us, length us, event | category | flops | bytes accessed | tf_op | source)
XLA Modules:
  0.0 190.5 jit_solution(4586280313205748383)
XLA Ops:
  0.0 0.8 broadcast_in_dim.10
  0.8 25.9 %all_to_all.35 = bf16[16,16,1024]{2,1,0:T(8,128)(2,1)S(1)} all-to-all(bf16[16,16,1024]{2,1,0:T(8,128)(2,1)S(1)} %broadcast_in_dim.10), channel_id=1, replica_groups=mesh['yh'=4,'x'=4,'c'=2,'z'=8,'yl'=2] {'yh','x'}, dimensions={0} | all-to-all | bytes 1048576 | tf_op jit(solution)/shard_map/all_to_all | solution.py:34
  26.8 0.1 broadcast_in_dim.12
  26.9 4.7 %all_to_all.36 = bf16[2,256,1024]{2,1,0:T(8,128)(2,1)S(1)} all-to-all(bf16[2,256,1024]{2,1,0:T(8,128)(2,1)S(1)} %broadcast_in_dim.12), channel_id=1, replica_groups=mesh['yh'=4,'x'=4,'c'=2,'z'=8,'yl'=2] {'c'}, dimensions={0} | all-to-all | bytes 2097152 | tf_op jit(solution)/shard_map/all_to_all | solution.py:34
  31.6 1.3 fusion.2
  32.9 59.4 %all_to_all.37 = f32[16,64,512]{2,1,0:T(8,128)} all-to-all(f32[16,64,512]{2,1,0:T(8,128)S(1)} %fusion.2), channel_id=1, replica_groups=mesh['yh'=4,'x'=4,'c'=2,'z'=8,'yl'=2] {'yl','z'}, dimensions={0} | all-to-all | bytes 4194304 | tf_op jit(solution)/shard_map/all_to_all | solution.py:178
  92.3 1.8 reduce_sum.45
  94.1 0.1 multiply_reduce_fusion
  94.2 0.2 exponential_reduce_fusion
  94.4 0.1 subtract_reduce_fusion
  94.5 0.1 exponential_convert_fusion
  94.7 0.9 broadcast_in_dim.14
  95.6 4.2 %all-to-all-start.3 = ((bf16[8,72,512]{2,1,0:T(8,128)(2,1)}), bf16[8,72,512]{2,1,0:T(8,128)(2,1)S(1)}, u32[]{:S(2)}, u32[]{:S(2)}) async-start(bf16[8,72,512]{2,1,0:T(8,128)(2,1)} %broadcast_in_dim.14), calls=%async_computation.3 | async-start | bytes 1179648 | tf_op jit(solution)/shard_map/all_to_all | solution.py:34
  99.8 1.9 %collective-permute-start.3 = (bf16[1024,1024]{1,0:T(8,128)(2,1)S(1)}, bf16[1024,1024]{1,0:T(8,128)(2,1)}, u32[]{:S(2)}, u32[]{:S(2)}) collective-permute-start(bf16[1024,1024]{1,0:T(8,128)(2,1)S(1)} %copy-done), channel_id=1, source_target_pairs={{0,16},{16,0},{1,17},{17,1},{2,18},{18,2},{3,19},{19,3},{4,20},{20... | collective-permute-start | bytes 6291464 | tf_op jit(solution)/shard_map/ppermute | solution.py:168
  101.7 16.9 %all-to-all-done.3.own_ref = bf16[8,72,512]{2,1,0:T(8,128)(2,1)S(1)} async-done(((bf16[8,72,512]{2,1,0:T(8,128)(2,1)}), bf16[8,72,512]{2,1,0:T(8,128)(2,1)S(1)}, u32[]{:S(2)}, u32[]{:S(2)}) %all-to-all-start.3) | async-done | bytes 589856 | tf_op jit(solution)/shard_map/all_to_all | solution.py:34
  118.6 3.7 %collective-permute-start = (bf16[8,72,512]{2,1,0:T(8,128)(2,1)S(1)}, bf16[8,72,512]{2,1,0:T(8,128)(2,1)S(1)}, u32[]{:S(2)}, u32[]{:S(2)}) collective-permute-start(bf16[8,72,512]{2,1,0:T(8,128)(2,1)S(1)} %all-to-all-done.3.own_ref), channel_id=1, source_target_pairs={{0,1},{1,0},{2,3},{3,2},{4,5},{5,4},{6,7},{7,6},{8,9},{9,8},{10,11... | collective-permute-start | bytes 1769480 | tf_op jit(solution)/shard_map/ppermute | solution.py:191
  122.3 0.8 shard_map.37
  123.1 6.8 %all-to-all-start.4 = ((f32[64,1,512]{2,1,0:T(1,128)}), f32[64,1,512]{2,1,0:T(1,128)S(1)}, u32[]{:S(2)}, u32[]{:S(2)}) async-start(f32[64,1,512]{2,1,0:T(1,128)} %shard_map.37), calls=%async_computation.4 | async-start | bytes 262144 | tf_op jit(solution)/shard_map/all_to_all | solution.py:203
  130.0 0.6 reduce_sum.47
  130.6 0.6 broadcast_divide_fusion
  131.2 0.1 div.22
  131.4 2.0 %collective-permute-start.1 = (bf16[8,72,512]{2,1,0:T(8,128)(2,1)S(1)}, bf16[8,72,512]{2,1,0:T(8,128)(2,1)}, u32[]{:S(2)}, u32[]{:S(2)}) collective-permute-start(bf16[8,72,512]{2,1,0:T(8,128)(2,1)S(1)} %all-to-all-done.3.own_ref), channel_id=1, source_target_pairs={{0,16},{16,0},{1,17},{17,1},{2,18},{18,2},{3,19},{19,3},{4,20},{20... | collective-permute-start | bytes 1769480 | tf_op jit(solution)/shard_map/ppermute | solution.py:192
  133.4 7.5 %all-to-all-done.4.stats_ref = f32[64,1,512]{2,1,0:T(1,128)S(1)} async-done(((f32[64,1,512]{2,1,0:T(1,128)}), f32[64,1,512]{2,1,0:T(1,128)S(1)}, u32[]{:S(2)}, u32[]{:S(2)}) %all-to-all-start.4) | async-done | bytes 131104 | tf_op jit(solution)/shard_map/all_to_all | solution.py:203
  140.9 1.0 shard_map.38
  142.0 2.0 %collective-permute-start.2 = (bf16[8,72,512]{2,1,0:T(8,128)(2,1)S(1)}, bf16[8,72,512]{2,1,0:T(8,128)(2,1)}, u32[]{:S(2)}, u32[]{:S(2)}) collective-permute-start(bf16[8,72,512]{2,1,0:T(8,128)(2,1)S(1)} %collective-permute-done.other_ref), channel_id=1, source_target_pairs={{0,16},{16,0},{1,17},{17,1},{2,18},{18,2},{3,19},{19,3},{4,20},{20... | collective-permute-start | bytes 1769480 | tf_op jit(solution)/shard_map/ppermute | solution.py:213
  144.0 8.7 %all-to-all-start.5 = ((f32[64,1,512]{2,1,0:T(1,128)}), f32[64,1,512]{2,1,0:T(1,128)S(1)}, u32[]{:S(2)}, u32[]{:S(2)}) async-start(f32[64,1,512]{2,1,0:T(1,128)} %get-tuple-element.9), calls=%async_computation.5 | async-start | bytes 262144 | tf_op jit(solution)/shard_map/all_to_all | solution.py:211
  152.8 9.1 %all-to-all-done.5.sums_ref = f32[64,1,512]{2,1,0:T(1,128)S(1)} async-done(((f32[64,1,512]{2,1,0:T(1,128)}), f32[64,1,512]{2,1,0:T(1,128)S(1)}, u32[]{:S(2)}, u32[]{:S(2)}) %all-to-all-start.5) | async-done | bytes 131104 | tf_op jit(solution)/shard_map/all_to_all | solution.py:211
  161.9 4.5 %shard_map.39 = bf16[16,16,1152]{2,1,0:T(8,128)(2,1)S(1)} custom-call(s32[2]{0:T(128)S(1)} %pad_add_fusion.place_ref, f32[64,1,512]{2,1,0:T(1,128)S(1)} %all-to-all-done.5.sums_ref, f32[1,512]{1,0:T(1,128)S(1)} %get-tuple-element.10.far_ref, f32[1,512]{1,0:T(1,128)S(1)} %get-tuple-element.11.col_ref, f32[1,512]{1,0:T(1,128)S(1)} %div.24.b_ref, ...), custom_call_target="tpu_custom_call" | custom-call | tf_op jit(solution)/shard_map/pallas_call | solution.py:216
  166.4 23.2 %all_to_all.38 = bf16[16,16,1152]{2,1,0:T(8,128)(2,1)S(1)} all-to-all(bf16[16,16,1152]{2,1,0:T(8,128)(2,1)S(1)} %shard_map.39), channel_id=1, replica_groups=mesh['yh'=4,'x'=4,'c'=2,'z'=8,'yl'=2] {'yh','x'}, dimensions={0} | all-to-all | bytes 1179648 | tf_op jit(solution)/shard_map/all_to_all | solution.py:229
  189.6 0.1 convert_reduce_fusion
  189.7 0.1 slice_reduce_fusion
  189.8 0.7 fusion
  (15 shorter events, 0.2 us)
Async XLA Ops:
  26.8 4.8 %copy-start = (bf16[1024,1024]{1,0:T(8,128)(2,1)S(1)}, bf16[1024,1024]{1,0:T(8,128)(2,1)}, u32[]{:S(2)}) copy-start(bf16[1024,1024]{1,0:T(8,128)(2,1)} %train_ref.1) | copy-start | bytes 6291460
  94.1 35.9 %copy-start.1 = (f32[512]{0:T(512)S(1)}, f32[512]{0:T(512)}, u32[]{:S(2)}) copy-start(f32[512]{0:T(512)} %param.5) | copy-start | bytes 6148
  95.6 23.0 %all-to-all-start.3 = ((bf16[8,72,512]{2,1,0:T(8,128)(2,1)}), bf16[8,72,512]{2,1,0:T(8,128)(2,1)S(1)}, u32[]{:S(2)}, u32[]{:S(2)}) async-start(bf16[8,72,512]{2,1,0:T(8,128)(2,1)} %broadcast_in_dim.14), calls=%async_computation.3 | async-start | bytes 1179648 | tf_op jit(solution)/shard_map/all_to_all | solution.py:34
  99.8 53.0 %collective-permute-start.3 = (bf16[1024,1024]{1,0:T(8,128)(2,1)S(1)}, bf16[1024,1024]{1,0:T(8,128)(2,1)}, u32[]{:S(2)}, u32[]{:S(2)}) collective-permute-start(bf16[1024,1024]{1,0:T(8,128)(2,1)S(1)} %copy-done), channel_id=1, source_target_pairs={{0,16},{16,0},{1,17},{17,1},{2,18},{18,2},{3,19},{19,3},{4,20},{20... | collective-permute-start | bytes 6291464 | tf_op jit(solution)/shard_map/ppermute | solution.py:168
  118.6 23.4 %collective-permute-start = (bf16[8,72,512]{2,1,0:T(8,128)(2,1)S(1)}, bf16[8,72,512]{2,1,0:T(8,128)(2,1)S(1)}, u32[]{:S(2)}, u32[]{:S(2)}) collective-permute-start(bf16[8,72,512]{2,1,0:T(8,128)(2,1)S(1)} %all-to-all-done.3.own_ref), channel_id=1, source_target_pairs={{0,1},{1,0},{2,3},{3,2},{4,5},{5,4},{6,7},{7,6},{8,9},{9,8},{10,11... | collective-permute-start | bytes 1769480 | tf_op jit(solution)/shard_map/ppermute | solution.py:191
  123.1 17.8 %all-to-all-start.4 = ((f32[64,1,512]{2,1,0:T(1,128)}), f32[64,1,512]{2,1,0:T(1,128)S(1)}, u32[]{:S(2)}, u32[]{:S(2)}) async-start(f32[64,1,512]{2,1,0:T(1,128)} %shard_map.37), calls=%async_computation.4 | async-start | bytes 262144 | tf_op jit(solution)/shard_map/all_to_all | solution.py:203
  131.4 30.5 %collective-permute-start.1 = (bf16[8,72,512]{2,1,0:T(8,128)(2,1)S(1)}, bf16[8,72,512]{2,1,0:T(8,128)(2,1)}, u32[]{:S(2)}, u32[]{:S(2)}) collective-permute-start(bf16[8,72,512]{2,1,0:T(8,128)(2,1)S(1)} %all-to-all-done.3.own_ref), channel_id=1, source_target_pairs={{0,16},{16,0},{1,17},{17,1},{2,18},{18,2},{3,19},{19,3},{4,20},{20... | collective-permute-start | bytes 1769480 | tf_op jit(solution)/shard_map/ppermute | solution.py:192
  142.0 19.9 %collective-permute-start.2 = (bf16[8,72,512]{2,1,0:T(8,128)(2,1)S(1)}, bf16[8,72,512]{2,1,0:T(8,128)(2,1)}, u32[]{:S(2)}, u32[]{:S(2)}) collective-permute-start(bf16[8,72,512]{2,1,0:T(8,128)(2,1)S(1)} %collective-permute-done.other_ref), channel_id=1, source_target_pairs={{0,16},{16,0},{1,17},{17,1},{2,18},{18,2},{3,19},{19,3},{4,20},{20... | collective-permute-start | bytes 1769480 | tf_op jit(solution)/shard_map/ppermute | solution.py:213
  144.0 17.9 %all-to-all-start.5 = ((f32[64,1,512]{2,1,0:T(1,128)}), f32[64,1,512]{2,1,0:T(1,128)S(1)}, u32[]{:S(2)}, u32[]{:S(2)}) async-start(f32[64,1,512]{2,1,0:T(1,128)} %get-tuple-element.9), calls=%async_computation.5 | async-start | bytes 262144 | tf_op jit(solution)/shard_map/all_to_all | solution.py:211

commit v4 on v3

--- a/solution.py
+++ b/solution.py
@@ -18,15 +18,89 @@
 TAIL = 8
 SWAP = [(0, 1), (1, 0)]
 VMEM = pltpu.VMEM
+MIDDLE = pltpu.CompilerParams(vmem_limit_bytes=12 * 2**20)
 SMALL = pltpu.CompilerParams(vmem_limit_bytes=4 * 2**20)
 LARGE = pltpu.CompilerParams(vmem_limit_bytes=24 * 2**20)
 
 
-def split3(v):
-    hi = lax.reduce_precision(v, 8, 7)
-    rest = v - hi
-    mid = lax.reduce_precision(rest, 8, 7)
-    return hi, mid, rest - mid
+SPAN = 249.0
+BASE = 124.0
+
+
+def round_up(v):
+    return (v * (1.0 + 2.0**-7)).astype(jnp.bfloat16).astype(jnp.float32)
+
+
+def encode_kernel(sub, train_ref, targets_ref, out_ref, partial_ref):
+    _, _, nt = out_ref.shape
+    rows = train_ref.shape[0]
+    step = partial_ref.shape[0]
+    on_diagonal = lax.broadcasted_iota(jnp.int32, (sub, 128), 0) == (
+        lax.broadcasted_iota(jnp.int32, (sub, 128), 1)
+    )
+    for start in range(0, rows, step):
+        partial_ref[...] = lax.dot_general(
+            train_ref[start : start + step, :],
+            targets_ref[...],
+            (((1,), (1,)), ((), ())),
+            preferred_element_type=jnp.float32,
+        )
+        for j in range(step // sub):
+            k = start // sub + j
+            p = partial_ref[j * sub : (j + 1) * sub, :]
+            high = jnp.max(p, axis=1, keepdims=True)
+            low = jnp.min(p, axis=1, keepdims=True)
+            p = p - 0.5 * (high + low)
+            wide = jnp.max(jnp.abs(p), axis=1, keepdims=True)
+            row = round_up(jnp.maximum(wide, 1e-30))
+            p = p * (1.0 / row)
+            col = round_up(jnp.maximum(jnp.max(jnp.abs(p), axis=0, keepdims=True), 1e-30))
+            u = p * (1.0 / col)
+            code = jnp.exp2(jnp.minimum(jnp.abs(u), 1.0) * SPAN - BASE)
+            out_ref[k, :sub, :] = jnp.where(u < 0, -code, code).astype(jnp.bfloat16)
+            row = jnp.sum(jnp.where(on_diagonal, row, 0.0), axis=0, keepdims=True)
+            row = jnp.concatenate([row, jnp.zeros((1, nt - 128), jnp.float32)], axis=1)
+            index = lax.broadcasted_iota(jnp.int32, (TAIL, nt), 0)
+            tail = jnp.where(index == 0, col, jnp.where(index == 1, row, 0.0))
+            out_ref[k, sub : sub + TAIL, :] = tail.astype(jnp.bfloat16)
+
+
+def rows_kernel(sub, scale, codes_ref, out_ref, logits_ref):
+    nf, _, nt = codes_ref.shape
+    nz = out_ref.shape[0]
+    on_diagonal = lax.broadcasted_iota(jnp.int32, (sub, 128), 0) == (
+        lax.broadcasted_iota(jnp.int32, (sub, 128), 1)
+    )
+    cols, rows = [], []
+    for k in range(nf):
+        tail = codes_ref[k, sub : sub + TAIL, :].astype(jnp.float32)
+        cols.append(tail[0:1, :] * (scale / SPAN))
+        row = jnp.where(on_diagonal, tail[1:2, :128], 0.0)
+        rows.append(jnp.sum(row, axis=1, keepdims=True))
+    for start in range(0, nt, 128):
+        part = slice(start, start + 128)
+        total = jnp.zeros((sub, 128), jnp.float32)
+        for k in range(nf):
+            code = codes_ref[k, :sub, part].astype(jnp.float32)
+            size = jnp.log(jnp.abs(code)) * (1.0 / math.log(2.0)) + BASE
+            size = jnp.where(code < 0, -size, size)
+            total += size * cols[k][:, part] * rows[k]
+        logits_ref[:, part] = total
+
+    logits = logits_ref[...]
+    top = jnp.max(logits, axis=1, keepdims=True)
+    v = logits - top
+    v = v - jnp.log(jnp.sum(jnp.exp(v), axis=1, keepdims=True))
+    shift = jnp.max(v, axis=0, keepdims=True)
+    kern = jnp.exp(v - shift).astype(jnp.bfloat16)
+    hi = shift.astype(jnp.bfloat16).astype(jnp.float32)
+    mid = (shift - hi).astype(jnp.bfloat16).astype(jnp.float32)
+    index = lax.broadcasted_iota(jnp.int32, (TAIL, nt), 0)
+    lo = jnp.where(index == 2, shift - hi - mid, 0.0)
+    tail = jnp.where(index == 0, hi, jnp.where(index == 1, mid, lo)).astype(jnp.bfloat16)
+    for z in range(nz):
+        out_ref[z, :sub, :] = kern
+        out_ref[z, sub : sub + TAIL, :] = tail
 
 
 def spread(block, axes, n):
@@ -172,22 +246,25 @@
     mass = mass.reshape(nchips, nc, mine).transpose(1, 0, 2).reshape(1, nt)
     b = mass / jnp.sum(mass)
 
-    partial = lax.dot_general(
-        train, targets, (((1,), (1,)), ((), ())), preferred_element_type=jnp.float32
-    )
-    parts = lax.all_to_all(partial.reshape(nf, sub, nt), PIECES, 0, 0, tiled=True)
-    logits = jnp.sum(parts, axis=0) * scale
-
-    top = jnp.max(logits, axis=1, keepdims=True)
-    total = jnp.sum(jnp.exp(logits - top), axis=1, keepdims=True)
-    v = logits - top - jnp.log(total)
-    shift = jnp.max(v, axis=0)
-    kern = jnp.exp(v - shift[None, :]).astype(jnp.bfloat16)
-    tail = jnp.stack(split3(shift)).astype(jnp.bfloat16)
-    tail = jnp.concatenate([tail, jnp.zeros((TAIL - 3, nt), jnp.bfloat16)], axis=0)
-    block = jnp.concatenate([kern, tail], axis=0)
-
-    own = spread(block, "z", nz).reshape(nz, sub + TAIL, nt)
+    codes = pl.pallas_call(
+        functools.partial(encode_kernel, sub),
+        out_shape=jax.ShapeDtypeStruct((nf, sub + TAIL, nt), jnp.bfloat16),
+        in_specs=[full] * 2,
+        out_specs=full,
+        scratch_shapes=[VMEM((4 * sub, nt), jnp.float32)],
+        compiler_params=MIDDLE,
+    )(train, targets)
+    codes = lax.all_to_all(codes, PIECES, 0, 0, tiled=True)
+    blocks = pl.pallas_call(
+        functools.partial(rows_kernel, sub, scale),
+        out_shape=jax.ShapeDtypeStruct((nz, sub + TAIL, nt), jnp.bfloat16),
+        in_specs=[full],
+        out_specs=full,
+        scratch_shapes=[VMEM((sub, nt), jnp.float32)],
+        compiler_params=MIDDLE,
+    )(codes)
+
+    own = lax.all_to_all(blocks, "z", 0, 0, tiled=True)
     other = lax.ppermute(own, "yl", SWAP)
     core_own = lax.ppermute(own, "c", SWAP)
 

time: 192 us -> 173 us (0.901)
  blocking collectives: 113 us -> 95.5 us
  Pallas kernels: 6.32 us -> 10.8 us
  other arithmetic: 4.52 us -> 2.22 us
    all_to_all x1, blocking collectives: 59.4 us -> 41.6 us  [shards(): codes = lax.all_to_all(codes, PIECES, 0, 0, tiled=True)]
    pallas_call x0 -> x2, Pallas kernels: none -> 4.51 us  [the longest x1 2.49 us: shards(): pl.pallas_call(functools.partial(encode_kernel, sub), out_shape=jax.Shape...]
    reduce_sum x2 -> x0, other arithmetic: 1.96 us -> none  [the longest x1 1.76 us: shards(): logits = jnp.sum(parts, axis=0) * scale]
where the time goes in v4:
time: 173 us; the launch traced here: 172 us
  blocking collectives  95.5 us (55%)
  waiting for transfers between devices  32.3 us (19%)
  starting transfers between devices  29.4 us (17%)
  Pallas kernels  10.8 us (6%)
  other arithmetic  2.22 us (1%)
    all_to_all x1, blocking collectives, shards(): codes = lax.all_to_all(codes, PIECES, 0, 0, tiled=True)  41.6 us
    all_to_all x2, blocking collectives, spread(): return lax.all_to_all(copies, axes, 0, 0, tiled=True)  30.6 us
    all_to_all x1, blocking collectives, shards(): got = lax.all_to_all(send, CHIPS, 0, 0, tiled=True)  23.2 us
    all_to_all x1, waiting for transfers between devices, shards(): own = lax.all_to_all(blocks, 'z', 0, 0, tiled=True)  15.7 us
    all_to_all x1, waiting for transfers between devices, shards(): sums = lax.all_to_all(sums, ROWS, 0, 0, tiled=True)  9.12 us
    all_to_all x1, starting transfers between devices, shards(): sums = lax.all_to_all(sums, ROWS, 0, 0, tiled=True)  8.77 us
    all_to_all x1, waiting for transfers between devices, shards(): stats = lax.all_to_all(stats, ROWS, 0, 0, tiled=True)  7.54 us
    all_to_all x1, starting transfers between devices, shards(): stats = lax.all_to_all(stats, ROWS, 0, 0, tiled=True)  6.81 us
  transfers between devices with their start and end apart: 7, of which 3 were waited for; matrix products, arithmetic and copies ran while one was open for 1% of the time, Pallas kernels for 1%

profile of v4, /device:TPU:6, one launch (start us, length us, event | category | flops | bytes accessed | tf_op | source)
XLA Modules:
  0.0 171.5 jit_solution(16201304584280298471)
XLA Ops:
  0.0 0.8 broadcast_in_dim.6
  0.8 25.9 %all_to_all.35 = bf16[16,16,1024]{2,1,0:T(8,128)(2,1)S(1)} all-to-all(bf16[16,16,1024]{2,1,0:T(8,128)(2,1)S(1)} %broadcast_in_dim.6), channel_id=1, replica_groups=mesh['yh'=4,'x'=4,'c'=2,'z'=8,'yl'=2] {'yh','x'}, dimensions={0} | all-to-all | bytes 1048576 | tf_op jit(solution)/shard_map/all_to_all | solution.py:108
  26.8 0.1 broadcast_in_dim.16
  26.9 0.0 copy-start
  26.9 4.7 %all_to_all.36 = bf16[2,256,1024]{2,1,0:T(8,128)(2,1)S(1)} all-to-all(bf16[2,256,1024]{2,1,0:T(8,128)(2,1)S(1)} %broadcast_in_dim.16), channel_id=1, replica_groups=mesh['yh'=4,'x'=4,'c'=2,'z'=8,'yl'=2] {'c'}, dimensions={0} | all-to-all | bytes 2097152 | tf_op jit(solution)/shard_map/all_to_all | solution.py:108
  31.6 2.5 %shard_map.37 = bf16[16,72,512]{2,1,0:T(8,128)(2,1)S(1)} custom-call(bf16[1024,1024]{1,0:T(8,128)(2,1)S(1)} %copy-done, bf16[512,1024]{1,0:T(8,128)(2,1)S(1)} %bitcast.5), custom_call_target="tpu_custom_call" | custom-call | tf_op jit(solution)/shard_map/pallas_call | solution.py:249
  34.1 41.6 %all_to_all.37.codes_ref = bf16[16,72,512]{2,1,0:T(8,128)(2,1)S(1)} all-to-all(bf16[16,72,512]{2,1,0:T(8,128)(2,1)S(1)} %shard_map.37), channel_id=1, replica_groups=mesh['yh'=4,'x'=4,'c'=2,'z'=8,'yl'=2] {'yl','z'}, dimensions={0} | all-to-all | bytes 2359296 | tf_op jit(solution)/shard_map/all_to_all | solution.py:257
  75.7 2.0 %shard_map.38 = bf16[8,72,512]{2,1,0:T(8,128)(2,1)} custom-call(bf16[16,72,512]{2,1,0:T(8,128)(2,1)S(1)} %all_to_all.37.codes_ref), custom_call_target="tpu_custom_call" | custom-call | tf_op jit(solution)/shard_map/pallas_call | solution.py:258
  77.7 3.7 %all-to-all-start.3 = ((bf16[8,72,512]{2,1,0:T(8,128)(2,1)}), bf16[8,72,512]{2,1,0:T(8,128)(2,1)S(1)}, u32[]{:S(2)}, u32[]{:S(2)}) async-start(bf16[8,72,512]{2,1,0:T(8,128)(2,1)} %shard_map.38), calls=%async_computation.3 | async-start | bytes 1179648 | tf_op jit(solution)/shard_map/all_to_all | solution.py:267
  81.4 1.9 %collective-permute-start.3 = (bf16[1024,1024]{1,0:T(8,128)(2,1)S(1)}, bf16[1024,1024]{1,0:T(8,128)(2,1)}, u32[]{:S(2)}, u32[]{:S(2)}) collective-permute-start(bf16[1024,1024]{1,0:T(8,128)(2,1)S(1)} %copy-done), channel_id=1, source_target_pairs={{0,16},{16,0},{1,17},{17,1},{2,18},{18,2},{3,19},{19,3},{4,20},{20... | collective-permute-start | bytes 6291464 | tf_op jit(solution)/shard_map/ppermute | solution.py:242
  83.4 15.7 %all-to-all-done.3.own_ref = bf16[8,72,512]{2,1,0:T(8,128)(2,1)S(1)} async-done(((bf16[8,72,512]{2,1,0:T(8,128)(2,1)}), bf16[8,72,512]{2,1,0:T(8,128)(2,1)S(1)}, u32[]{:S(2)}, u32[]{:S(2)}) %all-to-all-start.3) | async-done | bytes 589856 | tf_op jit(solution)/shard_map/all_to_all | solution.py:267
  99.0 4.2 %collective-permute-start = (bf16[8,72,512]{2,1,0:T(8,128)(2,1)S(1)}, bf16[8,72,512]{2,1,0:T(8,128)(2,1)S(1)}, u32[]{:S(2)}, u32[]{:S(2)}) collective-permute-start(bf16[8,72,512]{2,1,0:T(8,128)(2,1)S(1)} %all-to-all-done.3.own_ref), channel_id=1, source_target_pairs={{0,1},{1,0},{2,3},{3,2},{4,5},{5,4},{6,7},{7,6},{8,9},{9,8},{10,11... | collective-permute-start | bytes 1769480 | tf_op jit(solution)/shard_map/ppermute | solution.py:268
  103.2 0.8 shard_map.39
  104.0 6.8 %all-to-all-start.4 = ((f32[64,1,512]{2,1,0:T(1,128)}), f32[64,1,512]{2,1,0:T(1,128)S(1)}, u32[]{:S(2)}, u32[]{:S(2)}) async-start(f32[64,1,512]{2,1,0:T(1,128)} %shard_map.39), calls=%async_computation.4 | async-start | bytes 262144 | tf_op jit(solution)/shard_map/all_to_all | solution.py:280
  110.8 0.6 reduce_sum.27
  111.4 0.6 broadcast_divide_fusion
  112.1 0.1 div.22
  112.2 0.1 div.24.b_ref
  112.3 2.0 %collective-permute-start.1 = (bf16[8,72,512]{2,1,0:T(8,128)(2,1)S(1)}, bf16[8,72,512]{2,1,0:T(8,128)(2,1)}, u32[]{:S(2)}, u32[]{:S(2)}) collective-permute-start(bf16[8,72,512]{2,1,0:T(8,128)(2,1)S(1)} %all-to-all-done.3.own_ref), channel_id=1, source_target_pairs={{0,16},{16,0},{1,17},{17,1},{2,18},{18,2},{3,19},{19,3},{4,20},{20... | collective-permute-start | bytes 1769480 | tf_op jit(solution)/shard_map/ppermute | solution.py:269
  114.3 7.5 %all-to-all-done.4.stats_ref = f32[64,1,512]{2,1,0:T(1,128)S(1)} async-done(((f32[64,1,512]{2,1,0:T(1,128)}), f32[64,1,512]{2,1,0:T(1,128)S(1)}, u32[]{:S(2)}, u32[]{:S(2)}) %all-to-all-start.4) | async-done | bytes 131104 | tf_op jit(solution)/shard_map/all_to_all | solution.py:280
  121.9 1.0 shard_map.40
  122.9 0.0 collective-permute-done.other_ref
  122.9 2.0 %collective-permute-start.2 = (bf16[8,72,512]{2,1,0:T(8,128)(2,1)S(1)}, bf16[8,72,512]{2,1,0:T(8,128)(2,1)}, u32[]{:S(2)}, u32[]{:S(2)}) collective-permute-start(bf16[8,72,512]{2,1,0:T(8,128)(2,1)S(1)} %collective-permute-done.other_ref), channel_id=1, source_target_pairs={{0,16},{16,0},{1,17},{17,1},{2,18},{18,2},{3,19},{19,3},{4,20},{20... | collective-permute-start | bytes 1769480 | tf_op jit(solution)/shard_map/ppermute | solution.py:290
  124.9 8.8 %all-to-all-start.5 = ((f32[64,1,512]{2,1,0:T(1,128)}), f32[64,1,512]{2,1,0:T(1,128)S(1)}, u32[]{:S(2)}, u32[]{:S(2)}) async-start(f32[64,1,512]{2,1,0:T(1,128)} %get-tuple-element.9), calls=%async_computation.5 | async-start | bytes 262144 | tf_op jit(solution)/shard_map/all_to_all | solution.py:288
  133.7 0.1 pad_add_fusion.place_ref
  133.8 0.0 collective-permute-done.3.core_train_ref
  133.8 9.1 %all-to-all-done.5.sums_ref = f32[64,1,512]{2,1,0:T(1,128)S(1)} async-done(((f32[64,1,512]{2,1,0:T(1,128)}), f32[64,1,512]{2,1,0:T(1,128)S(1)}, u32[]{:S(2)}, u32[]{:S(2)}) %all-to-all-start.5) | async-done | bytes 131104 | tf_op jit(solution)/shard_map/all_to_all | solution.py:288
  142.9 4.5 %shard_map.41 = bf16[16,16,1152]{2,1,0:T(8,128)(2,1)S(1)} custom-call(s32[2]{0:T(128)S(1)} %pad_add_fusion.place_ref, f32[64,1,512]{2,1,0:T(1,128)S(1)} %all-to-all-done.5.sums_ref, f32[1,512]{1,0:T(1,128)S(1)} %get-tuple-element.10.far_ref, f32[1,512]{1,0:T(1,128)S(1)} %get-tuple-element.11.col_ref, f32[1,512]{1,0:T(1,128)S(1)} %div.24.b_ref, ...), custom_call_target="tpu_custom_call" | custom-call | tf_op jit(solution)/shard_map/pallas_call | solution.py:293
  147.4 23.2 %all_to_all.38 = bf16[16,16,1152]{2,1,0:T(8,128)(2,1)S(1)} all-to-all(bf16[16,16,1152]{2,1,0:T(8,128)(2,1)S(1)} %shard_map.41), channel_id=1, replica_groups=mesh['yh'=4,'x'=4,'c'=2,'z'=8,'yl'=2] {'yh','x'}, dimensions={0} | all-to-all | bytes 1179648 | tf_op jit(solution)/shard_map/all_to_all | solution.py:306
  170.6 0.1 convert_reduce_fusion
  170.7 0.1 slice_reduce_fusion
  170.8 0.7 fusion
  (6 shorter events, 0.0 us)
Async XLA Ops:
  26.9 4.7 %copy-start = (bf16[1024,1024]{1,0:T(8,128)(2,1)S(1)}, bf16[1024,1024]{1,0:T(8,128)(2,1)}, u32[]{:S(2)}) copy-start(bf16[1024,1024]{1,0:T(8,128)(2,1)} %train_ref.3) | copy-start | bytes 6291460
  77.7 33.1 %copy-start.1 = (f32[512]{0:T(512)S(1)}, f32[512]{0:T(512)}, u32[]{:S(2)}) copy-start(f32[512]{0:T(512)} %param.5) | copy-start | bytes 6148
  77.7 21.3 %all-to-all-start.3 = ((bf16[8,72,512]{2,1,0:T(8,128)(2,1)}), bf16[8,72,512]{2,1,0:T(8,128)(2,1)S(1)}, u32[]{:S(2)}, u32[]{:S(2)}) async-start(bf16[8,72,512]{2,1,0:T(8,128)(2,1)} %shard_map.38), calls=%async_computation.3 | async-start | bytes 1179648 | tf_op jit(solution)/shard_map/all_to_all | solution.py:267
  81.4 52.3 %collective-permute-start.3 = (bf16[1024,1024]{1,0:T(8,128)(2,1)S(1)}, bf16[1024,1024]{1,0:T(8,128)(2,1)}, u32[]{:S(2)}, u32[]{:S(2)}) collective-permute-start(bf16[1024,1024]{1,0:T(8,128)(2,1)S(1)} %copy-done), channel_id=1, source_target_pairs={{0,16},{16,0},{1,17},{17,1},{2,18},{18,2},{3,19},{19,3},{4,20},{20... | collective-permute-start | bytes 6291464 | tf_op jit(solution)/shard_map/ppermute | solution.py:242
  99.0 23.9 %collective-permute-start = (bf16[8,72,512]{2,1,0:T(8,128)(2,1)S(1)}, bf16[8,72,512]{2,1,0:T(8,128)(2,1)S(1)}, u32[]{:S(2)}, u32[]{:S(2)}) collective-permute-start(bf16[8,72,512]{2,1,0:T(8,128)(2,1)S(1)} %all-to-all-done.3.own_ref), channel_id=1, source_target_pairs={{0,1},{1,0},{2,3},{3,2},{4,5},{5,4},{6,7},{7,6},{8,9},{9,8},{10,11... | collective-permute-start | bytes 1769480 | tf_op jit(solution)/shard_map/ppermute | solution.py:268
  104.0 17.8 %all-to-all-start.4 = ((f32[64,1,512]{2,1,0:T(1,128)}), f32[64,1,512]{2,1,0:T(1,128)S(1)}, u32[]{:S(2)}, u32[]{:S(2)}) async-start(f32[64,1,512]{2,1,0:T(1,128)} %shard_map.39), calls=%async_computation.4 | async-start | bytes 262144 | tf_op jit(solution)/shard_map/all_to_all | solution.py:280
  112.3 30.6 %collective-permute-start.1 = (bf16[8,72,512]{2,1,0:T(8,128)(2,1)S(1)}, bf16[8,72,512]{2,1,0:T(8,128)(2,1)}, u32[]{:S(2)}, u32[]{:S(2)}) collective-permute-start(bf16[8,72,512]{2,1,0:T(8,128)(2,1)S(1)} %all-to-all-done.3.own_ref), channel_id=1, source_target_pairs={{0,16},{16,0},{1,17},{17,1},{2,18},{18,2},{3,19},{19,3},{4,20},{20... | collective-permute-start | bytes 1769480 | tf_op jit(solution)/shard_map/ppermute | solution.py:269
  122.9 20.0 %collective-permute-start.2 = (bf16[8,72,512]{2,1,0:T(8,128)(2,1)S(1)}, bf16[8,72,512]{2,1,0:T(8,128)(2,1)}, u32[]{:S(2)}, u32[]{:S(2)}) collective-permute-start(bf16[8,72,512]{2,1,0:T(8,128)(2,1)S(1)} %collective-permute-done.other_ref), channel_id=1, source_target_pairs={{0,16},{16,0},{1,17},{17,1},{2,18},{18,2},{3,19},{19,3},{4,20},{20... | collective-permute-start | bytes 1769480 | tf_op jit(solution)/shard_map/ppermute | solution.py:290
  124.9 18.0 %all-to-all-start.5 = ((f32[64,1,512]{2,1,0:T(1,128)}), f32[64,1,512]{2,1,0:T(1,128)S(1)}, u32[]{:S(2)}, u32[]{:S(2)}) async-start(f32[64,1,512]{2,1,0:T(1,128)} %get-tuple-element.9), calls=%async_computation.5 | async-start | bytes 262144 | tf_op jit(solution)/shard_map/all_to_all | solution.py:288

commit v5 on v4

v5 whole, which is shorter than its diff:
```python
import functools
import math

import jax
import jax.numpy as jnp
from jax import lax
from jax.experimental import pallas as pl
from jax.experimental.pallas import tpu as pltpu
from jax.sharding import Mesh, PartitionSpec as P


F = 16384
CHIPS = ("yh", "x")
EX = ("yh", "x", "c")
FEAT = ("z", "yl")
PIECES = ("yl", "z")
ROWS = ("yh", "x", "c", "yl")
CHIP_ROWS = ("yh", "x", "yl")
LANES = 128
CODE_TAIL = 8
KERNEL_TAIL = 16
MIXTURE_TAIL = 8
SWAP = [(0, 1), (1, 0)]
VMEM = pltpu.VMEM
MIDDLE = pltpu.CompilerParams(vmem_limit_bytes=12 * 2**20)
SMALL = pltpu.CompilerParams(vmem_limit_bytes=4 * 2**20)
LARGE = pltpu.CompilerParams(vmem_limit_bytes=24 * 2**20)


SPAN = 249.0
BASE = 124.0


def round_up(v):
    return (v * (1.0 + 2.0**-7)).astype(jnp.bfloat16).astype(jnp.float32)


def split3(v):
    hi = v.astype(jnp.bfloat16).astype(jnp.float32)
    mid = (v - hi).astype(jnp.bfloat16).astype(jnp.float32)
    return hi, mid, v - hi - mid


def stack_rows(rows, height):
    index = lax.broadcasted_iota(jnp.int32, (height, LANES), 0)
    out = jnp.zeros((height, LANES), jnp.float32)
    for k, row in enumerate(rows):
        out = jnp.where(index == k, row, out)
    return out


def lane_blocks(v):
    return [v[:, k : k + LANES] for k in range(0, v.shape[1], LANES)]


def diagonal(sub):
    return lax.broadcasted_iota(jnp.int32, (sub, LANES), 0) == (
        lax.broadcasted_iota(jnp.int32, (sub, LANES), 1)
    )


def encode_kernel(sub, train_ref, targets_ref, out_ref, partial_ref):
    rows = train_ref.shape[0]
    step = partial_ref.shape[0]
    on_diagonal = diagonal(sub)
    for start in range(0, rows, step):
        partial_ref[...] = lax.dot_general(
            train_ref[start : start + step, :],
            targets_ref[...],
            (((1,), (1,)), ((), ())),
            preferred_element_type=jnp.float32,
        )
        for j in range(step // sub):
            k = start // sub + j
            p = partial_ref[j * sub : (j + 1) * sub, :]
            high = jnp.max(p, axis=1, keepdims=True)
            low = jnp.min(p, axis=1, keepdims=True)
            p = p - 0.5 * (high + low)
            wide = jnp.max(jnp.abs(p), axis=1, keepdims=True)
            row = round_up(jnp.maximum(wide, 1e-30))
            p = p * (1.0 / row)
            col = round_up(jnp.maximum(jnp.max(jnp.abs(p), axis=0, keepdims=True), 1e-30))
            u = p * (1.0 / col)
            code = jnp.exp2(jnp.minimum(jnp.abs(u), 1.0) * SPAN - BASE)
            code = jnp.where(u < 0, -code, code).astype(jnp.bfloat16)
            parts = lane_blocks(code)
            for n, part in enumerate(parts):
                out_ref[k, n * sub : (n + 1) * sub, :] = part
            row = jnp.sum(jnp.where(on_diagonal, row, 0.0), axis=0, keepdims=True)
            tail = stack_rows(lane_blocks(col) + [row], CODE_TAIL)
            out_ref[k, len(parts) * sub :, :] = tail.astype(jnp.bfloat16)


def rows_kernel(sub, scale, codes_ref, out_ref, logits_ref):
    nf = codes_ref.shape[0]
    nz = out_ref.shape[0]
    nl = logits_ref.shape[1] // LANES
    on_diagonal = diagonal(sub)
    tails, rows = [], []
    for k in range(nf):
        tail = codes_ref[k, nl * sub :, :].astype(jnp.float32)
        tails.append(tail * (scale / SPAN))
        row = jnp.where(on_diagonal, tail[nl : nl + 1, :], 0.0)
        rows.append(jnp.sum(row, axis=1, keepdims=True))
    for n in range(nl):
        total = jnp.zeros((sub, LANES), jnp.float32)
        for k in range(nf):
            code = codes_ref[k, n * sub : (n + 1) * sub, :].astype(jnp.float32)
            size = jnp.log(jnp.abs(code)) * (1.0 / math.log(2.0)) + BASE
            size = jnp.where(code < 0, -size, size)
            total += size * tails[k][n : n + 1, :] * rows[k]
        logits_ref[:, n * LANES : (n + 1) * LANES] = total

    logits = logits_ref[...]
    top = jnp.max(logits, axis=1, keepdims=True)
    v = logits - top
    v = v - jnp.log(jnp.sum(jnp.exp(v), axis=1, keepdims=True))
    shift = jnp.max(v, axis=0, keepdims=True)
    kern = lane_blocks(jnp.exp(v - shift).astype(jnp.bfloat16))
    terms = [row for term in split3(shift) for row in lane_blocks(term)]
    tail = stack_rows(terms, KERNEL_TAIL).astype(jnp.bfloat16)
    for z in range(nz):
        for n, part in enumerate(kern):
            out_ref[z, n * sub : (n + 1) * sub, :] = part
        out_ref[z, nl * sub :, :] = tail


def spread(block, axes, n):
    copies = jnp.broadcast_to(block[None], (n,) + block.shape)
    return lax.all_to_all(copies, axes, 0, 0, tiled=True)


def block_shift(ref, z, sub, nl):
    tail = ref[z, nl * sub :, :].astype(jnp.float32)
    return tail[:nl] + tail[nl : 2 * nl] + tail[2 * nl : 3 * nl]


def block_part(ref, z, sub, n):
    return ref[z, n * sub : (n + 1) * sub, :].astype(jnp.float32)


def statistics_kernel(sub, own_ref, out_ref):
    nz = own_ref.shape[0]
    nl = out_ref.shape[1]
    shifts = [block_shift(own_ref, z, sub, nl) for z in range(nz)]
    top = functools.reduce(jnp.maximum, shifts)
    total = [jnp.zeros((1, LANES), jnp.float32)] * nl
    for z in range(nz):
        factor = jnp.exp(shifts[z] - top)
        for n in range(nl):
            part = jnp.sum(block_part(own_ref, z, sub, n), axis=0, keepdims=True)
            total[n] = total[n] + factor[n : n + 1] * part
    log_sum = top + jnp.log(stack_rows(total, nl))
    out_ref[...] = jnp.broadcast_to(log_sum[None], out_ref.shape)


def columns_kernel(sub, a, stats_ref, own_ref, core_ref, b_ref, far_ref, col_ref, out_ref):
    nz = own_ref.shape[0]
    nl = out_ref.shape[1]
    stats = stats_ref[...]
    far = jnp.max(stats, axis=0)
    col = b_ref[...] / jnp.sum(jnp.exp(stats - far[None]), axis=0)
    cols = [jnp.zeros((1, LANES), jnp.float32)] * nl
    for z in range(nz):
        for ref in (own_ref, core_ref):
            factor = jnp.exp(block_shift(ref, z, sub, nl) - far) * col
            plan = [block_part(ref, z, sub, n) * factor[n : n + 1] for n in range(nl)]
            row = a / jnp.sum(functools.reduce(jnp.add, plan), axis=1, keepdims=True)
            for n in range(nl):
                cols[n] = cols[n] + jnp.sum(plan[n] * row, axis=0, keepdims=True)
    far_ref[...] = far
    col_ref[...] = col
    out_ref[...] = jnp.broadcast_to(stack_rows(cols, nl)[None], out_ref.shape)


def copy_kernel(in_ref, out_ref):
    out_ref[...] = in_ref[...]


def mixture_kernel(
    sub,
    a,
    place_ref,
    sums_ref,
    far_ref,
    col_ref,
    b_ref,
    own_ref,
    other_ref,
    core_own_ref,
    core_other_ref,
    train_ref,
    core_train_ref,
    out_ref,
    plan_ref,
    cols_ref,
    train_vmem,
    sems,
):
    nz = own_ref.shape[0]
    nl = sums_ref.shape[1]
    nh = nl // 2
    rows = nz * sub
    c, yl = place_ref[0], place_ref[1]
    copies = [
        pltpu.make_async_copy(src, train_vmem.at[k], sems.at[k])
        for k, src in enumerate((train_ref, core_train_ref))
    ]
    for copy in copies:
        copy.start()
    far = far_ref[...]
    col = col_ref[...] * (b_ref[...] / jnp.sum(sums_ref[...], axis=0))

    refs = ((own_ref, 0, 0), (other_ref, 0, 1), (core_own_ref, 1, 0), (core_other_ref, 1, 1))

    def step(z, cols):
        cols = list(cols)
        for ref, k, flip in refs:
            factor = jnp.exp(block_shift(ref, z, sub, nl) - far) * col
            plan = [block_part(ref, z, sub, n) * factor[n : n + 1] for n in range(nl)]
            row = a / jnp.sum(functools.reduce(jnp.add, plan), axis=1, keepdims=True)
            side = yl + flip * (1 - 2 * yl)
            start = pl.multiple_of(side * rows + z * sub, sub)
            for n in range(nl):
                part = plan[n] * row
                cols[n] = cols[n] + jnp.sum(part, axis=0, keepdims=True)
                lane = (n % nh) * LANES
                plan_ref[n // nh, k, pl.ds(start, sub), lane : lane + LANES] = part.astype(
                    jnp.bfloat16
                )
        return tuple(cols)

    cols = lax.fori_loop(0, nz, step, (jnp.zeros((1, LANES), jnp.float32),) * nl)
    for n in range(nl):
        cols_ref[n // nh, n % nh] = cols[n]

    half = nh * LANES
    mixed = jnp.zeros((half, train_ref.shape[1]), jnp.float32)
    for k in range(2):
        copies[k].wait()
        mixed += lax.dot_general(
            plan_ref[c, k],
            train_vmem[k],
            (((0,), (0,)), ((), ())),
            preferred_element_type=jnp.float32,
        )
    nchips = out_ref.shape[0]
    mine = half // nchips
    parts = lane_blocks(mixed.astype(jnp.bfloat16))
    for n, part in enumerate(parts):
        out_ref[:, n * mine : (n + 1) * mine, :] = part.reshape(nchips, mine, LANES)
    per = LANES // mine
    for n in range(nh):
        tail = stack_rows(split3(cols_ref[c, n]), MIXTURE_TAIL).astype(jnp.bfloat16)
        out_ref[n * per : (n + 1) * per, len(parts) * mine :, :] = jnp.broadcast_to(
            tail[None], (per, MIXTURE_TAIL, LANES)
        )


def output_kernel(place_ref, got_ref, out_ref):
    mine, feats = out_ref.shape
    nl = feats // LANES
    total = jnp.sum(got_ref[...].astype(jnp.float32), axis=0)
    mass = total[nl * mine : nl * mine + 1] + (
        total[nl * mine + 1 : nl * mine + 2] + total[nl * mine + 2 : nl * mine + 3]
    )
    lane = lax.broadcasted_iota(jnp.int32, (mine, LANES), 1)
    target = lax.broadcasted_iota(jnp.int32, (mine, LANES), 0) + place_ref[2] * mine
    mass = jnp.sum(jnp.where(lane == target, mass, 0.0), axis=1, keepdims=True)
    for n in range(nl):
        part = total[n * mine : (n + 1) * mine] / mass
        out_ref[:, n * LANES : (n + 1) * LANES] = part.astype(jnp.bfloat16)


def shards(train, target, mass):
    rows, feats = train.shape
    nc = lax.axis_size("c")
    nchips = lax.axis_size(CHIPS)
    nex = nc * nchips
    nz = lax.axis_size("z")
    nf = lax.axis_size(FEAT)
    mine = target.shape[0]
    nt = mine * nex
    nl = nt // LANES
    half = nt // nc
    sub = rows // nf
    scale = 3.0 / math.sqrt(F)
    a = 1.0 / (rows * nex)
    full = pl.BlockSpec(memory_space=VMEM)
    anywhere = pl.BlockSpec(memory_space=pl.ANY)
    scalars = pl.BlockSpec(memory_space=pltpu.SMEM)

    core_train = lax.ppermute(train, "c", SWAP)

    same_core = spread(target, CHIPS, nchips).reshape(nchips * mine, feats)
    targets = spread(same_core, "c", nc).reshape(nt, feats)
    mass = mass.reshape(nchips, nc, mine).transpose(1, 0, 2).reshape(nl, LANES)
    b = mass / jnp.sum(mass)

    codes = pl.pallas_call(
        functools.partial(encode_kernel, sub),
        out_shape=jax.ShapeDtypeStruct((nf, nl * sub + CODE_TAIL, LANES), jnp.bfloat16),
        in_specs=[full] * 2,
        out_specs=full,
        scratch_shapes=[VMEM((4 * sub, nt), jnp.float32)],
        compiler_params=MIDDLE,
    )(train, targets)
    codes = lax.all_to_all(codes, PIECES, 0, 0, tiled=True)
    blocks = pl.pallas_call(
        functools.partial(rows_kernel, sub, scale),
        out_shape=jax.ShapeDtypeStruct((nz, nl * sub + KERNEL_TAIL, LANES), jnp.bfloat16),
        in_specs=[full],
        out_specs=full,
        scratch_shapes=[VMEM((sub, nt), jnp.float32)],
        compiler_params=MIDDLE,
    )(codes)

    own = lax.all_to_all(blocks, "z", 0, 0, tiled=True)
    other = lax.ppermute(own, "yl", SWAP)
    core_own = lax.ppermute(own, "c", SWAP)

    def copies(axes):
        return jax.ShapeDtypeStruct((lax.axis_size(axes), nl, LANES), jnp.float32)

    vector = jax.ShapeDtypeStruct((nl, LANES), jnp.float32)
    stats = pl.pallas_call(
        functools.partial(statistics_kernel, sub),
        out_shape=copies(ROWS),
        in_specs=[full],
        out_specs=full,
        compiler_params=SMALL,
    )(own)
    stats = lax.all_to_all(stats, ROWS, 0, 0, tiled=True)
    far, col, sums = pl.pallas_call(
        functools.partial(columns_kernel, sub, a),
        out_shape=(vector, vector, copies(CHIP_ROWS)),
        in_specs=[full] * 4,
        out_specs=(full,) * 3,
        compiler_params=SMALL,
    )(stats, own, core_own, b)
    sums = lax.all_to_all(sums, CHIP_ROWS, 0, 0, tiled=True)
    other_copy = pl.pallas_call(
        copy_kernel,
        out_shape=jax.ShapeDtypeStruct(other.shape, other.dtype),
        in_specs=[full],
        out_specs=full,
        compiler_params=SMALL,
    )(other)
    core_other = lax.ppermute(other_copy, "c", SWAP)

    slot = jnp.bitwise_and(lax.axis_index(CHIPS), LANES // mine - 1)
    place = jnp.stack([lax.axis_index("c"), lax.axis_index("yl"), slot]).astype(jnp.int32)
    block = feats // LANES * mine + MIXTURE_TAIL
    send = pl.pallas_call(
        functools.partial(mixture_kernel, sub, a),
        out_shape=jax.ShapeDtypeStruct((nchips, block, LANES), jnp.bfloat16),
        in_specs=[scalars] + [full] * 8 + [anywhere] * 2,
        out_specs=full,
        scratch_shapes=[
            VMEM((nc, 2, rows, half), jnp.bfloat16),
            VMEM((nc, nl // nc, 1, LANES), jnp.float32),
            VMEM((2, rows, feats), jnp.bfloat16),
            pltpu.SemaphoreType.DMA((2,)),
        ],
        compiler_params=LARGE,
    )(place, sums, far, col, b, own, other, core_own, core_other, train, core_train)
    got = lax.all_to_all(send, CHIPS, 0, 0, tiled=True)
    return pl.pallas_call(
        output_kernel,
        out_shape=jax.ShapeDtypeStruct((mine, feats), jnp.bfloat16),
        in_specs=[scalars, full],
        out_specs=full,
        compiler_params=SMALL,
    )(place, got)


def solution(mesh):
    fine = Mesh(mesh.devices.reshape(4, 4, 2, 8, 2), ("yh", "x", "c", "z", "yl"))

    return jax.shard_map(
        shards,
        mesh=fine,
        in_specs=(P(EX, FEAT), P(EX, FEAT), P()),
        out_specs=P(EX, FEAT),
        check_vma=False,
    )
```

time: 173 us -> 180 us (1.040)
  blocking collectives: 95.5 us -> 75.4 us
  waiting for transfers between devices: 32.3 us -> 50.1 us
  starting transfers between devices: 29.4 us -> 33.6 us
  Pallas kernels: 10.8 us -> 14.3 us
  local copies, waits for them, and re-layouts: 1.12 us -> 2.99 us
    all_to_all x1, blocking collectives: 41.6 us -> 23.2 us  [shards(): own = lax.all_to_all(blocks, 'z', 0, 0, tiled=True)]
    ppermute x1, waiting for transfers between devices: 0.01 us -> 9.02 us  [shards(): other = lax.ppermute(own, 'yl', SWAP)]
    all_to_all x2, waiting for transfers between devices: 24.8 us -> 33.3 us  [the longest x1 25.2 us: shards(): codes = lax.all_to_all(codes, PIECES, 0, 0, tiled=True)]
    all_to_all x2, starting transfers between devices: 12.4 us -> 16 us  [the longest x1 10.5 us: shards(): codes = lax.all_to_all(codes, PIECES, 0, 0, tiled=True)]
    pallas_call x0 -> x2, Pallas kernels: none -> 2.11 us  [the longest x1 1.27 us: shards(): pl.pallas_call(output_kernel, out_shape=jax.ShapeDtypeStruct((mine, feats...]
    unnamed x4 -> x8, local copies, waits for them, and re-layouts: 0.01 us -> 1.88 us
  transfers between devices with their start and end apart: 7 -> 7, of which waited for: 3 -> 4; matrix products, arithmetic and copies ran while one was open for 1% -> 1% of each run, Pallas kernels for 1% -> 3%
where the time goes in v5:
time: 180 us; the launch traced here: 178 us
  blocking collectives  75.4 us (42%)
  waiting for transfers between devices  50.1 us (28%)
  starting transfers between devices  33.6 us (19%)
  Pallas kernels  14.3 us (8%)
  local copies, waits for them, and re-layouts  2.99 us (2%)
    all_to_all x2, blocking collectives, spread(): return lax.all_to_all(copies, axes, 0, 0, tiled=True)  30.6 us
    all_to_all x1, waiting for transfers between devices, shards(): codes = lax.all_to_all(codes, PIECES, 0, 0, tiled=True)  25.2 us
    all_to_all x1, blocking collectives, shards(): own = lax.all_to_all(blocks, 'z', 0, 0, tiled=True)  23.2 us
    all_to_all x1, blocking collectives, shards(): got = lax.all_to_all(send, CHIPS, 0, 0, tiled=True)  21.6 us
    all_to_all x1, starting transfers between devices, shards(): codes = lax.all_to_all(codes, PIECES, 0, 0, tiled=True)  10.5 us
    ppermute x1, waiting for transfers between devices, shards(): other = lax.ppermute(own, 'yl', SWAP)  9.02 us
    all_to_all x1, waiting for transfers between devices, shards(): sums = lax.all_to_all(sums, CHIP_ROWS, 0, 0, tiled=True)  8.15 us
    all_to_all x1, starting transfers between devices, shards(): stats = lax.all_to_all(stats, ROWS, 0, 0, tiled=True)  8.05 us
  transfers between devices with their start and end apart: 7, of which 4 were waited for; matrix products, arithmetic and copies ran while one was open for 1% of the time, Pallas kernels for 3%

profile of v5, /device:TPU:6, one launch (start us, length us, event | category | flops | bytes accessed | tf_op | source)
XLA Modules:
  0.0 177.9 jit_solution(14475016326987031325)
XLA Ops:
  0.0 0.8 broadcast_in_dim.6
  0.8 25.9 %all_to_all.35 = bf16[16,16,1024]{2,1,0:T(8,128)(2,1)S(1)} all-to-all(bf16[16,16,1024]{2,1,0:T(8,128)(2,1)S(1)} %broadcast_in_dim.6), channel_id=1, replica_groups=mesh['yh'=4,'x'=4,'c'=2,'z'=8,'yl'=2] {'yh','x'}, dimensions={0} | all-to-all | bytes 1048576 | tf_op jit(solution)/shard_map/all_to_all | solution.py:130
  26.8 0.1 broadcast_in_dim.15
  26.9 4.7 %all_to_all.36 = bf16[2,256,1024]{2,1,0:T(8,128)(2,1)S(1)} all-to-all(bf16[2,256,1024]{2,1,0:T(8,128)(2,1)S(1)} %broadcast_in_dim.15), channel_id=1, replica_groups=mesh['yh'=4,'x'=4,'c'=2,'z'=8,'yl'=2] {'c'}, dimensions={0} | all-to-all | bytes 2097152 | tf_op jit(solution)/shard_map/all_to_all | solution.py:130
  31.6 3.6 %shard_map.37 = bf16[16,264,128]{2,1,0:T(8,128)(2,1)} custom-call(bf16[1024,1024]{1,0:T(8,128)(2,1)S(1)} %copy-done, bf16[512,1024]{1,0:T(8,128)(2,1)S(1)} %bitcast.6), custom_call_target="tpu_custom_call" | custom-call | tf_op jit(solution)/shard_map/pallas_call | solution.py:300
  35.2 10.5 %all-to-all-start.2 = ((bf16[16,264,128]{2,1,0:T(8,128)(2,1)}), bf16[16,264,128]{2,1,0:T(8,128)(2,1)}, u32[]{:S(2)}, u32[]{:S(2)}) async-start(bf16[16,264,128]{2,1,0:T(8,128)(2,1)} %shard_map.37), calls=%async_computation.2 | async-start | bytes 2162688 | tf_op jit(solution)/shard_map/all_to_all | solution.py:308
  45.6 0.0 copy-start.3
  45.6 1.9 %collective-permute-start.3 = (bf16[1024,1024]{1,0:T(8,128)(2,1)S(1)}, bf16[1024,1024]{1,0:T(8,128)(2,1)}, u32[]{:S(2)}, u32[]{:S(2)}) collective-permute-start(bf16[1024,1024]{1,0:T(8,128)(2,1)S(1)} %copy-done), channel_id=1, source_target_pairs={{0,16},{16,0},{1,17},{17,1},{2,18},{18,2},{3,19},{19,3},{4,20},{20... | collective-permute-start | bytes 6291464 | tf_op jit(solution)/shard_map/ppermute | solution.py:293
  47.6 25.2 %all-to-all-done.2.codes_ref = bf16[16,264,128]{2,1,0:T(8,128)(2,1)} async-done(((bf16[16,264,128]{2,1,0:T(8,128)(2,1)}), bf16[16,264,128]{2,1,0:T(8,128)(2,1)}, u32[]{:S(2)}, u32[]{:S(2)}) %all-to-all-start.2) | async-done | bytes 1081376 | tf_op jit(solution)/shard_map/all_to_all | solution.py:308
  72.8 2.4 %shard_map.38 = bf16[8,272,128]{2,1,0:T(8,128)(2,1)S(1)} custom-call(bf16[16,264,128]{2,1,0:T(8,128)(2,1)} %all-to-all-done.2.codes_ref), custom_call_target="tpu_custom_call" | custom-call | tf_op jit(solution)/shard_map/pallas_call | solution.py:309
  75.1 23.2 %all_to_all.37.own_ref = bf16[8,272,128]{2,1,0:T(8,128)(2,1)S(1)} all-to-all(bf16[8,272,128]{2,1,0:T(8,128)(2,1)S(1)} %shard_map.38), channel_id=1, replica_groups=mesh['yh'=4,'x'=4,'c'=2,'z'=8,'yl'=2] {'z'}, dimensions={0} | all-to-all | bytes 1114112 | tf_op jit(solution)/shard_map/all_to_all | solution.py:318
  98.3 3.8 %collective-permute-start.1 = (bf16[8,272,128]{2,1,0:T(8,128)(2,1)S(1)}, bf16[8,272,128]{2,1,0:T(8,128)(2,1)S(1)}, u32[]{:S(2)}, u32[]{:S(2)}) collective-permute-start(bf16[8,272,128]{2,1,0:T(8,128)(2,1)S(1)} %all_to_all.37.own_ref), channel_id=1, source_target_pairs={{0,1},{1,0},{2,3},{3,2},{4,5},{5,4},{6,7},{7,6},{8,9},{9,8},{10,11... | collective-permute-start | bytes 1671176 | tf_op jit(solution)/shard_map/ppermute | solution.py:319
  102.1 1.9 %collective-permute-start = (bf16[8,272,128]{2,1,0:T(8,128)(2,1)S(1)}, bf16[8,272,128]{2,1,0:T(8,128)(2,1)S(1)}, u32[]{:S(2)}, u32[]{:S(2)}) collective-permute-start(bf16[8,272,128]{2,1,0:T(8,128)(2,1)S(1)} %all_to_all.37.own_ref), channel_id=1, source_target_pairs={{0,16},{16,0},{1,17},{17,1},{2,18},{18,2},{3,19},{19,3},{4,20},{20... | collective-permute-start | bytes 1671176 | tf_op jit(solution)/shard_map/ppermute | solution.py:320
  104.0 9.0 %collective-permute-done.1.in_ref.other_ref = bf16[8,272,128]{2,1,0:T(8,128)(2,1)S(1)} collective-permute-done((bf16[8,272,128]{2,1,0:T(8,128)(2,1)S(1)}, bf16[8,272,128]{2,1,0:T(8,128)(2,1)S(1)}, u32[]{:S(2)}, u32[]{:S(2)}) %collective-permute-start.1) | collective-permute-done | bytes 557088 | tf_op jit(solution)/shard_map/ppermute | solution.py:319
  113.1 0.8 shard_map.41
  113.9 0.8 copy-done.1
  114.7 1.9 %collective-permute-start.2 = (bf16[8,272,128]{2,1,0:T(8,128)(2,1)}, bf16[8,272,128]{2,1,0:T(8,128)(2,1)}, u32[]{:S(2)}, u32[]{:S(2)}) collective-permute-start(bf16[8,272,128]{2,1,0:T(8,128)(2,1)} %shard_map.41), channel_id=1, source_target_pairs={{0,16},{16,0},{1,17},{17,1},{2,18},{18,2},{3,19},{19,3},{4,20},{20... | collective-permute-start | bytes 1671176 | tf_op jit(solution)/shard_map/ppermute | solution.py:349
  116.6 0.8 shard_map.39
  117.4 8.1 %all-to-all-start.4 = ((f32[64,4,128]{2,1,0:T(4,128)}), f32[64,4,128]{2,1,0:T(4,128)S(1)}, u32[]{:S(2)}, u32[]{:S(2)}) async-start(f32[64,4,128]{2,1,0:T(4,128)} %shard_map.39), calls=%async_computation.4 | async-start | bytes 262144 | tf_op jit(solution)/shard_map/all_to_all | solution.py:333
  125.5 0.6 reduce_sum.9
  126.1 0.6 broadcast_divide_fusion
  126.8 0.1 div.14
  126.9 0.1 div.16.b_ref
  127.0 7.8 %all-to-all-done.4.stats_ref = f32[64,4,128]{2,1,0:T(4,128)S(1)} async-done(((f32[64,4,128]{2,1,0:T(4,128)}), f32[64,4,128]{2,1,0:T(4,128)S(1)}, u32[]{:S(2)}, u32[]{:S(2)}) %all-to-all-start.4) | async-done | bytes 131104 | tf_op jit(solution)/shard_map/all_to_all | solution.py:333
  134.7 1.2 shard_map.40
  135.9 5.5 %all-to-all-start.5 = ((f32[32,4,128]{2,1,0:T(4,128)}), f32[32,4,128]{2,1,0:T(4,128)S(1)}, u32[]{:S(2)}, u32[]{:S(2)}) async-start(f32[32,4,128]{2,1,0:T(4,128)} %get-tuple-element.8), calls=%async_computation.5 | async-start | bytes 131072 | tf_op jit(solution)/shard_map/all_to_all | solution.py:341
  141.4 0.1 pad_add_fusion.place_ref
  141.5 8.2 %all-to-all-done.5.sums_ref = f32[32,4,128]{2,1,0:T(4,128)S(1)} async-done(((f32[32,4,128]{2,1,0:T(4,128)}), f32[32,4,128]{2,1,0:T(4,128)S(1)}, u32[]{:S(2)}, u32[]{:S(2)}) %all-to-all-start.5) | async-done | bytes 65568 | tf_op jit(solution)/shard_map/all_to_all | solution.py:341
  149.7 1.1 copy-done.2
  150.7 4.3 %shard_map.42 = bf16[16,136,128]{2,1,0:T(8,128)(2,1)S(1)} custom-call(s32[3]{0:T(128)S(1)} %pad_add_fusion.place_ref, f32[32,4,128]{2,1,0:T(4,128)S(1)} %all-to-all-done.5.sums_ref, f32[4,128]{1,0:T(4,128)S(1)} %get-tuple-element.9.far_ref, f32[4,128]{1,0:T(4,128)S(1)} %get-tuple-element.10.col_ref, f32[4,128]{1,0:T(4,128)S(1)} %div.16.b_ref, ...), custom_call_target="tpu_custom_call" | custom-call | tf_op jit(solution)/shard_map/pallas_call | solution.py:354
  155.0 21.6 %all_to_all.38.got_ref = bf16[16,136,128]{2,1,0:T(8,128)(2,1)S(1)} all-to-all(bf16[16,136,128]{2,1,0:T(8,128)(2,1)S(1)} %shard_map.42), channel_id=1, replica_groups=mesh['yh'=4,'x'=4,'c'=2,'z'=8,'yl'=2] {'yh','x'}, dimensions={0} | all-to-all | bytes 1114112 | tf_op jit(solution)/shard_map/all_to_all | solution.py:367
  176.6 1.3 shard_map.43
  (9 shorter events, 0.0 us)
Async XLA Ops:
  26.8 4.8 %copy-start = (bf16[1024,1024]{1,0:T(8,128)(2,1)S(1)}, bf16[1024,1024]{1,0:T(8,128)(2,1)}, u32[]{:S(2)}) copy-start(bf16[1024,1024]{1,0:T(8,128)(2,1)} %train_ref.3) | copy-start | bytes 6291460
  35.2 37.6 %all-to-all-start.2 = ((bf16[16,264,128]{2,1,0:T(8,128)(2,1)}), bf16[16,264,128]{2,1,0:T(8,128)(2,1)}, u32[]{:S(2)}, u32[]{:S(2)}) async-start(bf16[16,264,128]{2,1,0:T(8,128)(2,1)} %shard_map.37), calls=%async_computation.2 | async-start | bytes 2162688 | tf_op jit(solution)/shard_map/all_to_all | solution.py:308
  45.6 79.9 %copy-start.3 = (f32[512]{0:T(512)S(1)}, f32[512]{0:T(512)}, u32[]{:S(2)}) copy-start(f32[512]{0:T(512)} %param.5) | copy-start | bytes 6148
  45.6 95.9 %collective-permute-start.3 = (bf16[1024,1024]{1,0:T(8,128)(2,1)S(1)}, bf16[1024,1024]{1,0:T(8,128)(2,1)}, u32[]{:S(2)}, u32[]{:S(2)}) collective-permute-start(bf16[1024,1024]{1,0:T(8,128)(2,1)S(1)} %copy-done), channel_id=1, source_target_pairs={{0,16},{16,0},{1,17},{17,1},{2,18},{18,2},{3,19},{19,3},{4,20},{20... | collective-permute-start | bytes 6291464 | tf_op jit(solution)/shard_map/ppermute | solution.py:293
  98.3 14.7 %collective-permute-start.1 = (bf16[8,272,128]{2,1,0:T(8,128)(2,1)S(1)}, bf16[8,272,128]{2,1,0:T(8,128)(2,1)S(1)}, u32[]{:S(2)}, u32[]{:S(2)}) collective-permute-start(bf16[8,272,128]{2,1,0:T(8,128)(2,1)S(1)} %all_to_all.37.own_ref), channel_id=1, source_target_pairs={{0,1},{1,0},{2,3},{3,2},{4,5},{5,4},{6,7},{7,6},{8,9},{9,8},{10,11... | collective-permute-start | bytes 1671176 | tf_op jit(solution)/shard_map/ppermute | solution.py:319
  102.1 32.6 %collective-permute-start = (bf16[8,272,128]{2,1,0:T(8,128)(2,1)S(1)}, bf16[8,272,128]{2,1,0:T(8,128)(2,1)S(1)}, u32[]{:S(2)}, u32[]{:S(2)}) collective-permute-start(bf16[8,272,128]{2,1,0:T(8,128)(2,1)S(1)} %all_to_all.37.own_ref), channel_id=1, source_target_pairs={{0,16},{16,0},{1,17},{17,1},{2,18},{18,2},{3,19},{19,3},{4,20},{20... | collective-permute-start | bytes 1671176 | tf_op jit(solution)/shard_map/ppermute | solution.py:320
  113.9 0.8 copy-start.1
  114.7 35.0 %collective-permute-start.2 = (bf16[8,272,128]{2,1,0:T(8,128)(2,1)}, bf16[8,272,128]{2,1,0:T(8,128)(2,1)}, u32[]{:S(2)}, u32[]{:S(2)}) collective-permute-start(bf16[8,272,128]{2,1,0:T(8,128)(2,1)} %shard_map.41), channel_id=1, source_target_pairs={{0,16},{16,0},{1,17},{17,1},{2,18},{18,2},{3,19},{19,3},{4,20},{20... | collective-permute-start | bytes 1671176 | tf_op jit(solution)/shard_map/ppermute | solution.py:349
  117.4 17.3 %all-to-all-start.4 = ((f32[64,4,128]{2,1,0:T(4,128)}), f32[64,4,128]{2,1,0:T(4,128)S(1)}, u32[]{:S(2)}, u32[]{:S(2)}) async-start(f32[64,4,128]{2,1,0:T(4,128)} %shard_map.39), calls=%async_computation.4 | async-start | bytes 262144 | tf_op jit(solution)/shard_map/all_to_all | solution.py:333
  135.9 13.8 %all-to-all-start.5 = ((f32[32,4,128]{2,1,0:T(4,128)}), f32[32,4,128]{2,1,0:T(4,128)S(1)}, u32[]{:S(2)}, u32[]{:S(2)}) async-start(f32[32,4,128]{2,1,0:T(4,128)} %get-tuple-element.8), calls=%async_computation.5 | async-start | bytes 131072 | tf_op jit(solution)/shard_map/all_to_all | solution.py:341
  149.7 1.1 copy-start.2

commit v6 on v5

--- a/solution.py
+++ b/solution.py
@@ -194,43 +194,50 @@
     out_ref,
     plan_ref,
     cols_ref,
+    blocks_vmem,
     train_vmem,
     sems,
 ):
-    nz = own_ref.shape[0]
+    _, nz, _, _ = blocks_vmem.shape
     nl = sums_ref.shape[1]
     nh = nl // 2
     rows = nz * sub
     c, yl = place_ref[0], place_ref[1]
+    sources = (own_ref, core_own_ref, other_ref, core_other_ref)
+    loads = [
+        pltpu.make_async_copy(src, blocks_vmem.at[k], sems.at[k])
+        for k, src in enumerate(sources)
+    ]
     copies = [
-        pltpu.make_async_copy(src, train_vmem.at[k], sems.at[k])
+        pltpu.make_async_copy(src, train_vmem.at[k], sems.at[len(sources) + k])
         for k, src in enumerate((train_ref, core_train_ref))
     ]
-    for copy in copies:
+    for copy in loads + copies:
         copy.start()
     far = far_ref[...]
     col = col_ref[...] * (b_ref[...] / jnp.sum(sums_ref[...], axis=0))
 
-    refs = ((own_ref, 0, 0), (other_ref, 0, 1), (core_own_ref, 1, 0), (core_other_ref, 1, 1))
-
-    def step(z, cols):
+    def step(i, z, cols):
         cols = list(cols)
-        for ref, k, flip in refs:
-            factor = jnp.exp(block_shift(ref, z, sub, nl) - far) * col
-            plan = [block_part(ref, z, sub, n) * factor[n : n + 1] for n in range(nl)]
-            row = a / jnp.sum(functools.reduce(jnp.add, plan), axis=1, keepdims=True)
-            side = yl + flip * (1 - 2 * yl)
-            start = pl.multiple_of(side * rows + z * sub, sub)
-            for n in range(nl):
-                part = plan[n] * row
-                cols[n] = cols[n] + jnp.sum(part, axis=0, keepdims=True)
-                lane = (n % nh) * LANES
-                plan_ref[n // nh, k, pl.ds(start, sub), lane : lane + LANES] = part.astype(
-                    jnp.bfloat16
-                )
+        ref = blocks_vmem.at[i]
+        factor = jnp.exp(block_shift(ref, z, sub, nl) - far) * col
+        plan = [block_part(ref, z, sub, n) * factor[n : n + 1] for n in range(nl)]
+        row = a / jnp.sum(functools.reduce(jnp.add, plan), axis=1, keepdims=True)
+        side = yl if i < 2 else 1 - yl
+        start = pl.multiple_of(side * rows + z * sub, sub)
+        for n in range(nl):
+            part = plan[n] * row
+            cols[n] = cols[n] + jnp.sum(part, axis=0, keepdims=True)
+            lane = (n % nh) * LANES
+            plan_ref[n // nh, i % 2, pl.ds(start, sub), lane : lane + LANES] = part.astype(
+                jnp.bfloat16
+            )
         return tuple(cols)
 
-    cols = lax.fori_loop(0, nz, step, (jnp.zeros((1, LANES), jnp.float32),) * nl)
+    cols = (jnp.zeros((1, LANES), jnp.float32),) * nl
+    for i in range(len(sources)):
+        loads[i].wait()
+        cols = lax.fori_loop(0, nz, functools.partial(step, i), cols, unroll=2)
     for n in range(nl):
         cols_ref[n // nh, n % nh] = cols[n]
 
@@ -293,9 +300,10 @@
     core_train = lax.ppermute(train, "c", SWAP)
 
     same_core = spread(target, CHIPS, nchips).reshape(nchips * mine, feats)
-    targets = spread(same_core, "c", nc).reshape(nt, feats)
     mass = mass.reshape(nchips, nc, mine).transpose(1, 0, 2).reshape(nl, LANES)
     b = mass / jnp.sum(mass)
+    same_core, b = lax.optimization_barrier((same_core, b))
+    targets = spread(same_core, "c", nc).reshape(nt, feats)
 
     codes = pl.pallas_call(
         functools.partial(encode_kernel, sub),
@@ -354,13 +362,14 @@
     send = pl.pallas_call(
         functools.partial(mixture_kernel, sub, a),
         out_shape=jax.ShapeDtypeStruct((nchips, block, LANES), jnp.bfloat16),
-        in_specs=[scalars] + [full] * 8 + [anywhere] * 2,
+        in_specs=[scalars] + [full] * 4 + [anywhere] * 6,
         out_specs=full,
         scratch_shapes=[
             VMEM((nc, 2, rows, half), jnp.bfloat16),
             VMEM((nc, nl // nc, 1, LANES), jnp.float32),
+            VMEM((4,) + own.shape, jnp.bfloat16),
             VMEM((2, rows, feats), jnp.bfloat16),
-            pltpu.SemaphoreType.DMA((2,)),
+            pltpu.SemaphoreType.DMA((6,)),
         ],
         compiler_params=LARGE,
     )(place, sums, far, col, b, own, other, core_own, core_other, train, core_train)

time: 180 us -> 180 us (level)
  blocking collectives: 75.4 us -> 66.4 us
  waiting for transfers between devices: 50.1 us -> 55.5 us
  starting transfers between devices: 33.6 us -> 35.6 us
    all_to_all x2 -> x1, blocking collectives: 30.6 us -> 4.58 us  [spread(): return lax.all_to_all(copies, axes, 0, 0, tiled=True)]
    all_to_all x0 -> x1, blocking collectives: none -> 17.1 us  [shards(): stats = lax.all_to_all(stats, ROWS, 0, 0, tiled=True)]
    all_to_all x1, waiting for transfers between devices: 7.75 us -> 13.1 us  [spread(): return lax.all_to_all(copies, axes, 0, 0, tiled=True)]
    all_to_all x1, starting transfers between devices: 8.05 us -> 10.1 us  [spread(): return lax.all_to_all(copies, axes, 0, 0, tiled=True)]
  transfers between devices with their start and end apart: 7 -> 7, of which waited for: 4 -> 4; matrix products, arithmetic and copies ran while one was open for 1% -> 2% of each run, Pallas kernels for 3% -> 3%
where the time goes in v6:
time: 180 us; the launch traced here: 178 us
  blocking collectives  66.4 us (37%)
  waiting for transfers between devices  55.5 us (31%)
  starting transfers between devices  35.6 us (20%)
  Pallas kernels  13.1 us (7%)
  local copies, waits for them, and re-layouts  3.99 us (2%)
  other arithmetic  2.84 us (2%)
    all_to_all x1, waiting for transfers between devices, shards(): codes = lax.all_to_all(codes, PIECES, 0, 0, tiled=True)  25.2 us
    all_to_all x1, blocking collectives, shards(): own = lax.all_to_all(blocks, 'z', 0, 0, tiled=True)  23.2 us
    all_to_all x1, blocking collectives, shards(): got = lax.all_to_all(send, CHIPS, 0, 0, tiled=True)  21.6 us
    all_to_all x1, blocking collectives, shards(): stats = lax.all_to_all(stats, ROWS, 0, 0, tiled=True)  17.1 us
    all_to_all x1, waiting for transfers between devices, spread(): return lax.all_to_all(copies, axes, 0, 0, tiled=True)  13.1 us
    all_to_all x1, starting transfers between devices, shards(): codes = lax.all_to_all(codes, PIECES, 0, 0, tiled=True)  10.5 us
    all_to_all x1, starting transfers between devices, spread(): return lax.all_to_all(copies, axes, 0, 0, tiled=True)  10.1 us
    ppermute x1, waiting for transfers between devices, shards(): other = lax.ppermute(own, 'yl', SWAP)  9.01 us
  transfers between devices with their start and end apart: 7, of which 4 were waited for; matrix products, arithmetic and copies ran while one was open for 2% of the time, Pallas kernels for 3%

profile of v6, /device:TPU:6, one launch (start us, length us, event | category | flops | bytes accessed | tf_op | source)
XLA Modules:
  0.0 177.6 jit_solution(1781789669938842559)
XLA Ops:
  0.0 1.6 broadcast_in_dim.4
  1.6 10.1 %all-to-all-start = ((bf16[16,16,1024]{2,1,0:T(8,128)(2,1)}), bf16[16,16,1024]{2,1,0:T(8,128)(2,1)S(1)}, u32[]{:S(2)}, u32[]{:S(2)}) async-start(bf16[16,16,1024]{2,1,0:T(8,128)(2,1)} %broadcast_in_dim.4), calls=%async_computation | async-start | bytes 1048576 | tf_op jit(solution)/shard_map/all_to_all | solution.py:130
  11.7 1.4 reduce_sum.9
  13.1 1.3 broadcast_divide_fusion
  14.4 0.1 div.17
  14.6 0.1 div.19.b_ref
  14.6 13.1 %all-to-all-done = bf16[16,16,1024]{2,1,0:T(8,128)(2,1)S(1)} async-done(((bf16[16,16,1024]{2,1,0:T(8,128)(2,1)}), bf16[16,16,1024]{2,1,0:T(8,128)(2,1)S(1)}, u32[]{:S(2)}, u32[]{:S(2)}) %all-to-all-start) | async-done | bytes 524320 | tf_op jit(solution)/shard_map/all_to_all | solution.py:130
  27.8 0.1 broadcast_in_dim.5
  27.9 4.6 %all_to_all.35 = bf16[2,256,1024]{2,1,0:T(8,128)(2,1)S(1)} all-to-all(bf16[2,256,1024]{2,1,0:T(8,128)(2,1)S(1)} %broadcast_in_dim.5), channel_id=1, replica_groups=mesh['yh'=4,'x'=4,'c'=2,'z'=8,'yl'=2] {'c'}, dimensions={0} | all-to-all | bytes 2097152 | tf_op jit(solution)/shard_map/all_to_all | solution.py:130
  32.5 2.5 %shard_map.37 = bf16[16,264,128]{2,1,0:T(8,128)(2,1)S(1)} custom-call(bf16[1024,1024]{1,0:T(8,128)(2,1)S(1)} %copy-done, bf16[512,1024]{1,0:T(8,128)(2,1)S(1)} %bitcast.6), custom_call_target="tpu_custom_call" | custom-call | tf_op jit(solution)/shard_map/pallas_call | solution.py:308
  35.0 1.0 copy-done.1
  36.0 10.5 %all-to-all-start.2 = ((bf16[16,264,128]{2,1,0:T(8,128)(2,1)}), bf16[16,264,128]{2,1,0:T(8,128)(2,1)}, u32[]{:S(2)}, u32[]{:S(2)}) async-start(bf16[16,264,128]{2,1,0:T(8,128)(2,1)} %copy-done.1), calls=%async_computation.2 | async-start | bytes 2162688 | tf_op jit(solution)/shard_map/all_to_all | solution.py:316
  46.5 1.9 %collective-permute-start.3 = (bf16[1024,1024]{1,0:T(8,128)(2,1)S(1)}, bf16[1024,1024]{1,0:T(8,128)(2,1)}, u32[]{:S(2)}, u32[]{:S(2)}) collective-permute-start(bf16[1024,1024]{1,0:T(8,128)(2,1)S(1)} %copy-done), channel_id=1, source_target_pairs={{0,16},{16,0},{1,17},{17,1},{2,18},{18,2},{3,19},{19,3},{4,20},{20... | collective-permute-start | bytes 6291464 | tf_op jit(solution)/shard_map/ppermute | solution.py:300
  48.4 25.2 %all-to-all-done.2.codes_ref = bf16[16,264,128]{2,1,0:T(8,128)(2,1)} async-done(((bf16[16,264,128]{2,1,0:T(8,128)(2,1)}), bf16[16,264,128]{2,1,0:T(8,128)(2,1)}, u32[]{:S(2)}, u32[]{:S(2)}) %all-to-all-start.2) | async-done | bytes 1081376 | tf_op jit(solution)/shard_map/all_to_all | solution.py:316
  73.6 2.4 %shard_map.38 = bf16[8,272,128]{2,1,0:T(8,128)(2,1)S(1)} custom-call(bf16[16,264,128]{2,1,0:T(8,128)(2,1)} %all-to-all-done.2.codes_ref), custom_call_target="tpu_custom_call" | custom-call | tf_op jit(solution)/shard_map/pallas_call | solution.py:317
  76.0 23.2 %all_to_all.36.own_ref = bf16[8,272,128]{2,1,0:T(8,128)(2,1)S(1)} all-to-all(bf16[8,272,128]{2,1,0:T(8,128)(2,1)S(1)} %shard_map.38), channel_id=1, replica_groups=mesh['yh'=4,'x'=4,'c'=2,'z'=8,'yl'=2] {'z'}, dimensions={0} | all-to-all | bytes 1114112 | tf_op jit(solution)/shard_map/all_to_all | solution.py:326
  99.2 3.8 %collective-permute-start.1 = (bf16[8,272,128]{2,1,0:T(8,128)(2,1)S(1)}, bf16[8,272,128]{2,1,0:T(8,128)(2,1)S(1)}, u32[]{:S(2)}, u32[]{:S(2)}) collective-permute-start(bf16[8,272,128]{2,1,0:T(8,128)(2,1)S(1)} %all_to_all.36.own_ref), channel_id=1, source_target_pairs={{0,1},{1,0},{2,3},{3,2},{4,5},{5,4},{6,7},{7,6},{8,9},{9,8},{10,11... | collective-permute-start | bytes 1671176 | tf_op jit(solution)/shard_map/ppermute | solution.py:327
  103.0 1.9 %collective-permute-start = (bf16[8,272,128]{2,1,0:T(8,128)(2,1)S(1)}, bf16[8,272,128]{2,1,0:T(8,128)(2,1)S(1)}, u32[]{:S(2)}, u32[]{:S(2)}) collective-permute-start(bf16[8,272,128]{2,1,0:T(8,128)(2,1)S(1)} %all_to_all.36.own_ref), channel_id=1, source_target_pairs={{0,16},{16,0},{1,17},{17,1},{2,18},{18,2},{3,19},{19,3},{4,20},{20... | collective-permute-start | bytes 1671176 | tf_op jit(solution)/shard_map/ppermute | solution.py:328
  104.9 9.0 %collective-permute-done.1.in_ref.other_ref = bf16[8,272,128]{2,1,0:T(8,128)(2,1)S(1)} collective-permute-done((bf16[8,272,128]{2,1,0:T(8,128)(2,1)S(1)}, bf16[8,272,128]{2,1,0:T(8,128)(2,1)S(1)}, u32[]{:S(2)}, u32[]{:S(2)}) %collective-permute-start.1) | collective-permute-done | bytes 557088 | tf_op jit(solution)/shard_map/ppermute | solution.py:327
  113.9 0.9 shard_map.41
  114.8 1.9 %collective-permute-start.2 = (bf16[8,272,128]{2,1,0:T(8,128)(2,1)}, bf16[8,272,128]{2,1,0:T(8,128)(2,1)}, u32[]{:S(2)}, u32[]{:S(2)}) collective-permute-start(bf16[8,272,128]{2,1,0:T(8,128)(2,1)} %shard_map.41), channel_id=1, source_target_pairs={{0,16},{16,0},{1,17},{17,1},{2,18},{18,2},{3,19},{19,3},{4,20},{20... | collective-permute-start | bytes 1671176 | tf_op jit(solution)/shard_map/ppermute | solution.py:357
  116.7 0.1 shard_map.39
  116.9 17.1 %all_to_all.37.stats_ref = f32[64,4,128]{2,1,0:T(4,128)S(1)} all-to-all(f32[64,4,128]{2,1,0:T(4,128)S(1)} %shard_map.39), channel_id=1, replica_groups=mesh['yh'=4,'x'=4,'c'=2,'z'=8,'yl'=2] {'yh','x','c','yl'}, dimensions={0} | all-to-all | bytes 262144 | tf_op jit(solution)/shard_map/all_to_all | solution.py:341
  133.9 1.2 shard_map.40
  135.1 5.5 %all-to-all-start.5 = ((f32[32,4,128]{2,1,0:T(4,128)}), f32[32,4,128]{2,1,0:T(4,128)S(1)}, u32[]{:S(2)}, u32[]{:S(2)}) async-start(f32[32,4,128]{2,1,0:T(4,128)} %get-tuple-element.12), calls=%async_computation.5 | async-start | bytes 131072 | tf_op jit(solution)/shard_map/all_to_all | solution.py:349
  140.7 0.1 pad_add_fusion.place_ref
  140.8 8.2 %all-to-all-done.5.sums_ref = f32[32,4,128]{2,1,0:T(4,128)S(1)} async-done(((f32[32,4,128]{2,1,0:T(4,128)}), f32[32,4,128]{2,1,0:T(4,128)S(1)}, u32[]{:S(2)}, u32[]{:S(2)}) %all-to-all-start.5) | async-done | bytes 65568 | tf_op jit(solution)/shard_map/all_to_all | solution.py:349
  148.9 0.0 collective-permute-done.2.core_other_ref
  148.9 1.1 copy-done.3
  150.0 4.7 %shard_map.42 = bf16[16,136,128]{2,1,0:T(8,128)(2,1)S(1)} custom-call(s32[3]{0:T(128)S(1)} %pad_add_fusion.place_ref, f32[32,4,128]{2,1,0:T(4,128)S(1)} %all-to-all-done.5.sums_ref, f32[4,128]{1,0:T(4,128)S(1)} %get-tuple-element.13.far_ref, f32[4,128]{1,0:T(4,128)S(1)} %get-tuple-element.14.col_ref, f32[4,128]{1,0:T(4,128)S(1)} %div.19.b_ref, ...), custom_call_target="tpu_custom_call" | custom-call | tf_op jit(solution)/shard_map/pallas_call | solution.py:362
  154.7 21.6 %all_to_all.38.got_ref = bf16[16,136,128]{2,1,0:T(8,128)(2,1)S(1)} all-to-all(bf16[16,136,128]{2,1,0:T(8,128)(2,1)S(1)} %shard_map.42), channel_id=1, replica_groups=mesh['yh'=4,'x'=4,'c'=2,'z'=8,'yl'=2] {'yh','x'}, dimensions={0} | all-to-all | bytes 1114112 | tf_op jit(solution)/shard_map/all_to_all | solution.py:376
  176.3 1.3 shard_map.43
  (9 shorter events, 0.0 us)
Async XLA Ops:
  1.6 26.1 %all-to-all-start = ((bf16[16,16,1024]{2,1,0:T(8,128)(2,1)}), bf16[16,16,1024]{2,1,0:T(8,128)(2,1)S(1)}, u32[]{:S(2)}, u32[]{:S(2)}) async-start(bf16[16,16,1024]{2,1,0:T(8,128)(2,1)} %broadcast_in_dim.4), calls=%async_computation | async-start | bytes 1048576 | tf_op jit(solution)/shard_map/all_to_all | solution.py:130
  11.7 20.8 %copy-start = (bf16[1024,1024]{1,0:T(8,128)(2,1)S(1)}, bf16[1024,1024]{1,0:T(8,128)(2,1)}, u32[]{:S(2)}) copy-start(bf16[1024,1024]{1,0:T(8,128)(2,1)} %train_ref.3) | copy-start | bytes 6291460
  35.0 1.0 copy-start.1
  36.0 37.6 %all-to-all-start.2 = ((bf16[16,264,128]{2,1,0:T(8,128)(2,1)}), bf16[16,264,128]{2,1,0:T(8,128)(2,1)}, u32[]{:S(2)}, u32[]{:S(2)}) async-start(bf16[16,264,128]{2,1,0:T(8,128)(2,1)} %copy-done.1), calls=%async_computation.2 | async-start | bytes 2162688 | tf_op jit(solution)/shard_map/all_to_all | solution.py:316
  46.5 94.3 %collective-permute-start.3 = (bf16[1024,1024]{1,0:T(8,128)(2,1)S(1)}, bf16[1024,1024]{1,0:T(8,128)(2,1)}, u32[]{:S(2)}, u32[]{:S(2)}) collective-permute-start(bf16[1024,1024]{1,0:T(8,128)(2,1)S(1)} %copy-done), channel_id=1, source_target_pairs={{0,16},{16,0},{1,17},{17,1},{2,18},{18,2},{3,19},{19,3},{4,20},{20... | collective-permute-start | bytes 6291464 | tf_op jit(solution)/shard_map/ppermute | solution.py:300
  99.2 14.7 %collective-permute-start.1 = (bf16[8,272,128]{2,1,0:T(8,128)(2,1)S(1)}, bf16[8,272,128]{2,1,0:T(8,128)(2,1)S(1)}, u32[]{:S(2)}, u32[]{:S(2)}) collective-permute-start(bf16[8,272,128]{2,1,0:T(8,128)(2,1)S(1)} %all_to_all.36.own_ref), channel_id=1, source_target_pairs={{0,1},{1,0},{2,3},{3,2},{4,5},{5,4},{6,7},{7,6},{8,9},{9,8},{10,11... | collective-permute-start | bytes 1671176 | tf_op jit(solution)/shard_map/ppermute | solution.py:327
  103.0 31.0 %collective-permute-start = (bf16[8,272,128]{2,1,0:T(8,128)(2,1)S(1)}, bf16[8,272,128]{2,1,0:T(8,128)(2,1)S(1)}, u32[]{:S(2)}, u32[]{:S(2)}) collective-permute-start(bf16[8,272,128]{2,1,0:T(8,128)(2,1)S(1)} %all_to_all.36.own_ref), channel_id=1, source_target_pairs={{0,16},{16,0},{1,17},{17,1},{2,18},{18,2},{3,19},{19,3},{4,20},{20... | collective-permute-start | bytes 1671176 | tf_op jit(solution)/shard_map/ppermute | solution.py:328
  113.9 20.0 %copy-start.2 = (bf16[8,272,128]{2,1,0:T(8,128)(2,1)}, bf16[8,272,128]{2,1,0:T(8,128)(2,1)S(1)}, u32[]{:S(2)}) copy-start(bf16[8,272,128]{2,1,0:T(8,128)(2,1)S(1)} %collective-permute-done.1.in_ref.other_ref) | copy-start | bytes 1671172
  114.8 34.1 %collective-permute-start.2 = (bf16[8,272,128]{2,1,0:T(8,128)(2,1)}, bf16[8,272,128]{2,1,0:T(8,128)(2,1)}, u32[]{:S(2)}, u32[]{:S(2)}) collective-permute-start(bf16[8,272,128]{2,1,0:T(8,128)(2,1)} %shard_map.41), channel_id=1, source_target_pairs={{0,16},{16,0},{1,17},{17,1},{2,18},{18,2},{3,19},{19,3},{4,20},{20... | collective-permute-start | bytes 1671176 | tf_op jit(solution)/shard_map/ppermute | solution.py:357
  135.1 13.8 %all-to-all-start.5 = ((f32[32,4,128]{2,1,0:T(4,128)}), f32[32,4,128]{2,1,0:T(4,128)S(1)}, u32[]{:S(2)}, u32[]{:S(2)}) async-start(f32[32,4,128]{2,1,0:T(4,128)} %get-tuple-element.12), calls=%async_computation.5 | async-start | bytes 131072 | tf_op jit(solution)/shard_map/all_to_all | solution.py:349
  148.9 1.1 copy-start.3

commit v7 on v6

--- a/solution.py
+++ b/solution.py
@@ -61,10 +61,11 @@
 
 def encode_kernel(sub, train_ref, targets_ref, out_ref, partial_ref):
     rows = train_ref.shape[0]
-    step = partial_ref.shape[0]
+    step = partial_ref.shape[1]
     on_diagonal = diagonal(sub)
     for start in range(0, rows, step):
-        partial_ref[...] = lax.dot_general(
+        slot = start // step % 2
+        partial_ref[slot] = lax.dot_general(
             train_ref[start : start + step, :],
             targets_ref[...],
             (((1,), (1,)), ((), ())),
@@ -72,7 +73,7 @@
         )
         for j in range(step // sub):
             k = start // sub + j
-            p = partial_ref[j * sub : (j + 1) * sub, :]
+            p = partial_ref[slot, j * sub : (j + 1) * sub, :]
             high = jnp.max(p, axis=1, keepdims=True)
             low = jnp.min(p, axis=1, keepdims=True)
             p = p - 0.5 * (high + low)
@@ -81,7 +82,7 @@
             p = p * (1.0 / row)
             col = round_up(jnp.maximum(jnp.max(jnp.abs(p), axis=0, keepdims=True), 1e-30))
             u = p * (1.0 / col)
-            code = jnp.exp2(jnp.minimum(jnp.abs(u), 1.0) * SPAN - BASE)
+            code = jnp.exp2(jnp.abs(u) * SPAN - BASE)
             code = jnp.where(u < 0, -code, code).astype(jnp.bfloat16)
             parts = lane_blocks(code)
             for n, part in enumerate(parts):
@@ -139,36 +140,44 @@
     return ref[z, n * sub : (n + 1) * sub, :].astype(jnp.float32)
 
 
+def group_sum(v):
+    return functools.reduce(jnp.add, [v[k : k + 8] for k in range(0, v.shape[0], 8)])
+
+
 def statistics_kernel(sub, own_ref, out_ref):
     nz = own_ref.shape[0]
     nl = out_ref.shape[1]
     shifts = [block_shift(own_ref, z, sub, nl) for z in range(nz)]
     top = functools.reduce(jnp.maximum, shifts)
-    total = [jnp.zeros((1, LANES), jnp.float32)] * nl
+    total = [jnp.zeros((8, LANES), jnp.float32)] * nl
     for z in range(nz):
         factor = jnp.exp(shifts[z] - top)
         for n in range(nl):
-            part = jnp.sum(block_part(own_ref, z, sub, n), axis=0, keepdims=True)
+            part = group_sum(block_part(own_ref, z, sub, n))
             total[n] = total[n] + factor[n : n + 1] * part
+    total = [jnp.sum(t, axis=0, keepdims=True) for t in total]
     log_sum = top + jnp.log(stack_rows(total, nl))
     out_ref[...] = jnp.broadcast_to(log_sum[None], out_ref.shape)
 
 
-def columns_kernel(sub, a, stats_ref, own_ref, core_ref, b_ref, far_ref, col_ref, out_ref):
+def columns_kernel(sub, a, stats_ref, own_ref, core_ref, mass_ref, far_ref, col_ref, b_ref, out_ref):
     nz = own_ref.shape[0]
     nl = out_ref.shape[1]
     stats = stats_ref[...]
     far = jnp.max(stats, axis=0)
-    col = b_ref[...] / jnp.sum(jnp.exp(stats - far[None]), axis=0)
-    cols = [jnp.zeros((1, LANES), jnp.float32)] * nl
+    b = mass_ref[...] / jnp.sum(mass_ref[...])
+    col = b / jnp.sum(jnp.exp(stats - far[None]), axis=0)
+    cols = [jnp.zeros((8, LANES), jnp.float32)] * nl
     for z in range(nz):
         for ref in (own_ref, core_ref):
             factor = jnp.exp(block_shift(ref, z, sub, nl) - far) * col
             plan = [block_part(ref, z, sub, n) * factor[n : n + 1] for n in range(nl)]
             row = a / jnp.sum(functools.reduce(jnp.add, plan), axis=1, keepdims=True)
             for n in range(nl):
-                cols[n] = cols[n] + jnp.sum(plan[n] * row, axis=0, keepdims=True)
+                cols[n] = cols[n] + group_sum(plan[n] * row)
+    cols = [jnp.sum(t, axis=0, keepdims=True) for t in cols]
     far_ref[...] = far
+    b_ref[...] = b
     col_ref[...] = col
     out_ref[...] = jnp.broadcast_to(stack_rows(cols, nl)[None], out_ref.shape)
 
@@ -193,7 +202,6 @@
     core_train_ref,
     out_ref,
     plan_ref,
-    cols_ref,
     blocks_vmem,
     train_vmem,
     sems,
@@ -218,39 +226,34 @@
     col = col_ref[...] * (b_ref[...] / jnp.sum(sums_ref[...], axis=0))
 
     def step(i, z, cols):
-        cols = list(cols)
         ref = blocks_vmem.at[i]
         factor = jnp.exp(block_shift(ref, z, sub, nl) - far) * col
         plan = [block_part(ref, z, sub, n) * factor[n : n + 1] for n in range(nl)]
         row = a / jnp.sum(functools.reduce(jnp.add, plan), axis=1, keepdims=True)
         side = yl if i < 2 else 1 - yl
-        start = pl.multiple_of(side * rows + z * sub, sub)
-        for n in range(nl):
-            part = plan[n] * row
-            cols[n] = cols[n] + jnp.sum(part, axis=0, keepdims=True)
-            lane = (n % nh) * LANES
-            plan_ref[n // nh, i % 2, pl.ds(start, sub), lane : lane + LANES] = part.astype(
-                jnp.bfloat16
-            )
-        return tuple(cols)
-
-    cols = (jnp.zeros((1, LANES), jnp.float32),) * nl
+        start = pl.multiple_of((i % 2 * 2 + side) * rows + z * sub, sub)
+        sums = []
+        for n in range(nh):
+            part = jnp.where(c == 0, plan[n], plan[nh + n]) * row
+            sums.append(cols[n] + group_sum(part))
+            lane = n * LANES
+            plan_ref[pl.ds(start, sub), lane : lane + LANES] = part.astype(jnp.bfloat16)
+        return tuple(sums)
+
+    cols = (jnp.zeros((8, LANES), jnp.float32),) * nh
     for i in range(len(sources)):
         loads[i].wait()
         cols = lax.fori_loop(0, nz, functools.partial(step, i), cols, unroll=2)
-    for n in range(nl):
-        cols_ref[n // nh, n % nh] = cols[n]
 
     half = nh * LANES
-    mixed = jnp.zeros((half, train_ref.shape[1]), jnp.float32)
-    for k in range(2):
-        copies[k].wait()
-        mixed += lax.dot_general(
-            plan_ref[c, k],
-            train_vmem[k],
-            (((0,), (0,)), ((), ())),
-            preferred_element_type=jnp.float32,
-        )
+    for copy in copies:
+        copy.wait()
+    mixed = lax.dot_general(
+        plan_ref[...],
+        train_vmem[...].reshape(4 * rows, train_ref.shape[1]),
+        (((0,), (0,)), ((), ())),
+        preferred_element_type=jnp.float32,
+    )
     nchips = out_ref.shape[0]
     mine = half // nchips
     parts = lane_blocks(mixed.astype(jnp.bfloat16))
@@ -258,7 +261,8 @@
         out_ref[:, n * mine : (n + 1) * mine, :] = part.reshape(nchips, mine, LANES)
     per = LANES // mine
     for n in range(nh):
-        tail = stack_rows(split3(cols_ref[c, n]), MIXTURE_TAIL).astype(jnp.bfloat16)
+        total = jnp.sum(cols[n], axis=0, keepdims=True)
+        tail = stack_rows(split3(total), MIXTURE_TAIL).astype(jnp.bfloat16)
         out_ref[n * per : (n + 1) * per, len(parts) * mine :, :] = jnp.broadcast_to(
             tail[None], (per, MIXTURE_TAIL, LANES)
         )
@@ -301,8 +305,6 @@
 
     same_core = spread(target, CHIPS, nchips).reshape(nchips * mine, feats)
     mass = mass.reshape(nchips, nc, mine).transpose(1, 0, 2).reshape(nl, LANES)
-    b = mass / jnp.sum(mass)
-    same_core, b = lax.optimization_barrier((same_core, b))
     targets = spread(same_core, "c", nc).reshape(nt, feats)
 
     codes = pl.pallas_call(
@@ -310,7 +312,7 @@
         out_shape=jax.ShapeDtypeStruct((nf, nl * sub + CODE_TAIL, LANES), jnp.bfloat16),
         in_specs=[full] * 2,
         out_specs=full,
-        scratch_shapes=[VMEM((4 * sub, nt), jnp.float32)],
+        scratch_shapes=[VMEM((2, 4 * sub, nt), jnp.float32)],
         compiler_params=MIDDLE,
     )(train, targets)
     codes = lax.all_to_all(codes, PIECES, 0, 0, tiled=True)
@@ -339,13 +341,13 @@
         compiler_params=SMALL,
     )(own)
     stats = lax.all_to_all(stats, ROWS, 0, 0, tiled=True)
-    far, col, sums = pl.pallas_call(
+    far, col, b, sums = pl.pallas_call(
         functools.partial(columns_kernel, sub, a),
-        out_shape=(vector, vector, copies(CHIP_ROWS)),
+        out_shape=(vector, vector, vector, copies(CHIP_ROWS)),
         in_specs=[full] * 4,
-        out_specs=(full,) * 3,
+        out_specs=(full,) * 4,
         compiler_params=SMALL,
-    )(stats, own, core_own, b)
+    )(stats, own, core_own, mass)
     sums = lax.all_to_all(sums, CHIP_ROWS, 0, 0, tiled=True)
     other_copy = pl.pallas_call(
         copy_kernel,
@@ -365,8 +367,7 @@
         in_specs=[scalars] + [full] * 4 + [anywhere] * 6,
         out_specs=full,
         scratch_shapes=[
-            VMEM((nc, 2, rows, half), jnp.bfloat16),
-            VMEM((nc, nl // nc, 1, LANES), jnp.float32),
+            VMEM((nc * rows, half), jnp.bfloat16),
             VMEM((4,) + own.shape, jnp.bfloat16),
             VMEM((2, rows, feats), jnp.bfloat16),
             pltpu.SemaphoreType.DMA((6,)),

time: 180 us -> 180 us (level)
  blocking collectives: 66.4 us -> 75.4 us
  waiting for transfers between devices: 55.5 us -> 51.3 us
  other arithmetic: 2.84 us -> 0.08 us
  starting transfers between devices: 35.6 us -> 33.6 us
    all_to_all x1 -> x2, blocking collectives: 4.58 us -> 30.6 us  [spread(): return lax.all_to_all(copies, axes, 0, 0, tiled=True)]
    all_to_all x1 -> x0, blocking collectives: 17.1 us -> none  [shards(): stats = lax.all_to_all(stats, ROWS, 0, 0, tiled=True)]
    all_to_all x1, waiting for transfers between devices: 13.1 us -> 9.01 us  [shards(): stats = lax.all_to_all(stats, ROWS, 0, 0, tiled=True)]
    all_to_all x1, starting transfers between devices: 10.1 us -> 8.07 us  [shards(): stats = lax.all_to_all(stats, ROWS, 0, 0, tiled=True)]
  transfers between devices with their start and end apart: 7 -> 7, of which waited for: 4 -> 4; matrix products, arithmetic and copies ran while one was open for 2% -> 0% of each run, Pallas kernels for 3% -> 3%
where the time goes in v7:
time: 180 us; the launch traced here: 178 us
  blocking collectives  75.4 us (42%)
  waiting for transfers between devices  51.3 us (28%)
  starting transfers between devices  33.6 us (19%)
  Pallas kernels  13.1 us (7%)
  local copies, waits for them, and re-layouts  3.96 us (2%)
    all_to_all x2, blocking collectives, spread(): return lax.all_to_all(copies, axes, 0, 0, tiled=True)  30.6 us
    all_to_all x1, waiting for transfers between devices, shards(): codes = lax.all_to_all(codes, PIECES, 0, 0, tiled=True)  25.2 us
    all_to_all x1, blocking collectives, shards(): own = lax.all_to_all(blocks, 'z', 0, 0, tiled=True)  23.2 us
    all_to_all x1, blocking collectives, shards(): got = lax.all_to_all(send, CHIPS, 0, 0, tiled=True)  21.6 us
    all_to_all x1, starting transfers between devices, shards(): codes = lax.all_to_all(codes, PIECES, 0, 0, tiled=True)  10.5 us
    all_to_all x1, waiting for transfers between devices, shards(): stats = lax.all_to_all(stats, ROWS, 0, 0, tiled=True)  9.01 us
    ppermute x1, waiting for transfers between devices, shards(): other = lax.ppermute(own, 'yl', SWAP)  8.99 us
    all_to_all x1, waiting for transfers between devices, shards(): sums = lax.all_to_all(sums, CHIP_ROWS, 0, 0, tiled=True)  8.15 us
  transfers between devices with their start and end apart: 7, of which 4 were waited for; matrix products, arithmetic and copies ran while one was open for 0% of the time, Pallas kernels for 3%

profile of v7, /device:TPU:6, one launch (start us, length us, event | category | flops | bytes accessed | tf_op | source)
XLA Modules:
  0.0 177.7 jit_solution(14158450256073988208)
XLA Ops:
  0.0 0.8 broadcast_in_dim.6
  0.8 25.9 %all_to_all.35 = bf16[16,16,1024]{2,1,0:T(8,128)(2,1)S(1)} all-to-all(bf16[16,16,1024]{2,1,0:T(8,128)(2,1)S(1)} %broadcast_in_dim.6), channel_id=1, replica_groups=mesh['yh'=4,'x'=4,'c'=2,'z'=8,'yl'=2] {'yh','x'}, dimensions={0} | all-to-all | bytes 1048576 | tf_op jit(solution)/shard_map/all_to_all | solution.py:131
  26.8 0.1 broadcast_in_dim.15
  26.9 4.7 %all_to_all.36 = bf16[2,256,1024]{2,1,0:T(8,128)(2,1)S(1)} all-to-all(bf16[2,256,1024]{2,1,0:T(8,128)(2,1)S(1)} %broadcast_in_dim.15), channel_id=1, replica_groups=mesh['yh'=4,'x'=4,'c'=2,'z'=8,'yl'=2] {'c'}, dimensions={0} | all-to-all | bytes 2097152 | tf_op jit(solution)/shard_map/all_to_all | solution.py:131
  31.6 2.5 %shard_map.37 = bf16[16,264,128]{2,1,0:T(8,128)(2,1)S(1)} custom-call(bf16[1024,1024]{1,0:T(8,128)(2,1)S(1)} %copy-done, bf16[512,1024]{1,0:T(8,128)(2,1)S(1)} %bitcast.6), custom_call_target="tpu_custom_call" | custom-call | tf_op jit(solution)/shard_map/pallas_call | solution.py:310
  34.1 1.0 copy-done.1
  35.1 10.5 %all-to-all-start.2 = ((bf16[16,264,128]{2,1,0:T(8,128)(2,1)}), bf16[16,264,128]{2,1,0:T(8,128)(2,1)}, u32[]{:S(2)}, u32[]{:S(2)}) async-start(bf16[16,264,128]{2,1,0:T(8,128)(2,1)} %copy-done.1), calls=%async_computation.2 | async-start | bytes 2162688 | tf_op jit(solution)/shard_map/all_to_all | solution.py:318
  45.5 0.0 copy-start.4
  45.5 1.9 %collective-permute-start.3 = (bf16[1024,1024]{1,0:T(8,128)(2,1)S(1)}, bf16[1024,1024]{1,0:T(8,128)(2,1)}, u32[]{:S(2)}, u32[]{:S(2)}) collective-permute-start(bf16[1024,1024]{1,0:T(8,128)(2,1)S(1)} %copy-done), channel_id=1, source_target_pairs={{0,16},{16,0},{1,17},{17,1},{2,18},{18,2},{3,19},{19,3},{4,20},{20... | collective-permute-start | bytes 6291464 | tf_op jit(solution)/shard_map/ppermute | solution.py:304
  47.5 25.2 %all-to-all-done.2.codes_ref = bf16[16,264,128]{2,1,0:T(8,128)(2,1)} async-done(((bf16[16,264,128]{2,1,0:T(8,128)(2,1)}), bf16[16,264,128]{2,1,0:T(8,128)(2,1)}, u32[]{:S(2)}, u32[]{:S(2)}) %all-to-all-start.2) | async-done | bytes 1081376 | tf_op jit(solution)/shard_map/all_to_all | solution.py:318
  72.7 2.4 %shard_map.38 = bf16[8,272,128]{2,1,0:T(8,128)(2,1)S(1)} custom-call(bf16[16,264,128]{2,1,0:T(8,128)(2,1)} %all-to-all-done.2.codes_ref), custom_call_target="tpu_custom_call" | custom-call | tf_op jit(solution)/shard_map/pallas_call | solution.py:319
  75.0 23.2 %all_to_all.37.own_ref = bf16[8,272,128]{2,1,0:T(8,128)(2,1)S(1)} all-to-all(bf16[8,272,128]{2,1,0:T(8,128)(2,1)S(1)} %shard_map.38), channel_id=1, replica_groups=mesh['yh'=4,'x'=4,'c'=2,'z'=8,'yl'=2] {'z'}, dimensions={0} | all-to-all | bytes 1114112 | tf_op jit(solution)/shard_map/all_to_all | solution.py:328
  98.2 3.8 %collective-permute-start.1 = (bf16[8,272,128]{2,1,0:T(8,128)(2,1)S(1)}, bf16[8,272,128]{2,1,0:T(8,128)(2,1)S(1)}, u32[]{:S(2)}, u32[]{:S(2)}) collective-permute-start(bf16[8,272,128]{2,1,0:T(8,128)(2,1)S(1)} %all_to_all.37.own_ref), channel_id=1, source_target_pairs={{0,1},{1,0},{2,3},{3,2},{4,5},{5,4},{6,7},{7,6},{8,9},{9,8},{10,11... | collective-permute-start | bytes 1671176 | tf_op jit(solution)/shard_map/ppermute | solution.py:329
  102.0 1.9 %collective-permute-start = (bf16[8,272,128]{2,1,0:T(8,128)(2,1)S(1)}, bf16[8,272,128]{2,1,0:T(8,128)(2,1)S(1)}, u32[]{:S(2)}, u32[]{:S(2)}) collective-permute-start(bf16[8,272,128]{2,1,0:T(8,128)(2,1)S(1)} %all_to_all.37.own_ref), channel_id=1, source_target_pairs={{0,16},{16,0},{1,17},{17,1},{2,18},{18,2},{3,19},{19,3},{4,20},{20... | collective-permute-start | bytes 1671176 | tf_op jit(solution)/shard_map/ppermute | solution.py:330
  104.0 9.0 %collective-permute-done.1.in_ref.other_ref = bf16[8,272,128]{2,1,0:T(8,128)(2,1)S(1)} collective-permute-done((bf16[8,272,128]{2,1,0:T(8,128)(2,1)S(1)}, bf16[8,272,128]{2,1,0:T(8,128)(2,1)S(1)}, u32[]{:S(2)}, u32[]{:S(2)}) %collective-permute-start.1) | collective-permute-done | bytes 557088 | tf_op jit(solution)/shard_map/ppermute | solution.py:329
  112.9 0.8 shard_map.41
  113.8 0.8 copy-done.2
  114.6 1.9 %collective-permute-start.2 = (bf16[8,272,128]{2,1,0:T(8,128)(2,1)}, bf16[8,272,128]{2,1,0:T(8,128)(2,1)}, u32[]{:S(2)}, u32[]{:S(2)}) collective-permute-start(bf16[8,272,128]{2,1,0:T(8,128)(2,1)} %shard_map.41), channel_id=1, source_target_pairs={{0,16},{16,0},{1,17},{17,1},{2,18},{18,2},{3,19},{19,3},{4,20},{20... | collective-permute-start | bytes 1671176 | tf_op jit(solution)/shard_map/ppermute | solution.py:359
  116.5 0.8 shard_map.39
  117.3 8.1 %all-to-all-start.4 = ((f32[64,4,128]{2,1,0:T(4,128)}), f32[64,4,128]{2,1,0:T(4,128)S(1)}, u32[]{:S(2)}, u32[]{:S(2)}) async-start(f32[64,4,128]{2,1,0:T(4,128)} %shard_map.39), calls=%async_computation.4 | async-start | bytes 262144 | tf_op jit(solution)/shard_map/all_to_all | solution.py:343
  125.4 0.1 reshape.12
  125.5 0.1 reshape.13.mass_ref
  125.6 9.0 %all-to-all-done.4.stats_ref = f32[64,4,128]{2,1,0:T(4,128)S(1)} async-done(((f32[64,4,128]{2,1,0:T(4,128)}), f32[64,4,128]{2,1,0:T(4,128)S(1)}, u32[]{:S(2)}, u32[]{:S(2)}) %all-to-all-start.4) | async-done | bytes 131104 | tf_op jit(solution)/shard_map/all_to_all | solution.py:343
  134.6 0.0 collective-permute-done.core_ref.core_own_ref
  134.6 1.2 shard_map.40
  135.7 5.5 %all-to-all-start.5 = ((f32[32,4,128]{2,1,0:T(4,128)}), f32[32,4,128]{2,1,0:T(4,128)S(1)}, u32[]{:S(2)}, u32[]{:S(2)}) async-start(f32[32,4,128]{2,1,0:T(4,128)} %get-tuple-element.9), calls=%async_computation.5 | async-start | bytes 131072 | tf_op jit(solution)/shard_map/all_to_all | solution.py:351
  141.3 0.1 pad_add_fusion.place_ref
  141.4 8.2 %all-to-all-done.5.sums_ref = f32[32,4,128]{2,1,0:T(4,128)S(1)} async-done(((f32[32,4,128]{2,1,0:T(4,128)}), f32[32,4,128]{2,1,0:T(4,128)S(1)}, u32[]{:S(2)}, u32[]{:S(2)}) %all-to-all-start.5) | async-done | bytes 65568 | tf_op jit(solution)/shard_map/all_to_all | solution.py:351
  149.5 1.1 copy-done.3
  150.6 4.3 %shard_map.42 = bf16[16,136,128]{2,1,0:T(8,128)(2,1)S(1)} custom-call(s32[3]{0:T(128)S(1)} %pad_add_fusion.place_ref, f32[32,4,128]{2,1,0:T(4,128)S(1)} %all-to-all-done.5.sums_ref, f32[4,128]{1,0:T(4,128)S(1)} %get-tuple-element.10.far_ref, f32[4,128]{1,0:T(4,128)S(1)} %get-tuple-element.11.col_ref, f32[4,128]{1,0:T(4,128)S(1)} %get-tuple-element.12.b_ref, ...), custom_call_target="tpu_custom_call" | custom-call | tf_op jit(solution)/shard_map/pallas_call | solution.py:364
  154.9 21.6 %all_to_all.38.got_ref = bf16[16,136,128]{2,1,0:T(8,128)(2,1)S(1)} all-to-all(bf16[16,136,128]{2,1,0:T(8,128)(2,1)S(1)} %shard_map.42), channel_id=1, replica_groups=mesh['yh'=4,'x'=4,'c'=2,'z'=8,'yl'=2] {'yh','x'}, dimensions={0} | all-to-all | bytes 1114112 | tf_op jit(solution)/shard_map/all_to_all | solution.py:377
  176.5 1.3 shard_map.43
  (9 shorter events, 0.0 us)
Async XLA Ops:
  26.8 4.8 %copy-start = (bf16[1024,1024]{1,0:T(8,128)(2,1)S(1)}, bf16[1024,1024]{1,0:T(8,128)(2,1)}, u32[]{:S(2)}) copy-start(bf16[1024,1024]{1,0:T(8,128)(2,1)} %train_ref.3) | copy-start | bytes 6291460
  34.0 1.0 copy-start.1
  35.1 37.6 %all-to-all-start.2 = ((bf16[16,264,128]{2,1,0:T(8,128)(2,1)}), bf16[16,264,128]{2,1,0:T(8,128)(2,1)}, u32[]{:S(2)}, u32[]{:S(2)}) async-start(bf16[16,264,128]{2,1,0:T(8,128)(2,1)} %copy-done.1), calls=%async_computation.2 | async-start | bytes 2162688 | tf_op jit(solution)/shard_map/all_to_all | solution.py:318
  45.5 79.8 %copy-start.4 = (f32[512]{0:T(512)S(1)}, f32[512]{0:T(512)}, u32[]{:S(2)}) copy-start(f32[512]{0:T(512)} %param.5) | copy-start | bytes 6148
  45.5 95.8 %collective-permute-start.3 = (bf16[1024,1024]{1,0:T(8,128)(2,1)S(1)}, bf16[1024,1024]{1,0:T(8,128)(2,1)}, u32[]{:S(2)}, u32[]{:S(2)}) collective-permute-start(bf16[1024,1024]{1,0:T(8,128)(2,1)S(1)} %copy-done), channel_id=1, source_target_pairs={{0,16},{16,0},{1,17},{17,1},{2,18},{18,2},{3,19},{19,3},{4,20},{20... | collective-permute-start | bytes 6291464 | tf_op jit(solution)/shard_map/ppermute | solution.py:304
  98.2 14.7 %collective-permute-start.1 = (bf16[8,272,128]{2,1,0:T(8,128)(2,1)S(1)}, bf16[8,272,128]{2,1,0:T(8,128)(2,1)S(1)}, u32[]{:S(2)}, u32[]{:S(2)}) collective-permute-start(bf16[8,272,128]{2,1,0:T(8,128)(2,1)S(1)} %all_to_all.37.own_ref), channel_id=1, source_target_pairs={{0,1},{1,0},{2,3},{3,2},{4,5},{5,4},{6,7},{7,6},{8,9},{9,8},{10,11... | collective-permute-start | bytes 1671176 | tf_op jit(solution)/shard_map/ppermute | solution.py:329
  102.0 32.5 %collective-permute-start = (bf16[8,272,128]{2,1,0:T(8,128)(2,1)S(1)}, bf16[8,272,128]{2,1,0:T(8,128)(2,1)S(1)}, u32[]{:S(2)}, u32[]{:S(2)}) collective-permute-start(bf16[8,272,128]{2,1,0:T(8,128)(2,1)S(1)} %all_to_all.37.own_ref), channel_id=1, source_target_pairs={{0,16},{16,0},{1,17},{17,1},{2,18},{18,2},{3,19},{19,3},{4,20},{20... | collective-permute-start | bytes 1671176 | tf_op jit(solution)/shard_map/ppermute | solution.py:330
  113.8 0.8 copy-start.2
  114.6 34.9 %collective-permute-start.2 = (bf16[8,272,128]{2,1,0:T(8,128)(2,1)}, bf16[8,272,128]{2,1,0:T(8,128)(2,1)}, u32[]{:S(2)}, u32[]{:S(2)}) collective-permute-start(bf16[8,272,128]{2,1,0:T(8,128)(2,1)} %shard_map.41), channel_id=1, source_target_pairs={{0,16},{16,0},{1,17},{17,1},{2,18},{18,2},{3,19},{19,3},{4,20},{20... | collective-permute-start | bytes 1671176 | tf_op jit(solution)/shard_map/ppermute | solution.py:359
  117.3 17.3 %all-to-all-start.4 = ((f32[64,4,128]{2,1,0:T(4,128)}), f32[64,4,128]{2,1,0:T(4,128)S(1)}, u32[]{:S(2)}, u32[]{:S(2)}) async-start(f32[64,4,128]{2,1,0:T(4,128)} %shard_map.39), calls=%async_computation.4 | async-start | bytes 262144 | tf_op jit(solution)/shard_map/all_to_all | solution.py:343
  135.7 13.8 %all-to-all-start.5 = ((f32[32,4,128]{2,1,0:T(4,128)}), f32[32,4,128]{2,1,0:T(4,128)S(1)}, u32[]{:S(2)}, u32[]{:S(2)}) async-start(f32[32,4,128]{2,1,0:T(4,128)} %get-tuple-element.9), calls=%async_computation.5 | async-start | bytes 131072 | tf_op jit(solution)/shard_map/all_to_all | solution.py:351
  149.5 1.1 copy-start.3

commit v8 on v7

--- a/solution.py
+++ b/solution.py
@@ -10,7 +10,7 @@
 
 
 F = 16384
-CHIPS = ("yh", "x")
+CHIPS = ("x", "yh")
 EX = ("yh", "x", "c")
 FEAT = ("z", "yl")
 PIECES = ("yl", "z")
@@ -304,7 +304,8 @@
     core_train = lax.ppermute(train, "c", SWAP)
 
     same_core = spread(target, CHIPS, nchips).reshape(nchips * mine, feats)
-    mass = mass.reshape(nchips, nc, mine).transpose(1, 0, 2).reshape(nl, LANES)
+    mass = mass.reshape(lax.axis_size("yh"), lax.axis_size("x"), nc, mine)
+    mass = mass.transpose(2, 1, 0, 3).reshape(nl, LANES)
     targets = spread(same_core, "c", nc).reshape(nt, feats)
 
     codes = pl.pallas_call(

time: 180 us -> 179 us (level)
  no operation moved by 1% of the time
where the time goes in v8:
time: 179 us; the launch traced here: 178 us
  blocking collectives  76.1 us (43%)
  waiting for transfers between devices  51.3 us (29%)
  starting transfers between devices  32.8 us (18%)
  Pallas kernels  13.1 us (7%)
  local copies, waits for them, and re-layouts  3.97 us (2%)
    all_to_all x2, blocking collectives, spread(): return lax.all_to_all(copies, axes, 0, 0, tiled=True)  31 us
    all_to_all x1, waiting for transfers between devices, shards(): codes = lax.all_to_all(codes, PIECES, 0, 0, tiled=True)  25.2 us
    all_to_all x1, blocking collectives, shards(): own = lax.all_to_all(blocks, 'z', 0, 0, tiled=True)  23.2 us
    all_to_all x1, blocking collectives, shards(): got = lax.all_to_all(send, CHIPS, 0, 0, tiled=True)  21.8 us
    all_to_all x1, starting transfers between devices, shards(): codes = lax.all_to_all(codes, PIECES, 0, 0, tiled=True)  10.5 us
    all_to_all x1, waiting for transfers between devices, shards(): stats = lax.all_to_all(stats, ROWS, 0, 0, tiled=True)  9 us
    ppermute x1, waiting for transfers between devices, shards(): other = lax.ppermute(own, 'yl', SWAP)  8.99 us
    all_to_all x1, waiting for transfers between devices, shards(): sums = lax.all_to_all(sums, CHIP_ROWS, 0, 0, tiled=True)  8.15 us
  transfers between devices with their start and end apart: 7, of which 4 were waited for; matrix products, arithmetic and copies ran while one was open for 0% of the time, Pallas kernels for 3%

profile of v8, /device:TPU:6, one launch (start us, length us, event | category | flops | bytes accessed | tf_op | source)
XLA Modules:
  0.0 177.5 jit_solution(12034782580866839634)
XLA Ops:
  0.0 0.8 broadcast_in_dim.6
  0.8 26.3 %all_to_all.35 = bf16[16,16,1024]{2,1,0:T(8,128)(2,1)S(1)} all-to-all(bf16[16,16,1024]{2,1,0:T(8,128)(2,1)S(1)} %broadcast_in_dim.6), channel_id=1, replica_groups=mesh['yh'=4,'x'=4,'c'=2,'z'=8,'yl'=2] {'x','yh'}, dimensions={0} | all-to-all | bytes 1048576 | tf_op jit(solution)/shard_map/all_to_all | solution.py:131
  27.2 0.1 broadcast_in_dim.15
  27.3 4.7 %all_to_all.36 = bf16[2,256,1024]{2,1,0:T(8,128)(2,1)S(1)} all-to-all(bf16[2,256,1024]{2,1,0:T(8,128)(2,1)S(1)} %broadcast_in_dim.15), channel_id=1, replica_groups=mesh['yh'=4,'x'=4,'c'=2,'z'=8,'yl'=2] {'c'}, dimensions={0} | all-to-all | bytes 2097152 | tf_op jit(solution)/shard_map/all_to_all | solution.py:131
  32.0 2.5 %shard_map.37 = bf16[16,264,128]{2,1,0:T(8,128)(2,1)S(1)} custom-call(bf16[1024,1024]{1,0:T(8,128)(2,1)S(1)} %copy-done, bf16[512,1024]{1,0:T(8,128)(2,1)S(1)} %bitcast.6), custom_call_target="tpu_custom_call" | custom-call | tf_op jit(solution)/shard_map/pallas_call | solution.py:311
  34.5 1.0 copy-done.1
  35.5 10.5 %all-to-all-start.2 = ((bf16[16,264,128]{2,1,0:T(8,128)(2,1)}), bf16[16,264,128]{2,1,0:T(8,128)(2,1)}, u32[]{:S(2)}, u32[]{:S(2)}) async-start(bf16[16,264,128]{2,1,0:T(8,128)(2,1)} %copy-done.1), calls=%async_computation.2 | async-start | bytes 2162688 | tf_op jit(solution)/shard_map/all_to_all | solution.py:319
  45.9 0.0 copy-start.4
  45.9 1.9 %collective-permute-start.3 = (bf16[1024,1024]{1,0:T(8,128)(2,1)S(1)}, bf16[1024,1024]{1,0:T(8,128)(2,1)}, u32[]{:S(2)}, u32[]{:S(2)}) collective-permute-start(bf16[1024,1024]{1,0:T(8,128)(2,1)S(1)} %copy-done), channel_id=1, source_target_pairs={{0,16},{16,0},{1,17},{17,1},{2,18},{18,2},{3,19},{19,3},{4,20},{20... | collective-permute-start | bytes 6291464 | tf_op jit(solution)/shard_map/ppermute | solution.py:304
  47.9 25.2 %all-to-all-done.2.codes_ref = bf16[16,264,128]{2,1,0:T(8,128)(2,1)} async-done(((bf16[16,264,128]{2,1,0:T(8,128)(2,1)}), bf16[16,264,128]{2,1,0:T(8,128)(2,1)}, u32[]{:S(2)}, u32[]{:S(2)}) %all-to-all-start.2) | async-done | bytes 1081376 | tf_op jit(solution)/shard_map/all_to_all | solution.py:319
  73.1 2.4 %shard_map.38 = bf16[8,272,128]{2,1,0:T(8,128)(2,1)S(1)} custom-call(bf16[16,264,128]{2,1,0:T(8,128)(2,1)} %all-to-all-done.2.codes_ref), custom_call_target="tpu_custom_call" | custom-call | tf_op jit(solution)/shard_map/pallas_call | solution.py:320
  75.4 23.2 %all_to_all.37.own_ref = bf16[8,272,128]{2,1,0:T(8,128)(2,1)S(1)} all-to-all(bf16[8,272,128]{2,1,0:T(8,128)(2,1)S(1)} %shard_map.38), channel_id=1, replica_groups=mesh['yh'=4,'x'=4,'c'=2,'z'=8,'yl'=2] {'z'}, dimensions={0} | all-to-all | bytes 1114112 | tf_op jit(solution)/shard_map/all_to_all | solution.py:329
  98.6 3.8 %collective-permute-start.1 = (bf16[8,272,128]{2,1,0:T(8,128)(2,1)S(1)}, bf16[8,272,128]{2,1,0:T(8,128)(2,1)S(1)}, u32[]{:S(2)}, u32[]{:S(2)}) collective-permute-start(bf16[8,272,128]{2,1,0:T(8,128)(2,1)S(1)} %all_to_all.37.own_ref), channel_id=1, source_target_pairs={{0,1},{1,0},{2,3},{3,2},{4,5},{5,4},{6,7},{7,6},{8,9},{9,8},{10,11... | collective-permute-start | bytes 1671176 | tf_op jit(solution)/shard_map/ppermute | solution.py:330
  102.4 1.9 %collective-permute-start = (bf16[8,272,128]{2,1,0:T(8,128)(2,1)S(1)}, bf16[8,272,128]{2,1,0:T(8,128)(2,1)S(1)}, u32[]{:S(2)}, u32[]{:S(2)}) collective-permute-start(bf16[8,272,128]{2,1,0:T(8,128)(2,1)S(1)} %all_to_all.37.own_ref), channel_id=1, source_target_pairs={{0,16},{16,0},{1,17},{17,1},{2,18},{18,2},{3,19},{19,3},{4,20},{20... | collective-permute-start | bytes 1671176 | tf_op jit(solution)/shard_map/ppermute | solution.py:331
  104.4 9.0 %collective-permute-done.1.in_ref.other_ref = bf16[8,272,128]{2,1,0:T(8,128)(2,1)S(1)} collective-permute-done((bf16[8,272,128]{2,1,0:T(8,128)(2,1)S(1)}, bf16[8,272,128]{2,1,0:T(8,128)(2,1)S(1)}, u32[]{:S(2)}, u32[]{:S(2)}) %collective-permute-start.1) | collective-permute-done | bytes 557088 | tf_op jit(solution)/shard_map/ppermute | solution.py:330
  113.3 0.8 shard_map.41
  114.2 0.8 copy-done.2
  115.0 1.9 %collective-permute-start.2 = (bf16[8,272,128]{2,1,0:T(8,128)(2,1)}, bf16[8,272,128]{2,1,0:T(8,128)(2,1)}, u32[]{:S(2)}, u32[]{:S(2)}) collective-permute-start(bf16[8,272,128]{2,1,0:T(8,128)(2,1)} %shard_map.41), channel_id=1, source_target_pairs={{0,16},{16,0},{1,17},{17,1},{2,18},{18,2},{3,19},{19,3},{4,20},{20... | collective-permute-start | bytes 1671176 | tf_op jit(solution)/shard_map/ppermute | solution.py:360
  116.9 0.8 shard_map.39
  117.7 7.2 %all-to-all-start.4 = ((f32[64,4,128]{2,1,0:T(4,128)}), f32[64,4,128]{2,1,0:T(4,128)S(1)}, u32[]{:S(2)}, u32[]{:S(2)}) async-start(f32[64,4,128]{2,1,0:T(4,128)} %shard_map.39), calls=%async_computation.4 | async-start | bytes 262144 | tf_op jit(solution)/shard_map/all_to_all | solution.py:344
  124.9 0.1 reshape.12
  125.0 0.1 reshape.13.mass_ref
  125.1 9.0 %all-to-all-done.4.stats_ref = f32[64,4,128]{2,1,0:T(4,128)S(1)} async-done(((f32[64,4,128]{2,1,0:T(4,128)}), f32[64,4,128]{2,1,0:T(4,128)S(1)}, u32[]{:S(2)}, u32[]{:S(2)}) %all-to-all-start.4) | async-done | bytes 131104 | tf_op jit(solution)/shard_map/all_to_all | solution.py:344
  134.1 0.0 collective-permute-done.core_ref.core_own_ref
  134.1 1.2 shard_map.40
  135.3 5.5 %all-to-all-start.5 = ((f32[32,4,128]{2,1,0:T(4,128)}), f32[32,4,128]{2,1,0:T(4,128)S(1)}, u32[]{:S(2)}, u32[]{:S(2)}) async-start(f32[32,4,128]{2,1,0:T(4,128)} %get-tuple-element.9), calls=%async_computation.5 | async-start | bytes 131072 | tf_op jit(solution)/shard_map/all_to_all | solution.py:352
  140.8 0.1 pad_add_fusion.place_ref
  140.9 8.2 %all-to-all-done.5.sums_ref = f32[32,4,128]{2,1,0:T(4,128)S(1)} async-done(((f32[32,4,128]{2,1,0:T(4,128)}), f32[32,4,128]{2,1,0:T(4,128)S(1)}, u32[]{:S(2)}, u32[]{:S(2)}) %all-to-all-start.5) | async-done | bytes 65568 | tf_op jit(solution)/shard_map/all_to_all | solution.py:352
  149.1 1.1 copy-done.3
  150.1 4.3 %shard_map.42 = bf16[16,136,128]{2,1,0:T(8,128)(2,1)S(1)} custom-call(s32[3]{0:T(128)S(1)} %pad_add_fusion.place_ref, f32[32,4,128]{2,1,0:T(4,128)S(1)} %all-to-all-done.5.sums_ref, f32[4,128]{1,0:T(4,128)S(1)} %get-tuple-element.10.far_ref, f32[4,128]{1,0:T(4,128)S(1)} %get-tuple-element.11.col_ref, f32[4,128]{1,0:T(4,128)S(1)} %get-tuple-element.12.b_ref, ...), custom_call_target="tpu_custom_call" | custom-call | tf_op jit(solution)/shard_map/pallas_call | solution.py:365
  154.4 21.8 %all_to_all.38.got_ref = bf16[16,136,128]{2,1,0:T(8,128)(2,1)S(1)} all-to-all(bf16[16,136,128]{2,1,0:T(8,128)(2,1)S(1)} %shard_map.42), channel_id=1, replica_groups=mesh['yh'=4,'x'=4,'c'=2,'z'=8,'yl'=2] {'x','yh'}, dimensions={0} | all-to-all | bytes 1114112 | tf_op jit(solution)/shard_map/all_to_all | solution.py:378
  176.2 1.3 shard_map.43
  (9 shorter events, 0.0 us)
Async XLA Ops:
  27.1 4.8 %copy-start = (bf16[1024,1024]{1,0:T(8,128)(2,1)S(1)}, bf16[1024,1024]{1,0:T(8,128)(2,1)}, u32[]{:S(2)}) copy-start(bf16[1024,1024]{1,0:T(8,128)(2,1)} %train_ref.3) | copy-start | bytes 6291460
  34.4 1.0 copy-start.1
  35.5 37.6 %all-to-all-start.2 = ((bf16[16,264,128]{2,1,0:T(8,128)(2,1)}), bf16[16,264,128]{2,1,0:T(8,128)(2,1)}, u32[]{:S(2)}, u32[]{:S(2)}) async-start(bf16[16,264,128]{2,1,0:T(8,128)(2,1)} %copy-done.1), calls=%async_computation.2 | async-start | bytes 2162688 | tf_op jit(solution)/shard_map/all_to_all | solution.py:319
  45.9 79.0 %copy-start.4 = (f32[512]{0:T(512)S(1)}, f32[512]{0:T(512)}, u32[]{:S(2)}) copy-start(f32[512]{0:T(512)} %param.5) | copy-start | bytes 6148
  45.9 95.0 %collective-permute-start.3 = (bf16[1024,1024]{1,0:T(8,128)(2,1)S(1)}, bf16[1024,1024]{1,0:T(8,128)(2,1)}, u32[]{:S(2)}, u32[]{:S(2)}) collective-permute-start(bf16[1024,1024]{1,0:T(8,128)(2,1)S(1)} %copy-done), channel_id=1, source_target_pairs={{0,16},{16,0},{1,17},{17,1},{2,18},{18,2},{3,19},{19,3},{4,20},{20... | collective-permute-start | bytes 6291464 | tf_op jit(solution)/shard_map/ppermute | solution.py:304
  98.6 14.7 %collective-permute-start.1 = (bf16[8,272,128]{2,1,0:T(8,128)(2,1)S(1)}, bf16[8,272,128]{2,1,0:T(8,128)(2,1)S(1)}, u32[]{:S(2)}, u32[]{:S(2)}) collective-permute-start(bf16[8,272,128]{2,1,0:T(8,128)(2,1)S(1)} %all_to_all.37.own_ref), channel_id=1, source_target_pairs={{0,1},{1,0},{2,3},{3,2},{4,5},{5,4},{6,7},{7,6},{8,9},{9,8},{10,11... | collective-permute-start | bytes 1671176 | tf_op jit(solution)/shard_map/ppermute | solution.py:330
  102.4 31.7 %collective-permute-start = (bf16[8,272,128]{2,1,0:T(8,128)(2,1)S(1)}, bf16[8,272,128]{2,1,0:T(8,128)(2,1)S(1)}, u32[]{:S(2)}, u32[]{:S(2)}) collective-permute-start(bf16[8,272,128]{2,1,0:T(8,128)(2,1)S(1)} %all_to_all.37.own_ref), channel_id=1, source_target_pairs={{0,16},{16,0},{1,17},{17,1},{2,18},{18,2},{3,19},{19,3},{4,20},{20... | collective-permute-start | bytes 1671176 | tf_op jit(solution)/shard_map/ppermute | solution.py:331
  114.2 0.8 copy-start.2
  115.0 34.1 %collective-permute-start.2 = (bf16[8,272,128]{2,1,0:T(8,128)(2,1)}, bf16[8,272,128]{2,1,0:T(8,128)(2,1)}, u32[]{:S(2)}, u32[]{:S(2)}) collective-permute-start(bf16[8,272,128]{2,1,0:T(8,128)(2,1)} %shard_map.41), channel_id=1, source_target_pairs={{0,16},{16,0},{1,17},{17,1},{2,18},{18,2},{3,19},{19,3},{4,20},{20... | collective-permute-start | bytes 1671176 | tf_op jit(solution)/shard_map/ppermute | solution.py:360
  117.7 16.4 %all-to-all-start.4 = ((f32[64,4,128]{2,1,0:T(4,128)}), f32[64,4,128]{2,1,0:T(4,128)S(1)}, u32[]{:S(2)}, u32[]{:S(2)}) async-start(f32[64,4,128]{2,1,0:T(4,128)} %shard_map.39), calls=%async_computation.4 | async-start | bytes 262144 | tf_op jit(solution)/shard_map/all_to_all | solution.py:344
  135.3 13.8 %all-to-all-start.5 = ((f32[32,4,128]{2,1,0:T(4,128)}), f32[32,4,128]{2,1,0:T(4,128)S(1)}, u32[]{:S(2)}, u32[]{:S(2)}) async-start(f32[32,4,128]{2,1,0:T(4,128)} %get-tuple-element.9), calls=%async_computation.5 | async-start | bytes 131072 | tf_op jit(solution)/shard_map/all_to_all | solution.py:352
  149.1 1.1 copy-start.3

commit v9 on v8

--- a/solution.py
+++ b/solution.py
@@ -14,8 +14,8 @@
 EX = ("yh", "x", "c")
 FEAT = ("z", "yl")
 PIECES = ("yl", "z")
-ROWS = ("yh", "x", "c", "yl")
-CHIP_ROWS = ("yh", "x", "yl")
+ROWS = ("x", "yh", "yl", "c")
+CHIP_ROWS = ("x", "yh", "yl")
 LANES = 128
 CODE_TAIL = 8
 KERNEL_TAIL = 16
@@ -195,8 +195,8 @@
     col_ref,
     b_ref,
     own_ref,
+    core_own_ref,
     other_ref,
-    core_own_ref,
     core_other_ref,
     train_ref,
     core_train_ref,
@@ -211,13 +211,14 @@
     nh = nl // 2
     rows = nz * sub
     c, yl = place_ref[0], place_ref[1]
-    sources = (own_ref, core_own_ref, other_ref, core_other_ref)
+    late = (other_ref, core_other_ref)
     loads = [
         pltpu.make_async_copy(src, blocks_vmem.at[k], sems.at[k])
-        for k, src in enumerate(sources)
+        for k, src in enumerate(late)
     ]
+    sources = (own_ref, core_own_ref, blocks_vmem.at[0], blocks_vmem.at[1])
     copies = [
-        pltpu.make_async_copy(src, train_vmem.at[k], sems.at[len(sources) + k])
+        pltpu.make_async_copy(src, train_vmem.at[k], sems.at[len(late) + k])
         for k, src in enumerate((train_ref, core_train_ref))
     ]
     for copy in loads + copies:
@@ -226,7 +227,7 @@
     col = col_ref[...] * (b_ref[...] / jnp.sum(sums_ref[...], axis=0))
 
     def step(i, z, cols):
-        ref = blocks_vmem.at[i]
+        ref = sources[i]
         factor = jnp.exp(block_shift(ref, z, sub, nl) - far) * col
         plan = [block_part(ref, z, sub, n) * factor[n : n + 1] for n in range(nl)]
         row = a / jnp.sum(functools.reduce(jnp.add, plan), axis=1, keepdims=True)
@@ -242,7 +243,8 @@
 
     cols = (jnp.zeros((8, LANES), jnp.float32),) * nh
     for i in range(len(sources)):
-        loads[i].wait()
+        if i >= 2:
+            loads[i - 2].wait()
         cols = lax.fori_loop(0, nz, functools.partial(step, i), cols, unroll=2)
 
     half = nh * LANES
@@ -365,16 +367,16 @@
     send = pl.pallas_call(
         functools.partial(mixture_kernel, sub, a),
         out_shape=jax.ShapeDtypeStruct((nchips, block, LANES), jnp.bfloat16),
-        in_specs=[scalars] + [full] * 4 + [anywhere] * 6,
+        in_specs=[scalars] + [full] * 6 + [anywhere] * 4,
         out_specs=full,
         scratch_shapes=[
             VMEM((nc * rows, half), jnp.bfloat16),
-            VMEM((4,) + own.shape, jnp.bfloat16),
+            VMEM((2,) + own.shape, jnp.bfloat16),
             VMEM((2, rows, feats), jnp.bfloat16),
-            pltpu.SemaphoreType.DMA((6,)),
+            pltpu.SemaphoreType.DMA((4,)),
         ],
         compiler_params=LARGE,
-    )(place, sums, far, col, b, own, other, core_own, core_other, train, core_train)
+    )(place, sums, far, col, b, own, core_own, other, core_other, train, core_train)
     got = lax.all_to_all(send, CHIPS, 0, 0, tiled=True)
     return pl.pallas_call(
         output_kernel,

time: 179 us -> 179 us (level)
  no operation moved by 1% of the time
where the time goes in v9:
time: 179 us; the launch traced here: 177 us
  blocking collectives  75.8 us (42%)
  waiting for transfers between devices  50.9 us (28%)
  starting transfers between devices  33.2 us (19%)
  Pallas kernels  13 us (7%)
  local copies, waits for them, and re-layouts  3.97 us (2%)
    all_to_all x2, blocking collectives, spread(): return lax.all_to_all(copies, axes, 0, 0, tiled=True)  31 us
    all_to_all x1, waiting for transfers between devices, shards(): codes = lax.all_to_all(codes, PIECES, 0, 0, tiled=True)  25.2 us
    all_to_all x1, blocking collectives, shards(): own = lax.all_to_all(blocks, 'z', 0, 0, tiled=True)  23.2 us
    all_to_all x1, blocking collectives, shards(): got = lax.all_to_all(send, CHIPS, 0, 0, tiled=True)  21.6 us
    all_to_all x1, starting transfers between devices, shards(): codes = lax.all_to_all(codes, PIECES, 0, 0, tiled=True)  10.5 us
    ppermute x1, waiting for transfers between devices, shards(): other = lax.ppermute(own, 'yl', SWAP)  8.99 us
    all_to_all x1, waiting for transfers between devices, shards(): stats = lax.all_to_all(stats, ROWS, 0, 0, tiled=True)  8.64 us
    all_to_all x1, waiting for transfers between devices, shards(): sums = lax.all_to_all(sums, CHIP_ROWS, 0, 0, tiled=True)  8.04 us
  transfers between devices with their start and end apart: 7, of which 4 were waited for; matrix products, arithmetic and copies ran while one was open for 0% of the time, Pallas kernels for 3%

profile of v9, /device:TPU:6, one launch (start us, length us, event | category | flops | bytes accessed | tf_op | source)
XLA Modules:
  0.0 177.1 jit_solution(11932431280112934773)
XLA Ops:
  0.0 0.8 broadcast_in_dim.6
  0.8 26.3 %all_to_all.35 = bf16[16,16,1024]{2,1,0:T(8,128)(2,1)S(1)} all-to-all(bf16[16,16,1024]{2,1,0:T(8,128)(2,1)S(1)} %broadcast_in_dim.6), channel_id=1, replica_groups=mesh['yh'=4,'x'=4,'c'=2,'z'=8,'yl'=2] {'x','yh'}, dimensions={0} | all-to-all | bytes 1048576 | tf_op jit(solution)/shard_map/all_to_all | solution.py:131
  27.2 0.1 broadcast_in_dim.15
  27.3 4.7 %all_to_all.36 = bf16[2,256,1024]{2,1,0:T(8,128)(2,1)S(1)} all-to-all(bf16[2,256,1024]{2,1,0:T(8,128)(2,1)S(1)} %broadcast_in_dim.15), channel_id=1, replica_groups=mesh['yh'=4,'x'=4,'c'=2,'z'=8,'yl'=2] {'c'}, dimensions={0} | all-to-all | bytes 2097152 | tf_op jit(solution)/shard_map/all_to_all | solution.py:131
  32.0 2.5 %shard_map.37 = bf16[16,264,128]{2,1,0:T(8,128)(2,1)S(1)} custom-call(bf16[1024,1024]{1,0:T(8,128)(2,1)S(1)} %copy-done, bf16[512,1024]{1,0:T(8,128)(2,1)S(1)} %bitcast.6), custom_call_target="tpu_custom_call" | custom-call | tf_op jit(solution)/shard_map/pallas_call | solution.py:313
  34.5 1.0 copy-done.1
  35.5 10.5 %all-to-all-start.2 = ((bf16[16,264,128]{2,1,0:T(8,128)(2,1)}), bf16[16,264,128]{2,1,0:T(8,128)(2,1)}, u32[]{:S(2)}, u32[]{:S(2)}) async-start(bf16[16,264,128]{2,1,0:T(8,128)(2,1)} %copy-done.1), calls=%async_computation.2 | async-start | bytes 2162688 | tf_op jit(solution)/shard_map/all_to_all | solution.py:321
  45.9 0.0 copy-start.4
  45.9 1.9 %collective-permute-start.3 = (bf16[1024,1024]{1,0:T(8,128)(2,1)S(1)}, bf16[1024,1024]{1,0:T(8,128)(2,1)}, u32[]{:S(2)}, u32[]{:S(2)}) collective-permute-start(bf16[1024,1024]{1,0:T(8,128)(2,1)S(1)} %copy-done), channel_id=1, source_target_pairs={{0,16},{16,0},{1,17},{17,1},{2,18},{18,2},{3,19},{19,3},{4,20},{20... | collective-permute-start | bytes 6291464 | tf_op jit(solution)/shard_map/ppermute | solution.py:306
  47.9 25.2 %all-to-all-done.2.codes_ref = bf16[16,264,128]{2,1,0:T(8,128)(2,1)} async-done(((bf16[16,264,128]{2,1,0:T(8,128)(2,1)}), bf16[16,264,128]{2,1,0:T(8,128)(2,1)}, u32[]{:S(2)}, u32[]{:S(2)}) %all-to-all-start.2) | async-done | bytes 1081376 | tf_op jit(solution)/shard_map/all_to_all | solution.py:321
  73.1 2.4 %shard_map.38 = bf16[8,272,128]{2,1,0:T(8,128)(2,1)S(1)} custom-call(bf16[16,264,128]{2,1,0:T(8,128)(2,1)} %all-to-all-done.2.codes_ref), custom_call_target="tpu_custom_call" | custom-call | tf_op jit(solution)/shard_map/pallas_call | solution.py:322
  75.4 23.2 %all_to_all.37.own_ref = bf16[8,272,128]{2,1,0:T(8,128)(2,1)S(1)} all-to-all(bf16[8,272,128]{2,1,0:T(8,128)(2,1)S(1)} %shard_map.38), channel_id=1, replica_groups=mesh['yh'=4,'x'=4,'c'=2,'z'=8,'yl'=2] {'z'}, dimensions={0} | all-to-all | bytes 1114112 | tf_op jit(solution)/shard_map/all_to_all | solution.py:331
  98.6 3.8 %collective-permute-start.1 = (bf16[8,272,128]{2,1,0:T(8,128)(2,1)S(1)}, bf16[8,272,128]{2,1,0:T(8,128)(2,1)S(1)}, u32[]{:S(2)}, u32[]{:S(2)}) collective-permute-start(bf16[8,272,128]{2,1,0:T(8,128)(2,1)S(1)} %all_to_all.37.own_ref), channel_id=1, source_target_pairs={{0,1},{1,0},{2,3},{3,2},{4,5},{5,4},{6,7},{7,6},{8,9},{9,8},{10,11... | collective-permute-start | bytes 1671176 | tf_op jit(solution)/shard_map/ppermute | solution.py:332
  102.4 1.9 %collective-permute-start = (bf16[8,272,128]{2,1,0:T(8,128)(2,1)S(1)}, bf16[8,272,128]{2,1,0:T(8,128)(2,1)S(1)}, u32[]{:S(2)}, u32[]{:S(2)}) collective-permute-start(bf16[8,272,128]{2,1,0:T(8,128)(2,1)S(1)} %all_to_all.37.own_ref), channel_id=1, source_target_pairs={{0,16},{16,0},{1,17},{17,1},{2,18},{18,2},{3,19},{19,3},{4,20},{20... | collective-permute-start | bytes 1671176 | tf_op jit(solution)/shard_map/ppermute | solution.py:333
  104.4 9.0 %collective-permute-done.1.in_ref.other_ref = bf16[8,272,128]{2,1,0:T(8,128)(2,1)S(1)} collective-permute-done((bf16[8,272,128]{2,1,0:T(8,128)(2,1)S(1)}, bf16[8,272,128]{2,1,0:T(8,128)(2,1)S(1)}, u32[]{:S(2)}, u32[]{:S(2)}) %collective-permute-start.1) | collective-permute-done | bytes 557088 | tf_op jit(solution)/shard_map/ppermute | solution.py:332
  113.3 0.8 shard_map.41
  114.2 0.8 copy-done.2
  115.0 1.9 %collective-permute-start.2 = (bf16[8,272,128]{2,1,0:T(8,128)(2,1)}, bf16[8,272,128]{2,1,0:T(8,128)(2,1)}, u32[]{:S(2)}, u32[]{:S(2)}) collective-permute-start(bf16[8,272,128]{2,1,0:T(8,128)(2,1)} %shard_map.41), channel_id=1, source_target_pairs={{0,16},{16,0},{1,17},{17,1},{2,18},{18,2},{3,19},{19,3},{4,20},{20... | collective-permute-start | bytes 1671176 | tf_op jit(solution)/shard_map/ppermute | solution.py:362
  116.9 0.8 shard_map.39
  117.7 7.4 %all-to-all-start.4 = ((f32[64,4,128]{2,1,0:T(4,128)}), f32[64,4,128]{2,1,0:T(4,128)S(1)}, u32[]{:S(2)}, u32[]{:S(2)}) async-start(f32[64,4,128]{2,1,0:T(4,128)} %shard_map.39), calls=%async_computation.4 | async-start | bytes 262144 | tf_op jit(solution)/shard_map/all_to_all | solution.py:346
  125.1 0.1 reshape.12
  125.2 0.1 reshape.13.mass_ref
  125.3 8.6 %all-to-all-done.4.stats_ref = f32[64,4,128]{2,1,0:T(4,128)S(1)} async-done(((f32[64,4,128]{2,1,0:T(4,128)}), f32[64,4,128]{2,1,0:T(4,128)S(1)}, u32[]{:S(2)}, u32[]{:S(2)}) %all-to-all-start.4) | async-done | bytes 131104 | tf_op jit(solution)/shard_map/all_to_all | solution.py:346
  133.9 0.0 collective-permute-done.core_ref.core_own_ref
  133.9 1.2 shard_map.40
  135.1 5.8 %all-to-all-start.5 = ((f32[32,4,128]{2,1,0:T(4,128)}), f32[32,4,128]{2,1,0:T(4,128)S(1)}, u32[]{:S(2)}, u32[]{:S(2)}) async-start(f32[32,4,128]{2,1,0:T(4,128)} %get-tuple-element.9), calls=%async_computation.5 | async-start | bytes 131072 | tf_op jit(solution)/shard_map/all_to_all | solution.py:354
  140.9 0.1 pad_add_fusion.place_ref
  141.0 8.0 %all-to-all-done.5.sums_ref = f32[32,4,128]{2,1,0:T(4,128)S(1)} async-done(((f32[32,4,128]{2,1,0:T(4,128)}), f32[32,4,128]{2,1,0:T(4,128)S(1)}, u32[]{:S(2)}, u32[]{:S(2)}) %all-to-all-start.5) | async-done | bytes 65568 | tf_op jit(solution)/shard_map/all_to_all | solution.py:354
  149.1 1.1 copy-done.3
  150.1 4.1 %shard_map.42 = bf16[16,136,128]{2,1,0:T(8,128)(2,1)S(1)} custom-call(s32[3]{0:T(128)S(1)} %pad_add_fusion.place_ref, f32[32,4,128]{2,1,0:T(4,128)S(1)} %all-to-all-done.5.sums_ref, f32[4,128]{1,0:T(4,128)S(1)} %get-tuple-element.10.far_ref, f32[4,128]{1,0:T(4,128)S(1)} %get-tuple-element.11.col_ref, f32[4,128]{1,0:T(4,128)S(1)} %get-tuple-element.12.b_ref, ...), custom_call_target="tpu_custom_call" | custom-call | tf_op jit(solution)/shard_map/pallas_call | solution.py:367
  154.2 21.6 %all_to_all.38.got_ref = bf16[16,136,128]{2,1,0:T(8,128)(2,1)S(1)} all-to-all(bf16[16,136,128]{2,1,0:T(8,128)(2,1)S(1)} %shard_map.42), channel_id=1, replica_groups=mesh['yh'=4,'x'=4,'c'=2,'z'=8,'yl'=2] {'x','yh'}, dimensions={0} | all-to-all | bytes 1114112 | tf_op jit(solution)/shard_map/all_to_all | solution.py:380
  175.8 1.3 shard_map.43
  (9 shorter events, 0.0 us)
Async XLA Ops:
  27.1 4.8 %copy-start = (bf16[1024,1024]{1,0:T(8,128)(2,1)S(1)}, bf16[1024,1024]{1,0:T(8,128)(2,1)}, u32[]{:S(2)}) copy-start(bf16[1024,1024]{1,0:T(8,128)(2,1)} %train_ref.3) | copy-start | bytes 6291460
  34.4 1.0 copy-start.1
  35.5 37.6 %all-to-all-start.2 = ((bf16[16,264,128]{2,1,0:T(8,128)(2,1)}), bf16[16,264,128]{2,1,0:T(8,128)(2,1)}, u32[]{:S(2)}, u32[]{:S(2)}) async-start(bf16[16,264,128]{2,1,0:T(8,128)(2,1)} %copy-done.1), calls=%async_computation.2 | async-start | bytes 2162688 | tf_op jit(solution)/shard_map/all_to_all | solution.py:321
  45.9 79.2 %copy-start.4 = (f32[512]{0:T(512)S(1)}, f32[512]{0:T(512)}, u32[]{:S(2)}) copy-start(f32[512]{0:T(512)} %param.5) | copy-start | bytes 6148
  45.9 95.1 %collective-permute-start.3 = (bf16[1024,1024]{1,0:T(8,128)(2,1)S(1)}, bf16[1024,1024]{1,0:T(8,128)(2,1)}, u32[]{:S(2)}, u32[]{:S(2)}) collective-permute-start(bf16[1024,1024]{1,0:T(8,128)(2,1)S(1)} %copy-done), channel_id=1, source_target_pairs={{0,16},{16,0},{1,17},{17,1},{2,18},{18,2},{3,19},{19,3},{4,20},{20... | collective-permute-start | bytes 6291464 | tf_op jit(solution)/shard_map/ppermute | solution.py:306
  98.6 14.7 %collective-permute-start.1 = (bf16[8,272,128]{2,1,0:T(8,128)(2,1)S(1)}, bf16[8,272,128]{2,1,0:T(8,128)(2,1)S(1)}, u32[]{:S(2)}, u32[]{:S(2)}) collective-permute-start(bf16[8,272,128]{2,1,0:T(8,128)(2,1)S(1)} %all_to_all.37.own_ref), channel_id=1, source_target_pairs={{0,1},{1,0},{2,3},{3,2},{4,5},{5,4},{6,7},{7,6},{8,9},{9,8},{10,11... | collective-permute-start | bytes 1671176 | tf_op jit(solution)/shard_map/ppermute | solution.py:332
  102.4 31.5 %collective-permute-start = (bf16[8,272,128]{2,1,0:T(8,128)(2,1)S(1)}, bf16[8,272,128]{2,1,0:T(8,128)(2,1)S(1)}, u32[]{:S(2)}, u32[]{:S(2)}) collective-permute-start(bf16[8,272,128]{2,1,0:T(8,128)(2,1)S(1)} %all_to_all.37.own_ref), channel_id=1, source_target_pairs={{0,16},{16,0},{1,17},{17,1},{2,18},{18,2},{3,19},{19,3},{4,20},{20... | collective-permute-start | bytes 1671176 | tf_op jit(solution)/shard_map/ppermute | solution.py:333
  114.2 0.8 copy-start.2
  115.0 34.1 %collective-permute-start.2 = (bf16[8,272,128]{2,1,0:T(8,128)(2,1)}, bf16[8,272,128]{2,1,0:T(8,128)(2,1)}, u32[]{:S(2)}, u32[]{:S(2)}) collective-permute-start(bf16[8,272,128]{2,1,0:T(8,128)(2,1)} %shard_map.41), channel_id=1, source_target_pairs={{0,16},{16,0},{1,17},{17,1},{2,18},{18,2},{3,19},{19,3},{4,20},{20... | collective-permute-start | bytes 1671176 | tf_op jit(solution)/shard_map/ppermute | solution.py:362
  117.7 16.3 %all-to-all-start.4 = ((f32[64,4,128]{2,1,0:T(4,128)}), f32[64,4,128]{2,1,0:T(4,128)S(1)}, u32[]{:S(2)}, u32[]{:S(2)}) async-start(f32[64,4,128]{2,1,0:T(4,128)} %shard_map.39), calls=%async_computation.4 | async-start | bytes 262144 | tf_op jit(solution)/shard_map/all_to_all | solution.py:346
  135.1 13.9 %all-to-all-start.5 = ((f32[32,4,128]{2,1,0:T(4,128)}), f32[32,4,128]{2,1,0:T(4,128)S(1)}, u32[]{:S(2)}, u32[]{:S(2)}) async-start(f32[32,4,128]{2,1,0:T(4,128)} %get-tuple-element.9), calls=%async_computation.5 | async-start | bytes 131072 | tf_op jit(solution)/shard_map/all_to_all | solution.py:354
  149.1 1.1 copy-start.3

commit v10 on v9

--- a/solution.py
+++ b/solution.py
@@ -182,8 +182,8 @@
     out_ref[...] = jnp.broadcast_to(stack_rows(cols, nl)[None], out_ref.shape)
 
 
-def copy_kernel(in_ref, out_ref):
-    out_ref[...] = in_ref[...]
+def hold_kernel(in_ref, out_ref):
+    out_ref[...] = jnp.zeros_like(out_ref)
 
 
 def mixture_kernel(
@@ -200,6 +200,7 @@
     core_other_ref,
     train_ref,
     core_train_ref,
+    held_ref,
     out_ref,
     plan_ref,
     blocks_vmem,
@@ -352,14 +353,14 @@
         compiler_params=SMALL,
     )(stats, own, core_own, mass)
     sums = lax.all_to_all(sums, CHIP_ROWS, 0, 0, tiled=True)
-    other_copy = pl.pallas_call(
-        copy_kernel,
-        out_shape=jax.ShapeDtypeStruct(other.shape, other.dtype),
-        in_specs=[full],
+    held = pl.pallas_call(
+        hold_kernel,
+        out_shape=jax.ShapeDtypeStruct((8, LANES), jnp.float32),
+        in_specs=[anywhere],
         out_specs=full,
         compiler_params=SMALL,
     )(other)
-    core_other = lax.ppermute(other_copy, "c", SWAP)
+    core_other = lax.ppermute(other, "c", SWAP)
 
     slot = jnp.bitwise_and(lax.axis_index(CHIPS), LANES // mine - 1)
     place = jnp.stack([lax.axis_index("c"), lax.axis_index("yl"), slot]).astype(jnp.int32)
@@ -367,7 +368,7 @@
     send = pl.pallas_call(
         functools.partial(mixture_kernel, sub, a),
         out_shape=jax.ShapeDtypeStruct((nchips, block, LANES), jnp.bfloat16),
-        in_specs=[scalars] + [full] * 6 + [anywhere] * 4,
+        in_specs=[scalars] + [full] * 6 + [anywhere] * 5,
         out_specs=full,
         scratch_shapes=[
             VMEM((nc * rows, half), jnp.bfloat16),
@@ -376,7 +377,7 @@
             pltpu.SemaphoreType.DMA((4,)),
         ],
         compiler_params=LARGE,
-    )(place, sums, far, col, b, own, core_own, other, core_other, train, core_train)
+    )(place, sums, far, col, b, own, core_own, other, core_other, train, core_train, held)
     got = lax.all_to_all(send, CHIPS, 0, 0, tiled=True)
     return pl.pallas_call(
         output_kernel,

time: 179 us -> 178 us (level)
  local copies, waits for them, and re-layouts: 3.97 us -> 2.12 us
    unnamed x10 -> x6, local copies, waits for them, and re-layouts: 2.87 us -> 1.02 us
where the time goes in v10:
time: 178 us; the launch traced here: 176 us
  blocking collectives  75.8 us (43%)
  waiting for transfers between devices  50.8 us (29%)
  starting transfers between devices  33.2 us (19%)
  Pallas kernels  13.8 us (8%)
  local copies, waits for them, and re-layouts  2.12 us (1%)
    all_to_all x2, blocking collectives, spread(): return lax.all_to_all(copies, axes, 0, 0, tiled=True)  31 us
    all_to_all x1, waiting for transfers between devices, shards(): codes = lax.all_to_all(codes, PIECES, 0, 0, tiled=True)  25.2 us
    all_to_all x1, blocking collectives, shards(): own = lax.all_to_all(blocks, 'z', 0, 0, tiled=True)  23.2 us
    all_to_all x1, blocking collectives, shards(): got = lax.all_to_all(send, CHIPS, 0, 0, tiled=True)  21.6 us
    all_to_all x1, starting transfers between devices, shards(): codes = lax.all_to_all(codes, PIECES, 0, 0, tiled=True)  10.5 us
    ppermute x1, waiting for transfers between devices, shards(): other = lax.ppermute(own, 'yl', SWAP)  8.97 us
    all_to_all x1, waiting for transfers between devices, shards(): stats = lax.all_to_all(stats, ROWS, 0, 0, tiled=True)  8.64 us
    all_to_all x1, waiting for transfers between devices, shards(): sums = lax.all_to_all(sums, CHIP_ROWS, 0, 0, tiled=True)  8.04 us
  transfers between devices with their start and end apart: 7, of which 4 were waited for; matrix products, arithmetic and copies ran while one was open for 0% of the time, Pallas kernels for 3%

profile of v10, /device:TPU:6, one launch (start us, length us, event | category | flops | bytes accessed | tf_op | source)
XLA Modules:
  0.0 176.0 jit_solution(16704123824590776728)
XLA Ops:
  0.0 0.8 broadcast_in_dim.6
  0.8 26.3 %all_to_all.35 = bf16[16,16,1024]{2,1,0:T(8,128)(2,1)S(1)} all-to-all(bf16[16,16,1024]{2,1,0:T(8,128)(2,1)S(1)} %broadcast_in_dim.6), channel_id=1, replica_groups=mesh['yh'=4,'x'=4,'c'=2,'z'=8,'yl'=2] {'x','yh'}, dimensions={0} | all-to-all | bytes 1048576 | tf_op jit(solution)/shard_map/all_to_all | solution.py:131
  27.2 0.1 broadcast_in_dim.15
  27.3 4.7 %all_to_all.36 = bf16[2,256,1024]{2,1,0:T(8,128)(2,1)S(1)} all-to-all(bf16[2,256,1024]{2,1,0:T(8,128)(2,1)S(1)} %broadcast_in_dim.15), channel_id=1, replica_groups=mesh['yh'=4,'x'=4,'c'=2,'z'=8,'yl'=2] {'c'}, dimensions={0} | all-to-all | bytes 2097152 | tf_op jit(solution)/shard_map/all_to_all | solution.py:131
  32.0 0.0 copy-done
  32.0 2.5 %shard_map.37 = bf16[16,264,128]{2,1,0:T(8,128)(2,1)S(1)} custom-call(bf16[1024,1024]{1,0:T(8,128)(2,1)S(1)} %copy-done, bf16[512,1024]{1,0:T(8,128)(2,1)S(1)} %bitcast.6), custom_call_target="tpu_custom_call" | custom-call | tf_op jit(solution)/shard_map/pallas_call | solution.py:314
  34.5 1.0 copy-done.1
  35.5 10.5 %all-to-all-start.2 = ((bf16[16,264,128]{2,1,0:T(8,128)(2,1)}), bf16[16,264,128]{2,1,0:T(8,128)(2,1)}, u32[]{:S(2)}, u32[]{:S(2)}) async-start(bf16[16,264,128]{2,1,0:T(8,128)(2,1)} %copy-done.1), calls=%async_computation.2 | async-start | bytes 2162688 | tf_op jit(solution)/shard_map/all_to_all | solution.py:322
  45.9 0.0 copy-start.2
  45.9 1.9 %collective-permute-start.3 = (bf16[1024,1024]{1,0:T(8,128)(2,1)S(1)}, bf16[1024,1024]{1,0:T(8,128)(2,1)}, u32[]{:S(2)}, u32[]{:S(2)}) collective-permute-start(bf16[1024,1024]{1,0:T(8,128)(2,1)S(1)} %copy-done), channel_id=1, source_target_pairs={{0,16},{16,0},{1,17},{17,1},{2,18},{18,2},{3,19},{19,3},{4,20},{20... | collective-permute-start | bytes 6291464 | tf_op jit(solution)/shard_map/ppermute | solution.py:307
  47.9 25.2 %all-to-all-done.2.codes_ref = bf16[16,264,128]{2,1,0:T(8,128)(2,1)} async-done(((bf16[16,264,128]{2,1,0:T(8,128)(2,1)}), bf16[16,264,128]{2,1,0:T(8,128)(2,1)}, u32[]{:S(2)}, u32[]{:S(2)}) %all-to-all-start.2) | async-done | bytes 1081376 | tf_op jit(solution)/shard_map/all_to_all | solution.py:322
  73.1 2.4 %shard_map.38 = bf16[8,272,128]{2,1,0:T(8,128)(2,1)S(1)} custom-call(bf16[16,264,128]{2,1,0:T(8,128)(2,1)} %all-to-all-done.2.codes_ref), custom_call_target="tpu_custom_call" | custom-call | tf_op jit(solution)/shard_map/pallas_call | solution.py:323
  75.4 23.2 %all_to_all.37.own_ref = bf16[8,272,128]{2,1,0:T(8,128)(2,1)S(1)} all-to-all(bf16[8,272,128]{2,1,0:T(8,128)(2,1)S(1)} %shard_map.38), channel_id=1, replica_groups=mesh['yh'=4,'x'=4,'c'=2,'z'=8,'yl'=2] {'z'}, dimensions={0} | all-to-all | bytes 1114112 | tf_op jit(solution)/shard_map/all_to_all | solution.py:332
  98.6 3.8 %collective-permute-start.1 = (bf16[8,272,128]{2,1,0:T(8,128)(2,1)S(1)}, bf16[8,272,128]{2,1,0:T(8,128)(2,1)S(1)}, u32[]{:S(2)}, u32[]{:S(2)}) collective-permute-start(bf16[8,272,128]{2,1,0:T(8,128)(2,1)S(1)} %all_to_all.37.own_ref), channel_id=1, source_target_pairs={{0,1},{1,0},{2,3},{3,2},{4,5},{5,4},{6,7},{7,6},{8,9},{9,8},{10,11... | collective-permute-start | bytes 1671176 | tf_op jit(solution)/shard_map/ppermute | solution.py:333
  102.4 1.9 %collective-permute-start = (bf16[8,272,128]{2,1,0:T(8,128)(2,1)S(1)}, bf16[8,272,128]{2,1,0:T(8,128)(2,1)}, u32[]{:S(2)}, u32[]{:S(2)}) collective-permute-start(bf16[8,272,128]{2,1,0:T(8,128)(2,1)S(1)} %all_to_all.37.own_ref), channel_id=1, source_target_pairs={{0,16},{16,0},{1,17},{17,1},{2,18},{18,2},{3,19},{19,3},{4,20},{20... | collective-permute-start | bytes 1671176 | tf_op jit(solution)/shard_map/ppermute | solution.py:334
  104.4 9.0 %collective-permute-done.1.in_ref.other_ref = bf16[8,272,128]{2,1,0:T(8,128)(2,1)S(1)} collective-permute-done((bf16[8,272,128]{2,1,0:T(8,128)(2,1)S(1)}, bf16[8,272,128]{2,1,0:T(8,128)(2,1)S(1)}, u32[]{:S(2)}, u32[]{:S(2)}) %collective-permute-start.1) | collective-permute-done | bytes 557088 | tf_op jit(solution)/shard_map/ppermute | solution.py:333
  113.3 1.9 %collective-permute-start.2 = (bf16[8,272,128]{2,1,0:T(8,128)(2,1)S(1)}, bf16[8,272,128]{2,1,0:T(8,128)(2,1)}, u32[]{:S(2)}, u32[]{:S(2)}) collective-permute-start(bf16[8,272,128]{2,1,0:T(8,128)(2,1)S(1)} %collective-permute-done.1.in_ref.other_ref), channel_id=1, source_target_pairs={{0,16},{16,0},{1,17},{17,1},{2,18},{18,2},{3,19},{19,3},{4,20},{20... | collective-permute-start | bytes 1671176 | tf_op jit(solution)/shard_map/ppermute | solution.py:363
  115.3 0.8 shard_map.39
  116.0 7.4 %all-to-all-start.4 = ((f32[64,4,128]{2,1,0:T(4,128)}), f32[64,4,128]{2,1,0:T(4,128)S(1)}, u32[]{:S(2)}, u32[]{:S(2)}) async-start(f32[64,4,128]{2,1,0:T(4,128)} %shard_map.39), calls=%async_computation.4 | async-start | bytes 262144 | tf_op jit(solution)/shard_map/all_to_all | solution.py:347
  123.5 0.1 reshape.12
  123.6 0.1 reshape.13.mass_ref
  123.7 8.6 %all-to-all-done.4.stats_ref = f32[64,4,128]{2,1,0:T(4,128)S(1)} async-done(((f32[64,4,128]{2,1,0:T(4,128)}), f32[64,4,128]{2,1,0:T(4,128)S(1)}, u32[]{:S(2)}, u32[]{:S(2)}) %all-to-all-start.4) | async-done | bytes 131104 | tf_op jit(solution)/shard_map/all_to_all | solution.py:347
  132.3 0.0 collective-permute-done.core_ref.core_own_ref
  132.3 2.2 %shard_map.40 = (f32[4,128]{1,0:T(4,128)S(1)}, f32[4,128]{1,0:T(4,128)S(1)}, f32[4,128]{1,0:T(4,128)S(1)}, f32[32,4,128]{2,1,0:T(4,128)}) custom-call(f32[64,4,128]{2,1,0:T(4,128)S(1)} %all-to-all-done.4.stats_ref, bf16[8,272,128]{2,1,0:T(8,128)(2,1)S(1)} %all_to_all.37.own_ref, bf16[8,272,128]{2,1,0:T(8,128)(2,1)} %collective-permute-done.core_ref.core_own_ref, ...), custom_call_target="tpu_custom_call" | custom-call | tf_op jit(solution)/shard_map/pallas_call | solution.py:348
  134.5 5.8 %all-to-all-start.5 = ((f32[32,4,128]{2,1,0:T(4,128)}), f32[32,4,128]{2,1,0:T(4,128)S(1)}, u32[]{:S(2)}, u32[]{:S(2)}) async-start(f32[32,4,128]{2,1,0:T(4,128)} %get-tuple-element.9), calls=%async_computation.5 | async-start | bytes 131072 | tf_op jit(solution)/shard_map/all_to_all | solution.py:355
  140.4 0.1 pad_add_fusion.place_ref
  140.4 0.0 collective-permute-done.3.core_train_ref
  140.4 8.0 %all-to-all-done.5.sums_ref = f32[32,4,128]{2,1,0:T(4,128)S(1)} async-done(((f32[32,4,128]{2,1,0:T(4,128)}), f32[32,4,128]{2,1,0:T(4,128)S(1)}, u32[]{:S(2)}, u32[]{:S(2)}) %all-to-all-start.5) | async-done | bytes 65568 | tf_op jit(solution)/shard_map/all_to_all | solution.py:355
  148.5 0.0 collective-permute-done.2.core_other_ref
  148.5 4.7 %shard_map.42 = bf16[16,136,128]{2,1,0:T(8,128)(2,1)S(1)} custom-call(s32[3]{0:T(128)S(1)} %pad_add_fusion.place_ref, f32[32,4,128]{2,1,0:T(4,128)S(1)} %all-to-all-done.5.sums_ref, f32[4,128]{1,0:T(4,128)S(1)} %get-tuple-element.10.far_ref, f32[4,128]{1,0:T(4,128)S(1)} %get-tuple-element.11.col_ref, f32[4,128]{1,0:T(4,128)S(1)} %get-tuple-element.12.b_ref, ...), custom_call_target="tpu_custom_call" | custom-call | tf_op jit(solution)/shard_map/pallas_call | solution.py:368
  153.2 21.6 %all_to_all.38.got_ref = bf16[16,136,128]{2,1,0:T(8,128)(2,1)S(1)} all-to-all(bf16[16,136,128]{2,1,0:T(8,128)(2,1)S(1)} %shard_map.42), channel_id=1, replica_groups=mesh['yh'=4,'x'=4,'c'=2,'z'=8,'yl'=2] {'x','yh'}, dimensions={0} | all-to-all | bytes 1114112 | tf_op jit(solution)/shard_map/all_to_all | solution.py:381
  174.7 1.3 shard_map.43
  (5 shorter events, 0.0 us)
Async XLA Ops:
  27.1 4.8 %copy-start = (bf16[1024,1024]{1,0:T(8,128)(2,1)S(1)}, bf16[1024,1024]{1,0:T(8,128)(2,1)}, u32[]{:S(2)}) copy-start(bf16[1024,1024]{1,0:T(8,128)(2,1)} %train_ref.3) | copy-start | bytes 6291460
  34.4 1.0 copy-start.1
  35.5 37.6 %all-to-all-start.2 = ((bf16[16,264,128]{2,1,0:T(8,128)(2,1)}), bf16[16,264,128]{2,1,0:T(8,128)(2,1)}, u32[]{:S(2)}, u32[]{:S(2)}) async-start(bf16[16,264,128]{2,1,0:T(8,128)(2,1)} %copy-done.1), calls=%async_computation.2 | async-start | bytes 2162688 | tf_op jit(solution)/shard_map/all_to_all | solution.py:322
  45.9 77.5 %copy-start.2 = (f32[512]{0:T(512)S(1)}, f32[512]{0:T(512)}, u32[]{:S(2)}) copy-start(f32[512]{0:T(512)} %param.5) | copy-start | bytes 6148
  45.9 94.5 %collective-permute-start.3 = (bf16[1024,1024]{1,0:T(8,128)(2,1)S(1)}, bf16[1024,1024]{1,0:T(8,128)(2,1)}, u32[]{:S(2)}, u32[]{:S(2)}) collective-permute-start(bf16[1024,1024]{1,0:T(8,128)(2,1)S(1)} %copy-done), channel_id=1, source_target_pairs={{0,16},{16,0},{1,17},{17,1},{2,18},{18,2},{3,19},{19,3},{4,20},{20... | collective-permute-start | bytes 6291464 | tf_op jit(solution)/shard_map/ppermute | solution.py:307
  98.6 14.7 %collective-permute-start.1 = (bf16[8,272,128]{2,1,0:T(8,128)(2,1)S(1)}, bf16[8,272,128]{2,1,0:T(8,128)(2,1)S(1)}, u32[]{:S(2)}, u32[]{:S(2)}) collective-permute-start(bf16[8,272,128]{2,1,0:T(8,128)(2,1)S(1)} %all_to_all.37.own_ref), channel_id=1, source_target_pairs={{0,1},{1,0},{2,3},{3,2},{4,5},{5,4},{6,7},{7,6},{8,9},{9,8},{10,11... | collective-permute-start | bytes 1671176 | tf_op jit(solution)/shard_map/ppermute | solution.py:333
  102.4 29.9 %collective-permute-start = (bf16[8,272,128]{2,1,0:T(8,128)(2,1)S(1)}, bf16[8,272,128]{2,1,0:T(8,128)(2,1)}, u32[]{:S(2)}, u32[]{:S(2)}) collective-permute-start(bf16[8,272,128]{2,1,0:T(8,128)(2,1)S(1)} %all_to_all.37.own_ref), channel_id=1, source_target_pairs={{0,16},{16,0},{1,17},{17,1},{2,18},{18,2},{3,19},{19,3},{4,20},{20... | collective-permute-start | bytes 1671176 | tf_op jit(solution)/shard_map/ppermute | solution.py:334
  113.3 35.1 %collective-permute-start.2 = (bf16[8,272,128]{2,1,0:T(8,128)(2,1)S(1)}, bf16[8,272,128]{2,1,0:T(8,128)(2,1)}, u32[]{:S(2)}, u32[]{:S(2)}) collective-permute-start(bf16[8,272,128]{2,1,0:T(8,128)(2,1)S(1)} %collective-permute-done.1.in_ref.other_ref), channel_id=1, source_target_pairs={{0,16},{16,0},{1,17},{17,1},{2,18},{18,2},{3,19},{19,3},{4,20},{20... | collective-permute-start | bytes 1671176 | tf_op jit(solution)/shard_map/ppermute | solution.py:363
  116.0 16.3 %all-to-all-start.4 = ((f32[64,4,128]{2,1,0:T(4,128)}), f32[64,4,128]{2,1,0:T(4,128)S(1)}, u32[]{:S(2)}, u32[]{:S(2)}) async-start(f32[64,4,128]{2,1,0:T(4,128)} %shard_map.39), calls=%async_computation.4 | async-start | bytes 262144 | tf_op jit(solution)/shard_map/all_to_all | solution.py:347
  134.5 13.9 %all-to-all-start.5 = ((f32[32,4,128]{2,1,0:T(4,128)}), f32[32,4,128]{2,1,0:T(4,128)S(1)}, u32[]{:S(2)}, u32[]{:S(2)}) async-start(f32[32,4,128]{2,1,0:T(4,128)} %get-tuple-element.9), calls=%async_computation.5 | async-start | bytes 131072 | tf_op jit(solution)/shard_map/all_to_all | solution.py:355

commit v11 on v10

--- a/solution.py
+++ b/solution.py
@@ -160,16 +160,33 @@
     out_ref[...] = jnp.broadcast_to(log_sum[None], out_ref.shape)
 
 
-def columns_kernel(sub, a, stats_ref, own_ref, core_ref, mass_ref, far_ref, col_ref, b_ref, out_ref):
+def columns_kernel(
+    sub,
+    a,
+    stats_ref,
+    own_ref,
+    core_ref,
+    mass_ref,
+    far_ref,
+    col_ref,
+    b_ref,
+    out_ref,
+    core_vmem,
+    sem,
+):
     nz = own_ref.shape[0]
     nl = out_ref.shape[1]
+    load = pltpu.make_async_copy(core_ref, core_vmem, sem)
+    load.start()
     stats = stats_ref[...]
     far = jnp.max(stats, axis=0)
     b = mass_ref[...] / jnp.sum(mass_ref[...])
     col = b / jnp.sum(jnp.exp(stats - far[None]), axis=0)
     cols = [jnp.zeros((8, LANES), jnp.float32)] * nl
-    for z in range(nz):
-        for ref in (own_ref, core_ref):
+    for ref in (own_ref, core_vmem):
+        if ref is core_vmem:
+            load.wait()
+        for z in range(nz):
             factor = jnp.exp(block_shift(ref, z, sub, nl) - far) * col
             plan = [block_part(ref, z, sub, n) * factor[n : n + 1] for n in range(nl)]
             row = a / jnp.sum(functools.reduce(jnp.add, plan), axis=1, keepdims=True)
@@ -212,12 +229,12 @@
     nh = nl // 2
     rows = nz * sub
     c, yl = place_ref[0], place_ref[1]
-    late = (other_ref, core_other_ref)
+    late = (core_own_ref, other_ref, core_other_ref)
     loads = [
         pltpu.make_async_copy(src, blocks_vmem.at[k], sems.at[k])
         for k, src in enumerate(late)
     ]
-    sources = (own_ref, core_own_ref, blocks_vmem.at[0], blocks_vmem.at[1])
+    sources = (own_ref,) + tuple(blocks_vmem.at[k] for k in range(len(late)))
     copies = [
         pltpu.make_async_copy(src, train_vmem.at[k], sems.at[len(late) + k])
         for k, src in enumerate((train_ref, core_train_ref))
@@ -244,8 +261,8 @@
 
     cols = (jnp.zeros((8, LANES), jnp.float32),) * nh
     for i in range(len(sources)):
-        if i >= 2:
-            loads[i - 2].wait()
+        if i >= 1:
+            loads[i - 1].wait()
         cols = lax.fori_loop(0, nz, functools.partial(step, i), cols, unroll=2)
 
     half = nh * LANES
@@ -348,8 +365,9 @@
     far, col, b, sums = pl.pallas_call(
         functools.partial(columns_kernel, sub, a),
         out_shape=(vector, vector, vector, copies(CHIP_ROWS)),
-        in_specs=[full] * 4,
+        in_specs=[full, full, anywhere, full],
         out_specs=(full,) * 4,
+        scratch_shapes=[VMEM(own.shape, jnp.bfloat16), pltpu.SemaphoreType.DMA],
         compiler_params=SMALL,
     )(stats, own, core_own, mass)
     sums = lax.all_to_all(sums, CHIP_ROWS, 0, 0, tiled=True)
@@ -368,13 +386,13 @@
     send = pl.pallas_call(
         functools.partial(mixture_kernel, sub, a),
         out_shape=jax.ShapeDtypeStruct((nchips, block, LANES), jnp.bfloat16),
-        in_specs=[scalars] + [full] * 6 + [anywhere] * 5,
+        in_specs=[scalars] + [full] * 5 + [anywhere] * 6,
         out_specs=full,
         scratch_shapes=[
             VMEM((nc * rows, half), jnp.bfloat16),
-            VMEM((2,) + own.shape, jnp.bfloat16),
+            VMEM((3,) + own.shape, jnp.bfloat16),
             VMEM((2, rows, feats), jnp.bfloat16),
-            pltpu.SemaphoreType.DMA((4,)),
+            pltpu.SemaphoreType.DMA((5,)),
         ],
         compiler_params=LARGE,
     )(place, sums, far, col, b, own, core_own, other, core_other, train, core_train, held)

time: 178 us -> 178 us (level)
  no operation moved by 1% of the time
where the time goes in v11:
time: 178 us; the launch traced here: 176 us
  blocking collectives  75.8 us (43%)
  waiting for transfers between devices  50.8 us (29%)
  starting transfers between devices  33.2 us (19%)
  Pallas kernels  13.4 us (8%)
  local copies, waits for them, and re-layouts  2.12 us (1%)
    all_to_all x2, blocking collectives, spread(): return lax.all_to_all(copies, axes, 0, 0, tiled=True)  31 us
    all_to_all x1, waiting for transfers between devices, shards(): codes = lax.all_to_all(codes, PIECES, 0, 0, tiled=True)  25.2 us
    all_to_all x1, blocking collectives, shards(): own = lax.all_to_all(blocks, 'z', 0, 0, tiled=True)  23.2 us
    all_to_all x1, blocking collectives, shards(): got = lax.all_to_all(send, CHIPS, 0, 0, tiled=True)  21.6 us
    all_to_all x1, starting transfers between devices, shards(): codes = lax.all_to_all(codes, PIECES, 0, 0, tiled=True)  10.5 us
    ppermute x1, waiting for transfers between devices, shards(): other = lax.ppermute(own, 'yl', SWAP)  8.97 us
    all_to_all x1, waiting for transfers between devices, shards(): stats = lax.all_to_all(stats, ROWS, 0, 0, tiled=True)  8.64 us
    all_to_all x1, waiting for transfers between devices, shards(): sums = lax.all_to_all(sums, CHIP_ROWS, 0, 0, tiled=True)  8.04 us
  transfers between devices with their start and end apart: 7, of which 4 were waited for; matrix products, arithmetic and copies ran while one was open for 0% of the time, Pallas kernels for 3%

profile of v11, /device:TPU:6, one launch (start us, length us, event | category | flops | bytes accessed | tf_op | source)
XLA Modules:
  0.0 175.7 jit_solution(6521229877574862400)
XLA Ops:
  0.0 0.8 broadcast_in_dim.6
  0.8 26.3 %all_to_all.35 = bf16[16,16,1024]{2,1,0:T(8,128)(2,1)S(1)} all-to-all(bf16[16,16,1024]{2,1,0:T(8,128)(2,1)S(1)} %broadcast_in_dim.6), channel_id=1, replica_groups=mesh['yh'=4,'x'=4,'c'=2,'z'=8,'yl'=2] {'x','yh'}, dimensions={0} | all-to-all | bytes 1048576 | tf_op jit(solution)/shard_map/all_to_all | solution.py:131
  27.2 0.1 broadcast_in_dim.15
  27.3 4.7 %all_to_all.36 = bf16[2,256,1024]{2,1,0:T(8,128)(2,1)S(1)} all-to-all(bf16[2,256,1024]{2,1,0:T(8,128)(2,1)S(1)} %broadcast_in_dim.15), channel_id=1, replica_groups=mesh['yh'=4,'x'=4,'c'=2,'z'=8,'yl'=2] {'c'}, dimensions={0} | all-to-all | bytes 2097152 | tf_op jit(solution)/shard_map/all_to_all | solution.py:131
  32.0 0.0 copy-done
  32.0 2.5 %shard_map.37 = bf16[16,264,128]{2,1,0:T(8,128)(2,1)S(1)} custom-call(bf16[1024,1024]{1,0:T(8,128)(2,1)S(1)} %copy-done, bf16[512,1024]{1,0:T(8,128)(2,1)S(1)} %bitcast.6), custom_call_target="tpu_custom_call" | custom-call | tf_op jit(solution)/shard_map/pallas_call | solution.py:331
  34.5 1.0 copy-done.1
  35.5 10.5 %all-to-all-start.2 = ((bf16[16,264,128]{2,1,0:T(8,128)(2,1)}), bf16[16,264,128]{2,1,0:T(8,128)(2,1)}, u32[]{:S(2)}, u32[]{:S(2)}) async-start(bf16[16,264,128]{2,1,0:T(8,128)(2,1)} %copy-done.1), calls=%async_computation.2 | async-start | bytes 2162688 | tf_op jit(solution)/shard_map/all_to_all | solution.py:339
  45.9 0.0 copy-start.2
  45.9 1.9 %collective-permute-start.3 = (bf16[1024,1024]{1,0:T(8,128)(2,1)S(1)}, bf16[1024,1024]{1,0:T(8,128)(2,1)}, u32[]{:S(2)}, u32[]{:S(2)}) collective-permute-start(bf16[1024,1024]{1,0:T(8,128)(2,1)S(1)} %copy-done), channel_id=1, source_target_pairs={{0,16},{16,0},{1,17},{17,1},{2,18},{18,2},{3,19},{19,3},{4,20},{20... | collective-permute-start | bytes 6291464 | tf_op jit(solution)/shard_map/ppermute | solution.py:324
  47.9 25.2 %all-to-all-done.2.codes_ref = bf16[16,264,128]{2,1,0:T(8,128)(2,1)} async-done(((bf16[16,264,128]{2,1,0:T(8,128)(2,1)}), bf16[16,264,128]{2,1,0:T(8,128)(2,1)}, u32[]{:S(2)}, u32[]{:S(2)}) %all-to-all-start.2) | async-done | bytes 1081376 | tf_op jit(solution)/shard_map/all_to_all | solution.py:339
  73.1 2.4 %shard_map.38 = bf16[8,272,128]{2,1,0:T(8,128)(2,1)S(1)} custom-call(bf16[16,264,128]{2,1,0:T(8,128)(2,1)} %all-to-all-done.2.codes_ref), custom_call_target="tpu_custom_call" | custom-call | tf_op jit(solution)/shard_map/pallas_call | solution.py:340
  75.4 23.2 %all_to_all.37.own_ref = bf16[8,272,128]{2,1,0:T(8,128)(2,1)S(1)} all-to-all(bf16[8,272,128]{2,1,0:T(8,128)(2,1)S(1)} %shard_map.38), channel_id=1, replica_groups=mesh['yh'=4,'x'=4,'c'=2,'z'=8,'yl'=2] {'z'}, dimensions={0} | all-to-all | bytes 1114112 | tf_op jit(solution)/shard_map/all_to_all | solution.py:349
  98.6 3.8 %collective-permute-start.1 = (bf16[8,272,128]{2,1,0:T(8,128)(2,1)S(1)}, bf16[8,272,128]{2,1,0:T(8,128)(2,1)S(1)}, u32[]{:S(2)}, u32[]{:S(2)}) collective-permute-start(bf16[8,272,128]{2,1,0:T(8,128)(2,1)S(1)} %all_to_all.37.own_ref), channel_id=1, source_target_pairs={{0,1},{1,0},{2,3},{3,2},{4,5},{5,4},{6,7},{7,6},{8,9},{9,8},{10,11... | collective-permute-start | bytes 1671176 | tf_op jit(solution)/shard_map/ppermute | solution.py:350
  102.4 1.9 %collective-permute-start = (bf16[8,272,128]{2,1,0:T(8,128)(2,1)S(1)}, bf16[8,272,128]{2,1,0:T(8,128)(2,1)}, u32[]{:S(2)}, u32[]{:S(2)}) collective-permute-start(bf16[8,272,128]{2,1,0:T(8,128)(2,1)S(1)} %all_to_all.37.own_ref), channel_id=1, source_target_pairs={{0,16},{16,0},{1,17},{17,1},{2,18},{18,2},{3,19},{19,3},{4,20},{20... | collective-permute-start | bytes 1671176 | tf_op jit(solution)/shard_map/ppermute | solution.py:351
  104.4 9.0 %collective-permute-done.1.in_ref.other_ref = bf16[8,272,128]{2,1,0:T(8,128)(2,1)S(1)} collective-permute-done((bf16[8,272,128]{2,1,0:T(8,128)(2,1)S(1)}, bf16[8,272,128]{2,1,0:T(8,128)(2,1)S(1)}, u32[]{:S(2)}, u32[]{:S(2)}) %collective-permute-start.1) | collective-permute-done | bytes 557088 | tf_op jit(solution)/shard_map/ppermute | solution.py:350
  113.3 1.9 %collective-permute-start.2 = (bf16[8,272,128]{2,1,0:T(8,128)(2,1)S(1)}, bf16[8,272,128]{2,1,0:T(8,128)(2,1)}, u32[]{:S(2)}, u32[]{:S(2)}) collective-permute-start(bf16[8,272,128]{2,1,0:T(8,128)(2,1)S(1)} %collective-permute-done.1.in_ref.other_ref), channel_id=1, source_target_pairs={{0,16},{16,0},{1,17},{17,1},{2,18},{18,2},{3,19},{19,3},{4,20},{20... | collective-permute-start | bytes 1671176 | tf_op jit(solution)/shard_map/ppermute | solution.py:381
  115.3 0.8 shard_map.39
  116.0 7.4 %all-to-all-start.4 = ((f32[64,4,128]{2,1,0:T(4,128)}), f32[64,4,128]{2,1,0:T(4,128)S(1)}, u32[]{:S(2)}, u32[]{:S(2)}) async-start(f32[64,4,128]{2,1,0:T(4,128)} %shard_map.39), calls=%async_computation.4 | async-start | bytes 262144 | tf_op jit(solution)/shard_map/all_to_all | solution.py:364
  123.5 0.1 reshape.12
  123.6 0.1 reshape.13.mass_ref
  123.7 8.6 %all-to-all-done.4.stats_ref = f32[64,4,128]{2,1,0:T(4,128)S(1)} async-done(((f32[64,4,128]{2,1,0:T(4,128)}), f32[64,4,128]{2,1,0:T(4,128)S(1)}, u32[]{:S(2)}, u32[]{:S(2)}) %all-to-all-start.4) | async-done | bytes 131104 | tf_op jit(solution)/shard_map/all_to_all | solution.py:364
  132.3 0.0 collective-permute-done.core_ref.core_own_ref
  132.3 2.1 %shard_map.40 = (f32[4,128]{1,0:T(4,128)S(1)}, f32[4,128]{1,0:T(4,128)S(1)}, f32[4,128]{1,0:T(4,128)S(1)}, f32[32,4,128]{2,1,0:T(4,128)}) custom-call(f32[64,4,128]{2,1,0:T(4,128)S(1)} %all-to-all-done.4.stats_ref, bf16[8,272,128]{2,1,0:T(8,128)(2,1)S(1)} %all_to_all.37.own_ref, bf16[8,272,128]{2,1,0:T(8,128)(2,1)} %collective-permute-done.core_ref.core_own_ref, ...), custom_call_target="tpu_custom_call" | custom-call | tf_op jit(solution)/shard_map/pallas_call | solution.py:365
  134.5 5.8 %all-to-all-start.5 = ((f32[32,4,128]{2,1,0:T(4,128)}), f32[32,4,128]{2,1,0:T(4,128)S(1)}, u32[]{:S(2)}, u32[]{:S(2)}) async-start(f32[32,4,128]{2,1,0:T(4,128)} %get-tuple-element.9), calls=%async_computation.5 | async-start | bytes 131072 | tf_op jit(solution)/shard_map/all_to_all | solution.py:373
  140.3 0.1 pad_add_fusion.place_ref
  140.4 0.0 collective-permute-done.3.core_train_ref
  140.4 8.0 %all-to-all-done.5.sums_ref = f32[32,4,128]{2,1,0:T(4,128)S(1)} async-done(((f32[32,4,128]{2,1,0:T(4,128)}), f32[32,4,128]{2,1,0:T(4,128)S(1)}, u32[]{:S(2)}, u32[]{:S(2)}) %all-to-all-start.5) | async-done | bytes 65568 | tf_op jit(solution)/shard_map/all_to_all | solution.py:373
  148.4 0.0 collective-permute-done.2.core_other_ref
  148.4 4.4 %shard_map.42 = bf16[16,136,128]{2,1,0:T(8,128)(2,1)S(1)} custom-call(s32[3]{0:T(128)S(1)} %pad_add_fusion.place_ref, f32[32,4,128]{2,1,0:T(4,128)S(1)} %all-to-all-done.5.sums_ref, f32[4,128]{1,0:T(4,128)S(1)} %get-tuple-element.10.far_ref, f32[4,128]{1,0:T(4,128)S(1)} %get-tuple-element.11.col_ref, f32[4,128]{1,0:T(4,128)S(1)} %get-tuple-element.12.b_ref, ...), custom_call_target="tpu_custom_call" | custom-call | tf_op jit(solution)/shard_map/pallas_call | solution.py:386
  152.9 21.6 %all_to_all.38.got_ref = bf16[16,136,128]{2,1,0:T(8,128)(2,1)S(1)} all-to-all(bf16[16,136,128]{2,1,0:T(8,128)(2,1)S(1)} %shard_map.42), channel_id=1, replica_groups=mesh['yh'=4,'x'=4,'c'=2,'z'=8,'yl'=2] {'x','yh'}, dimensions={0} | all-to-all | bytes 1114112 | tf_op jit(solution)/shard_map/all_to_all | solution.py:399
  174.4 1.3 shard_map.43
  (5 shorter events, 0.0 us)
Async XLA Ops:
  27.1 4.8 %copy-start = (bf16[1024,1024]{1,0:T(8,128)(2,1)S(1)}, bf16[1024,1024]{1,0:T(8,128)(2,1)}, u32[]{:S(2)}) copy-start(bf16[1024,1024]{1,0:T(8,128)(2,1)} %train_ref.3) | copy-start | bytes 6291460
  34.4 1.0 copy-start.1
  35.5 37.6 %all-to-all-start.2 = ((bf16[16,264,128]{2,1,0:T(8,128)(2,1)}), bf16[16,264,128]{2,1,0:T(8,128)(2,1)}, u32[]{:S(2)}, u32[]{:S(2)}) async-start(bf16[16,264,128]{2,1,0:T(8,128)(2,1)} %copy-done.1), calls=%async_computation.2 | async-start | bytes 2162688 | tf_op jit(solution)/shard_map/all_to_all | solution.py:339
  45.9 77.5 %copy-start.2 = (f32[512]{0:T(512)S(1)}, f32[512]{0:T(512)}, u32[]{:S(2)}) copy-start(f32[512]{0:T(512)} %param.5) | copy-start | bytes 6148
  45.9 94.4 %collective-permute-start.3 = (bf16[1024,1024]{1,0:T(8,128)(2,1)S(1)}, bf16[1024,1024]{1,0:T(8,128)(2,1)}, u32[]{:S(2)}, u32[]{:S(2)}) collective-permute-start(bf16[1024,1024]{1,0:T(8,128)(2,1)S(1)} %copy-done), channel_id=1, source_target_pairs={{0,16},{16,0},{1,17},{17,1},{2,18},{18,2},{3,19},{19,3},{4,20},{20... | collective-permute-start | bytes 6291464 | tf_op jit(solution)/shard_map/ppermute | solution.py:324
  98.6 14.7 %collective-permute-start.1 = (bf16[8,272,128]{2,1,0:T(8,128)(2,1)S(1)}, bf16[8,272,128]{2,1,0:T(8,128)(2,1)S(1)}, u32[]{:S(2)}, u32[]{:S(2)}) collective-permute-start(bf16[8,272,128]{2,1,0:T(8,128)(2,1)S(1)} %all_to_all.37.own_ref), channel_id=1, source_target_pairs={{0,1},{1,0},{2,3},{3,2},{4,5},{5,4},{6,7},{7,6},{8,9},{9,8},{10,11... | collective-permute-start | bytes 1671176 | tf_op jit(solution)/shard_map/ppermute | solution.py:350
  102.4 29.9 %collective-permute-start = (bf16[8,272,128]{2,1,0:T(8,128)(2,1)S(1)}, bf16[8,272,128]{2,1,0:T(8,128)(2,1)}, u32[]{:S(2)}, u32[]{:S(2)}) collective-permute-start(bf16[8,272,128]{2,1,0:T(8,128)(2,1)S(1)} %all_to_all.37.own_ref), channel_id=1, source_target_pairs={{0,16},{16,0},{1,17},{17,1},{2,18},{18,2},{3,19},{19,3},{4,20},{20... | collective-permute-start | bytes 1671176 | tf_op jit(solution)/shard_map/ppermute | solution.py:351
  113.3 35.1 %collective-permute-start.2 = (bf16[8,272,128]{2,1,0:T(8,128)(2,1)S(1)}, bf16[8,272,128]{2,1,0:T(8,128)(2,1)}, u32[]{:S(2)}, u32[]{:S(2)}) collective-permute-start(bf16[8,272,128]{2,1,0:T(8,128)(2,1)S(1)} %collective-permute-done.1.in_ref.other_ref), channel_id=1, source_target_pairs={{0,16},{16,0},{1,17},{17,1},{2,18},{18,2},{3,19},{19,3},{4,20},{20... | collective-permute-start | bytes 1671176 | tf_op jit(solution)/shard_map/ppermute | solution.py:381
  116.0 16.3 %all-to-all-start.4 = ((f32[64,4,128]{2,1,0:T(4,128)}), f32[64,4,128]{2,1,0:T(4,128)S(1)}, u32[]{:S(2)}, u32[]{:S(2)}) async-start(f32[64,4,128]{2,1,0:T(4,128)} %shard_map.39), calls=%async_computation.4 | async-start | bytes 262144 | tf_op jit(solution)/shard_map/all_to_all | solution.py:364
  134.5 14.0 %all-to-all-start.5 = ((f32[32,4,128]{2,1,0:T(4,128)}), f32[32,4,128]{2,1,0:T(4,128)S(1)}, u32[]{:S(2)}, u32[]{:S(2)}) async-start(f32[32,4,128]{2,1,0:T(4,128)} %get-tuple-element.9), calls=%async_computation.5 | async-start | bytes 131072 | tf_op jit(solution)/shard_map/all_to_all | solution.py:373

commit v12 on v10

--- a/solution.py
+++ b/solution.py
@@ -15,7 +15,6 @@
 FEAT = ("z", "yl")
 PIECES = ("yl", "z")
 ROWS = ("x", "yh", "yl", "c")
-CHIP_ROWS = ("x", "yh", "yl")
 LANES = 128
 CODE_TAIL = 8
 KERNEL_TAIL = 16
@@ -160,7 +159,7 @@
     out_ref[...] = jnp.broadcast_to(log_sum[None], out_ref.shape)
 
 
-def columns_kernel(sub, a, stats_ref, own_ref, core_ref, mass_ref, far_ref, col_ref, b_ref, out_ref):
+def columns_kernel(sub, a, stats_ref, own_ref, mass_ref, far_ref, col_ref, b_ref, out_ref):
     nz = own_ref.shape[0]
     nl = out_ref.shape[1]
     stats = stats_ref[...]
@@ -169,12 +168,11 @@
     col = b / jnp.sum(jnp.exp(stats - far[None]), axis=0)
     cols = [jnp.zeros((8, LANES), jnp.float32)] * nl
     for z in range(nz):
-        for ref in (own_ref, core_ref):
-            factor = jnp.exp(block_shift(ref, z, sub, nl) - far) * col
-            plan = [block_part(ref, z, sub, n) * factor[n : n + 1] for n in range(nl)]
-            row = a / jnp.sum(functools.reduce(jnp.add, plan), axis=1, keepdims=True)
-            for n in range(nl):
-                cols[n] = cols[n] + group_sum(plan[n] * row)
+        factor = jnp.exp(block_shift(own_ref, z, sub, nl) - far) * col
+        plan = [block_part(own_ref, z, sub, n) * factor[n : n + 1] for n in range(nl)]
+        row = a / jnp.sum(functools.reduce(jnp.add, plan), axis=1, keepdims=True)
+        for n in range(nl):
+            cols[n] = cols[n] + group_sum(plan[n] * row)
     cols = [jnp.sum(t, axis=0, keepdims=True) for t in cols]
     far_ref[...] = far
     b_ref[...] = b
@@ -212,12 +210,12 @@
     nh = nl // 2
     rows = nz * sub
     c, yl = place_ref[0], place_ref[1]
-    late = (other_ref, core_other_ref)
+    late = (core_own_ref, other_ref, core_other_ref)
     loads = [
         pltpu.make_async_copy(src, blocks_vmem.at[k], sems.at[k])
         for k, src in enumerate(late)
     ]
-    sources = (own_ref, core_own_ref, blocks_vmem.at[0], blocks_vmem.at[1])
+    sources = (own_ref,) + tuple(blocks_vmem.at[k] for k in range(len(late)))
     copies = [
         pltpu.make_async_copy(src, train_vmem.at[k], sems.at[len(late) + k])
         for k, src in enumerate((train_ref, core_train_ref))
@@ -244,8 +242,8 @@
 
     cols = (jnp.zeros((8, LANES), jnp.float32),) * nh
     for i in range(len(sources)):
-        if i >= 2:
-            loads[i - 2].wait()
+        if i >= 1:
+            loads[i - 1].wait()
         cols = lax.fori_loop(0, nz, functools.partial(step, i), cols, unroll=2)
 
     half = nh * LANES
@@ -316,7 +314,7 @@
         out_shape=jax.ShapeDtypeStruct((nf, nl * sub + CODE_TAIL, LANES), jnp.bfloat16),
         in_specs=[full] * 2,
         out_specs=full,
-        scratch_shapes=[VMEM((2, 4 * sub, nt), jnp.float32)],
+        scratch_shapes=[VMEM((2, 8 * sub, nt), jnp.float32)],
         compiler_params=MIDDLE,
     )(train, targets)
     codes = lax.all_to_all(codes, PIECES, 0, 0, tiled=True)
@@ -347,12 +345,12 @@
     stats = lax.all_to_all(stats, ROWS, 0, 0, tiled=True)
     far, col, b, sums = pl.pallas_call(
         functools.partial(columns_kernel, sub, a),
-        out_shape=(vector, vector, vector, copies(CHIP_ROWS)),
-        in_specs=[full] * 4,
+        out_shape=(vector, vector, vector, copies(ROWS)),
+        in_specs=[full] * 3,
         out_specs=(full,) * 4,
         compiler_params=SMALL,
-    )(stats, own, core_own, mass)
-    sums = lax.all_to_all(sums, CHIP_ROWS, 0, 0, tiled=True)
+    )(stats, own, mass)
+    sums = lax.all_to_all(sums, ROWS, 0, 0, tiled=True)
     held = pl.pallas_call(
         hold_kernel,
         out_shape=jax.ShapeDtypeStruct((8, LANES), jnp.float32),
@@ -368,13 +366,13 @@
     send = pl.pallas_call(
         functools.partial(mixture_kernel, sub, a),
         out_shape=jax.ShapeDtypeStruct((nchips, block, LANES), jnp.bfloat16),
-        in_specs=[scalars] + [full] * 6 + [anywhere] * 5,
+        in_specs=[scalars] + [full] * 5 + [anywhere] * 6,
         out_specs=full,
         scratch_shapes=[
             VMEM((nc * rows, half), jnp.bfloat16),
-            VMEM((2,) + own.shape, jnp.bfloat16),
+            VMEM((3,) + own.shape, jnp.bfloat16),
             VMEM((2, rows, feats), jnp.bfloat16),
-            pltpu.SemaphoreType.DMA((4,)),
+            pltpu.SemaphoreType.DMA((5,)),
         ],
         compiler_params=LARGE,
     )(place, sums, far, col, b, own, core_own, other, core_other, train, core_train, held)

time: 178 us -> 180 us (1.011)
  blocking collectives: 75.8 us -> 77.8 us
    all_to_all x1, blocking collectives: 21.6 us -> 23.6 us  [shards(): got = lax.all_to_all(send, CHIPS, 0, 0, tiled=True)]
  transfers between devices with their start and end apart: 7 -> 7, of which waited for: 4 -> 4; matrix products, arithmetic and copies ran while one was open for 0% -> 0% of each run, Pallas kernels for 3% -> 2%
where the time goes in v12:
time: 180 us; the launch traced here: 178 us
  blocking collectives  77.8 us (43%)
  waiting for transfers between devices  51.6 us (29%)
  starting transfers between devices  33.8 us (19%)
  Pallas kernels  12.3 us (7%)
  local copies, waits for them, and re-layouts  2.12 us (1%)
    all_to_all x2, blocking collectives, spread(): return lax.all_to_all(copies, axes, 0, 0, tiled=True)  31 us
    all_to_all x1, waiting for transfers between devices, shards(): codes = lax.all_to_all(codes, PIECES, 0, 0, tiled=True)  25.2 us
    all_to_all x1, blocking collectives, shards(): got = lax.all_to_all(send, CHIPS, 0, 0, tiled=True)  23.6 us
    all_to_all x1, blocking collectives, shards(): own = lax.all_to_all(blocks, 'z', 0, 0, tiled=True)  23.2 us
    all_to_all x1, starting transfers between devices, shards(): codes = lax.all_to_all(codes, PIECES, 0, 0, tiled=True)  10.5 us
    ppermute x1, waiting for transfers between devices, shards(): other = lax.ppermute(own, 'yl', SWAP)  8.97 us
    all_to_all x1, waiting for transfers between devices, shards(): sums = lax.all_to_all(sums, ROWS, 0, 0, tiled=True)  8.75 us
    all_to_all x1, waiting for transfers between devices, shards(): stats = lax.all_to_all(stats, ROWS, 0, 0, tiled=True)  8.64 us
  transfers between devices with their start and end apart: 7, of which 4 were waited for; matrix products, arithmetic and copies ran while one was open for 0% of the time, Pallas kernels for 2%

profile of v12, /device:TPU:6, one launch (start us, length us, event | category | flops | bytes accessed | tf_op | source)
XLA Modules:
  0.0 177.9 jit_solution(8567592909549713730)
XLA Ops:
  0.0 0.8 broadcast_in_dim.6
  0.8 26.3 %all_to_all.35 = bf16[16,16,1024]{2,1,0:T(8,128)(2,1)S(1)} all-to-all(bf16[16,16,1024]{2,1,0:T(8,128)(2,1)S(1)} %broadcast_in_dim.6), channel_id=1, replica_groups=mesh['yh'=4,'x'=4,'c'=2,'z'=8,'yl'=2] {'x','yh'}, dimensions={0} | all-to-all | bytes 1048576 | tf_op jit(solution)/shard_map/all_to_all | solution.py:130
  27.2 0.1 broadcast_in_dim.15
  27.3 4.7 %all_to_all.36 = bf16[2,256,1024]{2,1,0:T(8,128)(2,1)S(1)} all-to-all(bf16[2,256,1024]{2,1,0:T(8,128)(2,1)S(1)} %broadcast_in_dim.15), channel_id=1, replica_groups=mesh['yh'=4,'x'=4,'c'=2,'z'=8,'yl'=2] {'c'}, dimensions={0} | all-to-all | bytes 2097152 | tf_op jit(solution)/shard_map/all_to_all | solution.py:130
  32.0 0.0 copy-done
  32.0 2.5 %shard_map.37 = bf16[16,264,128]{2,1,0:T(8,128)(2,1)S(1)} custom-call(bf16[1024,1024]{1,0:T(8,128)(2,1)S(1)} %copy-done, bf16[512,1024]{1,0:T(8,128)(2,1)S(1)} %bitcast.6), custom_call_target="tpu_custom_call" | custom-call | tf_op jit(solution)/shard_map/pallas_call | solution.py:312
  34.5 1.0 copy-done.1
  35.5 10.5 %all-to-all-start.2 = ((bf16[16,264,128]{2,1,0:T(8,128)(2,1)}), bf16[16,264,128]{2,1,0:T(8,128)(2,1)}, u32[]{:S(2)}, u32[]{:S(2)}) async-start(bf16[16,264,128]{2,1,0:T(8,128)(2,1)} %copy-done.1), calls=%async_computation.2 | async-start | bytes 2162688 | tf_op jit(solution)/shard_map/all_to_all | solution.py:320
  46.0 0.0 copy-start.2
  46.0 1.9 %collective-permute-start.3 = (bf16[1024,1024]{1,0:T(8,128)(2,1)S(1)}, bf16[1024,1024]{1,0:T(8,128)(2,1)}, u32[]{:S(2)}, u32[]{:S(2)}) collective-permute-start(bf16[1024,1024]{1,0:T(8,128)(2,1)S(1)} %copy-done), channel_id=1, source_target_pairs={{0,16},{16,0},{1,17},{17,1},{2,18},{18,2},{3,19},{19,3},{4,20},{20... | collective-permute-start | bytes 6291464 | tf_op jit(solution)/shard_map/ppermute | solution.py:305
  47.9 25.2 %all-to-all-done.2.codes_ref = bf16[16,264,128]{2,1,0:T(8,128)(2,1)} async-done(((bf16[16,264,128]{2,1,0:T(8,128)(2,1)}), bf16[16,264,128]{2,1,0:T(8,128)(2,1)}, u32[]{:S(2)}, u32[]{:S(2)}) %all-to-all-start.2) | async-done | bytes 1081376 | tf_op jit(solution)/shard_map/all_to_all | solution.py:320
  73.1 2.4 %shard_map.38 = bf16[8,272,128]{2,1,0:T(8,128)(2,1)S(1)} custom-call(bf16[16,264,128]{2,1,0:T(8,128)(2,1)} %all-to-all-done.2.codes_ref), custom_call_target="tpu_custom_call" | custom-call | tf_op jit(solution)/shard_map/pallas_call | solution.py:321
  75.5 23.2 %all_to_all.37.own_ref = bf16[8,272,128]{2,1,0:T(8,128)(2,1)S(1)} all-to-all(bf16[8,272,128]{2,1,0:T(8,128)(2,1)S(1)} %shard_map.38), channel_id=1, replica_groups=mesh['yh'=4,'x'=4,'c'=2,'z'=8,'yl'=2] {'z'}, dimensions={0} | all-to-all | bytes 1114112 | tf_op jit(solution)/shard_map/all_to_all | solution.py:330
  98.7 3.8 %collective-permute-start.1 = (bf16[8,272,128]{2,1,0:T(8,128)(2,1)S(1)}, bf16[8,272,128]{2,1,0:T(8,128)(2,1)S(1)}, u32[]{:S(2)}, u32[]{:S(2)}) collective-permute-start(bf16[8,272,128]{2,1,0:T(8,128)(2,1)S(1)} %all_to_all.37.own_ref), channel_id=1, source_target_pairs={{0,1},{1,0},{2,3},{3,2},{4,5},{5,4},{6,7},{7,6},{8,9},{9,8},{10,11... | collective-permute-start | bytes 1671176 | tf_op jit(solution)/shard_map/ppermute | solution.py:331
  102.5 1.9 %collective-permute-start = (bf16[8,272,128]{2,1,0:T(8,128)(2,1)S(1)}, bf16[8,272,128]{2,1,0:T(8,128)(2,1)}, u32[]{:S(2)}, u32[]{:S(2)}) collective-permute-start(bf16[8,272,128]{2,1,0:T(8,128)(2,1)S(1)} %all_to_all.37.own_ref), channel_id=1, source_target_pairs={{0,16},{16,0},{1,17},{17,1},{2,18},{18,2},{3,19},{19,3},{4,20},{20... | collective-permute-start | bytes 1671176 | tf_op jit(solution)/shard_map/ppermute | solution.py:332
  104.4 9.0 %collective-permute-done.1.in_ref.other_ref = bf16[8,272,128]{2,1,0:T(8,128)(2,1)S(1)} collective-permute-done((bf16[8,272,128]{2,1,0:T(8,128)(2,1)S(1)}, bf16[8,272,128]{2,1,0:T(8,128)(2,1)S(1)}, u32[]{:S(2)}, u32[]{:S(2)}) %collective-permute-start.1) | collective-permute-done | bytes 557088 | tf_op jit(solution)/shard_map/ppermute | solution.py:331
  113.4 1.9 %collective-permute-start.2 = (bf16[8,272,128]{2,1,0:T(8,128)(2,1)S(1)}, bf16[8,272,128]{2,1,0:T(8,128)(2,1)}, u32[]{:S(2)}, u32[]{:S(2)}) collective-permute-start(bf16[8,272,128]{2,1,0:T(8,128)(2,1)S(1)} %collective-permute-done.1.in_ref.other_ref), channel_id=1, source_target_pairs={{0,16},{16,0},{1,17},{17,1},{2,18},{18,2},{3,19},{19,3},{4,20},{20... | collective-permute-start | bytes 1671176 | tf_op jit(solution)/shard_map/ppermute | solution.py:361
  115.3 0.8 shard_map.39
  116.1 7.4 %all-to-all-start.4 = ((f32[64,4,128]{2,1,0:T(4,128)}), f32[64,4,128]{2,1,0:T(4,128)S(1)}, u32[]{:S(2)}, u32[]{:S(2)}) async-start(f32[64,4,128]{2,1,0:T(4,128)} %shard_map.39), calls=%async_computation.4 | async-start | bytes 262144 | tf_op jit(solution)/shard_map/all_to_all | solution.py:345
  123.5 0.1 reshape.12
  123.6 0.1 reshape.13.mass_ref
  123.7 8.6 %all-to-all-done.4.stats_ref = f32[64,4,128]{2,1,0:T(4,128)S(1)} async-done(((f32[64,4,128]{2,1,0:T(4,128)}), f32[64,4,128]{2,1,0:T(4,128)S(1)}, u32[]{:S(2)}, u32[]{:S(2)}) %all-to-all-start.4) | async-done | bytes 131104 | tf_op jit(solution)/shard_map/all_to_all | solution.py:345
  132.3 1.0 shard_map.40
  133.4 6.4 %all-to-all-start.5 = ((f32[64,4,128]{2,1,0:T(4,128)}), f32[64,4,128]{2,1,0:T(4,128)S(1)}, u32[]{:S(2)}, u32[]{:S(2)}) async-start(f32[64,4,128]{2,1,0:T(4,128)} %get-tuple-element.9), calls=%async_computation.5 | async-start | bytes 262144 | tf_op jit(solution)/shard_map/all_to_all | solution.py:353
  139.8 0.1 pad_add_fusion.place_ref
  139.8 0.0 collective-permute-done.3.core_train_ref
  139.8 8.8 %all-to-all-done.5.sums_ref = f32[64,4,128]{2,1,0:T(4,128)S(1)} async-done(((f32[64,4,128]{2,1,0:T(4,128)}), f32[64,4,128]{2,1,0:T(4,128)S(1)}, u32[]{:S(2)}, u32[]{:S(2)}) %all-to-all-start.5) | async-done | bytes 131104 | tf_op jit(solution)/shard_map/all_to_all | solution.py:353
  148.6 0.0 collective-permute-done.core_own_ref
  148.6 0.0 collective-permute-done.2.core_other_ref
  148.6 4.4 %shard_map.42 = bf16[16,136,128]{2,1,0:T(8,128)(2,1)S(1)} custom-call(s32[3]{0:T(128)S(1)} %pad_add_fusion.place_ref, f32[64,4,128]{2,1,0:T(4,128)S(1)} %all-to-all-done.5.sums_ref, f32[4,128]{1,0:T(4,128)S(1)} %get-tuple-element.10.far_ref, f32[4,128]{1,0:T(4,128)S(1)} %get-tuple-element.11.col_ref, f32[4,128]{1,0:T(4,128)S(1)} %get-tuple-element.12.b_ref, ...), custom_call_target="tpu_custom_call" | custom-call | tf_op jit(solution)/shard_map/pallas_call | solution.py:366
  153.0 23.6 %all_to_all.38.got_ref = bf16[16,136,128]{2,1,0:T(8,128)(2,1)S(1)} all-to-all(bf16[16,136,128]{2,1,0:T(8,128)(2,1)S(1)} %shard_map.42), channel_id=1, replica_groups=mesh['yh'=4,'x'=4,'c'=2,'z'=8,'yl'=2] {'x','yh'}, dimensions={0} | all-to-all | bytes 1114112 | tf_op jit(solution)/shard_map/all_to_all | solution.py:379
  176.6 1.3 shard_map.43
  (5 shorter events, 0.0 us)
Async XLA Ops:
  27.1 4.8 %copy-start = (bf16[1024,1024]{1,0:T(8,128)(2,1)S(1)}, bf16[1024,1024]{1,0:T(8,128)(2,1)}, u32[]{:S(2)}) copy-start(bf16[1024,1024]{1,0:T(8,128)(2,1)} %train_ref.3) | copy-start | bytes 6291460
  34.5 1.0 copy-start.1
  35.5 37.6 %all-to-all-start.2 = ((bf16[16,264,128]{2,1,0:T(8,128)(2,1)}), bf16[16,264,128]{2,1,0:T(8,128)(2,1)}, u32[]{:S(2)}, u32[]{:S(2)}) async-start(bf16[16,264,128]{2,1,0:T(8,128)(2,1)} %copy-done.1), calls=%async_computation.2 | async-start | bytes 2162688 | tf_op jit(solution)/shard_map/all_to_all | solution.py:320
  46.0 77.5 %copy-start.2 = (f32[512]{0:T(512)S(1)}, f32[512]{0:T(512)}, u32[]{:S(2)}) copy-start(f32[512]{0:T(512)} %param.5) | copy-start | bytes 6148
  46.0 93.8 %collective-permute-start.3 = (bf16[1024,1024]{1,0:T(8,128)(2,1)S(1)}, bf16[1024,1024]{1,0:T(8,128)(2,1)}, u32[]{:S(2)}, u32[]{:S(2)}) collective-permute-start(bf16[1024,1024]{1,0:T(8,128)(2,1)S(1)} %copy-done), channel_id=1, source_target_pairs={{0,16},{16,0},{1,17},{17,1},{2,18},{18,2},{3,19},{19,3},{4,20},{20... | collective-permute-start | bytes 6291464 | tf_op jit(solution)/shard_map/ppermute | solution.py:305
  98.7 14.7 %collective-permute-start.1 = (bf16[8,272,128]{2,1,0:T(8,128)(2,1)S(1)}, bf16[8,272,128]{2,1,0:T(8,128)(2,1)S(1)}, u32[]{:S(2)}, u32[]{:S(2)}) collective-permute-start(bf16[8,272,128]{2,1,0:T(8,128)(2,1)S(1)} %all_to_all.37.own_ref), channel_id=1, source_target_pairs={{0,1},{1,0},{2,3},{3,2},{4,5},{5,4},{6,7},{7,6},{8,9},{9,8},{10,11... | collective-permute-start | bytes 1671176 | tf_op jit(solution)/shard_map/ppermute | solution.py:331
  102.5 46.1 %collective-permute-start = (bf16[8,272,128]{2,1,0:T(8,128)(2,1)S(1)}, bf16[8,272,128]{2,1,0:T(8,128)(2,1)}, u32[]{:S(2)}, u32[]{:S(2)}) collective-permute-start(bf16[8,272,128]{2,1,0:T(8,128)(2,1)S(1)} %all_to_all.37.own_ref), channel_id=1, source_target_pairs={{0,16},{16,0},{1,17},{17,1},{2,18},{18,2},{3,19},{19,3},{4,20},{20... | collective-permute-start | bytes 1671176 | tf_op jit(solution)/shard_map/ppermute | solution.py:332
  113.4 35.2 %collective-permute-start.2 = (bf16[8,272,128]{2,1,0:T(8,128)(2,1)S(1)}, bf16[8,272,128]{2,1,0:T(8,128)(2,1)}, u32[]{:S(2)}, u32[]{:S(2)}) collective-permute-start(bf16[8,272,128]{2,1,0:T(8,128)(2,1)S(1)} %collective-permute-done.1.in_ref.other_ref), channel_id=1, source_target_pairs={{0,16},{16,0},{1,17},{17,1},{2,18},{18,2},{3,19},{19,3},{4,20},{20... | collective-permute-start | bytes 1671176 | tf_op jit(solution)/shard_map/ppermute | solution.py:361
  116.1 16.3 %all-to-all-start.4 = ((f32[64,4,128]{2,1,0:T(4,128)}), f32[64,4,128]{2,1,0:T(4,128)S(1)}, u32[]{:S(2)}, u32[]{:S(2)}) async-start(f32[64,4,128]{2,1,0:T(4,128)} %shard_map.39), calls=%async_computation.4 | async-start | bytes 262144 | tf_op jit(solution)/shard_map/all_to_all | solution.py:345
  133.4 15.2 %all-to-all-start.5 = ((f32[64,4,128]{2,1,0:T(4,128)}), f32[64,4,128]{2,1,0:T(4,128)S(1)}, u32[]{:S(2)}, u32[]{:S(2)}) async-start(f32[64,4,128]{2,1,0:T(4,128)} %get-tuple-element.9), calls=%async_computation.5 | async-start | bytes 262144 | tf_op jit(solution)/shard_map/all_to_all | solution.py:353
